TPU v7x, 256 devices: a whole 4x4x8 slice. The times are simulated.
256 devices in a mesh: gx: 32 (over z, y), gy: 4 (over x_lo, core), pa: 2 (over x_hi).
Axes of the slice: x: 4 (x_hi: 2, x_lo: 2; x = x_hi * 2 + x_lo), y: 4, z: 8, core: 2. Of those that a mesh axis runs over, the one named last changes fastest.
Arguments:
- conductivity: float32 [256, 512, 256], P('gx', 'gy', 'pa'), may hold values from 0.5 to 1
- stored_state: bfloat16 [256, 512, 256], P('gx', 'gy', 'pa'), may hold values from -4 to 5
- row_scales: float32 [256, 512], P('gx', 'gy'), may hold values from 0.5 to 4
- cotangent: float32 [256, 512, 256], P('gx', 'gy', 'pa'), may hold values from -5 to 6
- upper_bound: float32 [1], replicated, may hold values from 97 to 145
Outputs:
- grad_conductivity: float32 [256, 512, 256], P('gx', 'gy', 'pa')
- adjoint: float32 [256, 512, 256], P('gx', 'gy', 'pa')
- state_new: float32 [256, 512, 256], P('gx', 'gy', 'pa')
- residuals: float32 [2, 256, 512, 256], P(None, 'gx', 'gy', 'pa')
All inputs are finite; a program needn't handle non-finite values.
Results may differ from a plain program's by a relative error of at most 0.0003.
Values may be sent and summed in bfloat16 or wider, within the bound.
A program may use at most 128 MiB of HBM per device.

v0:
```python
import jax
import jax.numpy as jnp
from jax import lax
from jax.sharding import PartitionSpec as P

CHEB = 16


time_step = 8.0


def with_halo(cells, sides, width):
    for axis, dim in sides:
        count = lax.axis_size(axis)
        head = lax.slice_in_dim(cells, 0, width, axis=dim)
        tail = lax.slice_in_dim(cells, cells.shape[dim] - width, cells.shape[dim], axis=dim)
        cells = jnp.concatenate(
            [
                lax.ppermute(tail, axis, [(i, (i + 1) % count) for i in range(count)]),
                cells,
                lax.ppermute(head, axis, [((i + 1) % count, i) for i in range(count)]),
            ],
            axis=dim,
        )
    return cells


def swapped(x, axis, bit):
    return lax.ppermute(x, axis, [(i, i ^ 1 << bit) for i in range(lax.axis_size(axis))])


def region(arr, spatial, offset):
    extent = arr.shape[-3:]
    window = [slice(1, length - 1) for length in extent]
    window[spatial] = slice(offset, extent[spatial] - 2 + offset)
    leading = [slice(None)] * (arr.ndim - 3)
    return arr[tuple(leading + window)]


def apply_operator(padded, kpad):
    centre = region(padded, 0, 1)
    kcentre = region(kpad, 0, 1)
    summed = jnp.zeros_like(centre)
    for spatial in range(3):
        for offset in (0, 2):
            summed = summed + 0.5 * (kcentre + region(kpad, spatial, offset)) * (
                centre - region(padded, spatial, offset)
            )
    return centre + time_step * summed


def chebyshev(rhs, kpad, upper):
    theta = 0.5 * (upper + 1.0)
    delta = 0.5 * (upper - 1.0)
    sigma = theta / delta
    rho = 1.0 / sigma
    start = (jnp.zeros_like(rhs), rhs, rhs / theta, rho)

    def sweep(step, carry):
        solution, residual, direction, rho_now = carry
        padded = with_halo(direction, (("gx", 1), ("gy", 2), ("pa", 3)), 1)
        solution = solution + direction
        residual = residual - apply_operator(padded, kpad)
        rho_next = 1.0 / (2.0 * sigma - rho_now)
        direction = rho_next * rho_now * direction + 2.0 * rho_next / delta * residual
        return (solution, residual, direction, rho_next)

    final = lax.fori_loop(0, CHEB, sweep, start)
    return (final[0], final[1])


def body(conductivity, stored_state, row_scales, cotangent, upper_bound):
    upper = upper_bound[0]
    rim_width = 1
    kpad = with_halo(conductivity, (("gx", 0), ("gy", 1), ("pa", 2)), rim_width)
    partner = swapped(stored_state, "pa", 0)
    previous = partner.astype(jnp.float32) * row_scales[:, :, None]
    forward_sol, forward_res = chebyshev(previous[None], kpad, upper)
    adjoint_sol, adjoint_res = chebyshev(cotangent[None], kpad, upper)
    state_new = forward_sol[0]
    adjoint = adjoint_sol[0]
    residuals = jnp.concatenate((forward_res, adjoint_res), axis=0)
    pair = with_halo(jnp.stack((state_new, adjoint)), (("gx", 1), ("gy", 2), ("pa", 3)), 1)
    centre = region(pair, 0, 1)
    summed = jnp.zeros_like(state_new)
    for spatial in range(3):
        for offset in (0, 2):
            differ = centre - region(pair, spatial, offset)
            summed = summed + differ[0] * differ[1]
    grad_conductivity = -0.5 * time_step * summed
    return (grad_conductivity, adjoint, state_new, residuals)


def solution(mesh):
    return jax.shard_map(
        body,
        mesh=mesh,
        in_specs=(
            P("gx", "gy", "pa"),
            P("gx", "gy", "pa"),
            P("gx", "gy"),
            P("gx", "gy", "pa"),
            P(),
        ),
        out_specs=(
            P("gx", "gy", "pa"),
            P("gx", "gy", "pa"),
            P("gx", "gy", "pa"),
            P(None, "gx", "gy", "pa"),
        ),
        check_vma=False,
    )
```

profile of v0, /device:TPU:2, one launch (start us, length us, event | category | flops | bytes accessed | tf_op | source)
XLA Modules:
  0.0 886.3 jit_solution(16791058993234934576)
XLA Ops:
  5.1 6.8 collective-permute-start.14
  29.6 414.8 %while.39 = (s32[]{:T(128)}, f32[1,8,128,128]{3,2,1,0:T(8,128)}, f32[1,8,128,128]{3,2,1,0:T(8,128)}, f32[1,8,128,128]{3,2,1,0:T(8,128)}, f32[]{:T(128)}, /*index...) while((s32[]{:T(128)}, f32[1,8,128,128]{3,2,1,0:T(8,128)}, ...), condition=%wide.region_3.0_spmd.clone, body=%wide.region_2.0_spmd.clone.sunk | while | flops 5706760 | bytes 11741379 | solution.py:68
  30.7 5.4 collective-permute-start.7
  51.0 3.6 multiply_add_fusion.5
  55.8 5.3 collective-permute-start.7
  76.9 3.6 multiply_add_fusion.5
  81.6 5.3 collective-permute-start.7
  103.0 3.6 multiply_add_fusion.5
  107.8 5.3 collective-permute-start.7
  128.8 3.6 multiply_add_fusion.5
  133.6 5.3 collective-permute-start.7
  159.8 5.3 collective-permute-start.7
  185.6 5.3 collective-permute-start.7
  211.8 5.3 collective-permute-start.7
  237.6 5.3 collective-permute-start.7
  263.7 5.3 collective-permute-start.7
  289.5 5.3 collective-permute-start.7
  315.7 5.3 collective-permute-start.7
  336.7 3.6 multiply_add_fusion.5
  341.5 5.3 collective-permute-start.7
  362.9 3.6 multiply_add_fusion.5
  367.7 5.3 collective-permute-start.7
  388.7 3.6 multiply_add_fusion.5
  393.5 5.3 collective-permute-start.7
  414.9 3.6 multiply_add_fusion.5
  419.7 5.3 collective-permute-start.7
  444.3 389.4 %while.38 = (s32[]{:T(128)}, f32[1,8,128,128]{3,2,1,0:T(8,128)}, f32[1,8,128,128]{3,2,1,0:T(8,128)}, f32[1,8,128,128]{3,2,1,0:T(8,128)}, f32[]{:T(128)}, /*index...) while((s32[]{:T(128)}, f32[1,8,128,128]{3,2,1,0:T(8,128)}, ...), condition=%wide.region_1.0_spmd.clone, body=%wide.region_0.0_spmd.clone.sunk | while | flops 5706760 | bytes 15935739 | solution.py:68
  445.5 5.3 collective-permute-start.1
  470.0 5.3 collective-permute-start.1
  494.2 5.3 collective-permute-start.1
  518.7 5.3 collective-permute-start.1
  542.9 5.3 collective-permute-start.1
  567.4 5.3 collective-permute-start.1
  591.6 5.3 collective-permute-start.1
  616.1 5.3 collective-permute-start.1
  640.2 5.3 collective-permute-start.1
  664.8 5.3 collective-permute-start.1
  688.9 5.3 collective-permute-start.1
  713.5 5.3 collective-permute-start.1
  737.6 5.3 collective-permute-start.1
  762.1 5.3 collective-permute-start.1
  786.3 5.3 collective-permute-start.1
  810.8 5.3 collective-permute-start.1
  835.0 5.2 collective-permute-start.20
  842.7 5.8 collective-permute-done.19
  862.8 7.0 fusion.43
  871.9 10.4 %fusion.41 = (f32[2,8,128,128]{3,0,2,1:T(2,128)S(1)}, f32[2,8,128,128]{3,0,2,1:T(2,128)S(1)}) fusion(f32[2,10,130,1]{3,0,2,1:T(2,128)S(1)} %copy.45, f32[2,10,1,128]{3,0,2,1:T(2,128)S(1)} %collective-permute-done.22, f32[2,10,1,128]{3,0,2,1:T(2,128)S(1)} %collective-permute-done.21, f32[2,1,128,128]{3,0,2,1:T(2,128)S(1)} %collective-permute-done.20, ...), kind=kLoop, calls=%fused_computation.86 | loop fusion | flops 3932160 | bytes 3449152 | tf_op jit(solution)/shard_map/sub | solution.py:88
  882.4 4.0 fusion.58
  (890 shorter events, 641.0 us)
Async XLA Ops:
  3.5 10.6 %collective-permute-start.13 = (f32[1,128,128]{2,1,0:T(8,128)S(1)}, f32[1,128,128]{2,1,0:T(8,128)S(1)}, u32[]{:S(2)}, u32[]{:S(2)}) collective-permute-start(f32[1,128,128]{2,1,0:T(8,128)S(1)} %get-tuple-element.482), channel_id=1, source_target_pairs={{0,8},{8,16},{16,24},{24,32},{32,40},{40,48},{48,56},{56,64},{64,7... | collective-permute-start | bytes 196616 | tf_op jit(solution)/shard_map/ppermute | solution.py:19
  5.1 9.0 %collective-permute-start.14 = (f32[1,128,128]{2,1,0:T(8,128)S(1)}, f32[1,128,128]{2,1,0:T(8,128)S(1)}, u32[]{:S(2)}, u32[]{:S(2)}) collective-permute-start(f32[1,128,128]{2,1,0:T(8,128)S(1)} %get-tuple-element.481), channel_id=1, source_target_pairs={{8,0},{16,8},{24,16},{32,24},{40,32},{48,40},{56,48},{64,56},{72,6... | collective-permute-start | bytes 196616 | tf_op jit(solution)/shard_map/ppermute | solution.py:21
  14.8 13.6 %collective-permute-start.12 = (bf16[8,128,128]{2,1,0:T(8,128)(2,1)}, bf16[8,128,128]{2,1,0:T(8,128)(2,1)S(1)}, u32[]{:S(2)}, u32[]{:S(2)}) collective-permute-start(bf16[8,128,128]{2,1,0:T(8,128)(2,1)} %param.10), channel_id=1, source_target_pairs={{0,1},{1,0},{2,3},{3,2},{4,5},{5,4},{6,7},{7,6},{8,9},{9,8},{10,11... | collective-permute-start | bytes 786440 | tf_op jit(solution)/shard_map/ppermute | solution.py:29
  30.6 7.7 collective-permute-start.6
  30.7 8.5 collective-permute-start.7
  55.7 7.7 collective-permute-start.6
  55.8 9.5 %collective-permute-start.7 = (f32[1,1,128,128]{3,2,1,0:T(8,128)S(1)}, f32[1,1,128,128]{3,2,1,0:T(8,128)S(1)}, u32[]{:S(2)}, u32[]{:S(2)}) collective-permute-start(f32[1,1,128,128]{3,2,1,0:T(8,128)S(1)} %get-tuple-element.676), channel_id=1, source_target_pairs={{8,0},{16,8},{24,16},{32,24},{40,32},{48,40},{56,48},{64,56},{72,6... | collective-permute-start | bytes 196616 | tf_op jit(solution)/shard_map/while/body/eval_jaxpr/ppermute | solution.py:21
  81.6 7.7 collective-permute-start.6
  81.6 9.5 %collective-permute-start.7 = (f32[1,1,128,128]{3,2,1,0:T(8,128)S(1)}, f32[1,1,128,128]{3,2,1,0:T(8,128)S(1)}, u32[]{:S(2)}, u32[]{:S(2)}) collective-permute-start(f32[1,1,128,128]{3,2,1,0:T(8,128)S(1)} %get-tuple-element.676), channel_id=1, source_target_pairs={{8,0},{16,8},{24,16},{32,24},{40,32},{48,40},{56,48},{64,56},{72,6... | collective-permute-start | bytes 196616 | tf_op jit(solution)/shard_map/while/body/eval_jaxpr/ppermute | solution.py:21
  107.7 7.7 collective-permute-start.6
  107.8 9.5 %collective-permute-start.7 = (f32[1,1,128,128]{3,2,1,0:T(8,128)S(1)}, f32[1,1,128,128]{3,2,1,0:T(8,128)S(1)}, u32[]{:S(2)}, u32[]{:S(2)}) collective-permute-start(f32[1,1,128,128]{3,2,1,0:T(8,128)S(1)} %get-tuple-element.676), channel_id=1, source_target_pairs={{8,0},{16,8},{24,16},{32,24},{40,32},{48,40},{56,48},{64,56},{72,6... | collective-permute-start | bytes 196616 | tf_op jit(solution)/shard_map/while/body/eval_jaxpr/ppermute | solution.py:21
  133.5 7.7 collective-permute-start.6
  133.6 9.5 %collective-permute-start.7 = (f32[1,1,128,128]{3,2,1,0:T(8,128)S(1)}, f32[1,1,128,128]{3,2,1,0:T(8,128)S(1)}, u32[]{:S(2)}, u32[]{:S(2)}) collective-permute-start(f32[1,1,128,128]{3,2,1,0:T(8,128)S(1)} %get-tuple-element.676), channel_id=1, source_target_pairs={{8,0},{16,8},{24,16},{32,24},{40,32},{48,40},{56,48},{64,56},{72,6... | collective-permute-start | bytes 196616 | tf_op jit(solution)/shard_map/while/body/eval_jaxpr/ppermute | solution.py:21
  159.7 7.7 collective-permute-start.6
  159.8 9.5 %collective-permute-start.7 = (f32[1,1,128,128]{3,2,1,0:T(8,128)S(1)}, f32[1,1,128,128]{3,2,1,0:T(8,128)S(1)}, u32[]{:S(2)}, u32[]{:S(2)}) collective-permute-start(f32[1,1,128,128]{3,2,1,0:T(8,128)S(1)} %get-tuple-element.676), channel_id=1, source_target_pairs={{8,0},{16,8},{24,16},{32,24},{40,32},{48,40},{56,48},{64,56},{72,6... | collective-permute-start | bytes 196616 | tf_op jit(solution)/shard_map/while/body/eval_jaxpr/ppermute | solution.py:21
  185.5 7.7 collective-permute-start.6
  185.6 9.5 %collective-permute-start.7 = (f32[1,1,128,128]{3,2,1,0:T(8,128)S(1)}, f32[1,1,128,128]{3,2,1,0:T(8,128)S(1)}, u32[]{:S(2)}, u32[]{:S(2)}) collective-permute-start(f32[1,1,128,128]{3,2,1,0:T(8,128)S(1)} %get-tuple-element.676), channel_id=1, source_target_pairs={{8,0},{16,8},{24,16},{32,24},{40,32},{48,40},{56,48},{64,56},{72,6... | collective-permute-start | bytes 196616 | tf_op jit(solution)/shard_map/while/body/eval_jaxpr/ppermute | solution.py:21
  211.7 7.7 collective-permute-start.6
  211.8 9.5 %collective-permute-start.7 = (f32[1,1,128,128]{3,2,1,0:T(8,128)S(1)}, f32[1,1,128,128]{3,2,1,0:T(8,128)S(1)}, u32[]{:S(2)}, u32[]{:S(2)}) collective-permute-start(f32[1,1,128,128]{3,2,1,0:T(8,128)S(1)} %get-tuple-element.676), channel_id=1, source_target_pairs={{8,0},{16,8},{24,16},{32,24},{40,32},{48,40},{56,48},{64,56},{72,6... | collective-permute-start | bytes 196616 | tf_op jit(solution)/shard_map/while/body/eval_jaxpr/ppermute | solution.py:21
  237.5 7.7 collective-permute-start.6
  237.6 9.5 %collective-permute-start.7 = (f32[1,1,128,128]{3,2,1,0:T(8,128)S(1)}, f32[1,1,128,128]{3,2,1,0:T(8,128)S(1)}, u32[]{:S(2)}, u32[]{:S(2)}) collective-permute-start(f32[1,1,128,128]{3,2,1,0:T(8,128)S(1)} %get-tuple-element.676), channel_id=1, source_target_pairs={{8,0},{16,8},{24,16},{32,24},{40,32},{48,40},{56,48},{64,56},{72,6... | collective-permute-start | bytes 196616 | tf_op jit(solution)/shard_map/while/body/eval_jaxpr/ppermute | solution.py:21
  263.7 9.5 %collective-permute-start.7 = (f32[1,1,128,128]{3,2,1,0:T(8,128)S(1)}, f32[1,1,128,128]{3,2,1,0:T(8,128)S(1)}, u32[]{:S(2)}, u32[]{:S(2)}) collective-permute-start(f32[1,1,128,128]{3,2,1,0:T(8,128)S(1)} %get-tuple-element.676), channel_id=1, source_target_pairs={{8,0},{16,8},{24,16},{32,24},{40,32},{48,40},{56,48},{64,56},{72,6... | collective-permute-start | bytes 196616 | tf_op jit(solution)/shard_map/while/body/eval_jaxpr/ppermute | solution.py:21
  289.5 9.5 %collective-permute-start.7 = (f32[1,1,128,128]{3,2,1,0:T(8,128)S(1)}, f32[1,1,128,128]{3,2,1,0:T(8,128)S(1)}, u32[]{:S(2)}, u32[]{:S(2)}) collective-permute-start(f32[1,1,128,128]{3,2,1,0:T(8,128)S(1)} %get-tuple-element.676), channel_id=1, source_target_pairs={{8,0},{16,8},{24,16},{32,24},{40,32},{48,40},{56,48},{64,56},{72,6... | collective-permute-start | bytes 196616 | tf_op jit(solution)/shard_map/while/body/eval_jaxpr/ppermute | solution.py:21
  315.7 9.5 %collective-permute-start.7 = (f32[1,1,128,128]{3,2,1,0:T(8,128)S(1)}, f32[1,1,128,128]{3,2,1,0:T(8,128)S(1)}, u32[]{:S(2)}, u32[]{:S(2)}) collective-permute-start(f32[1,1,128,128]{3,2,1,0:T(8,128)S(1)} %get-tuple-element.676), channel_id=1, source_target_pairs={{8,0},{16,8},{24,16},{32,24},{40,32},{48,40},{56,48},{64,56},{72,6... | collective-permute-start | bytes 196616 | tf_op jit(solution)/shard_map/while/body/eval_jaxpr/ppermute | solution.py:21
  341.5 9.5 %collective-permute-start.7 = (f32[1,1,128,128]{3,2,1,0:T(8,128)S(1)}, f32[1,1,128,128]{3,2,1,0:T(8,128)S(1)}, u32[]{:S(2)}, u32[]{:S(2)}) collective-permute-start(f32[1,1,128,128]{3,2,1,0:T(8,128)S(1)} %get-tuple-element.676), channel_id=1, source_target_pairs={{8,0},{16,8},{24,16},{32,24},{40,32},{48,40},{56,48},{64,56},{72,6... | collective-permute-start | bytes 196616 | tf_op jit(solution)/shard_map/while/body/eval_jaxpr/ppermute | solution.py:21
  367.7 9.5 %collective-permute-start.7 = (f32[1,1,128,128]{3,2,1,0:T(8,128)S(1)}, f32[1,1,128,128]{3,2,1,0:T(8,128)S(1)}, u32[]{:S(2)}, u32[]{:S(2)}) collective-permute-start(f32[1,1,128,128]{3,2,1,0:T(8,128)S(1)} %get-tuple-element.676), channel_id=1, source_target_pairs={{8,0},{16,8},{24,16},{32,24},{40,32},{48,40},{56,48},{64,56},{72,6... | collective-permute-start | bytes 196616 | tf_op jit(solution)/shard_map/while/body/eval_jaxpr/ppermute | solution.py:21
  393.5 9.5 %collective-permute-start.7 = (f32[1,1,128,128]{3,2,1,0:T(8,128)S(1)}, f32[1,1,128,128]{3,2,1,0:T(8,128)S(1)}, u32[]{:S(2)}, u32[]{:S(2)}) collective-permute-start(f32[1,1,128,128]{3,2,1,0:T(8,128)S(1)} %get-tuple-element.676), channel_id=1, source_target_pairs={{8,0},{16,8},{24,16},{32,24},{40,32},{48,40},{56,48},{64,56},{72,6... | collective-permute-start | bytes 196616 | tf_op jit(solution)/shard_map/while/body/eval_jaxpr/ppermute | solution.py:21
  419.7 9.5 %collective-permute-start.7 = (f32[1,1,128,128]{3,2,1,0:T(8,128)S(1)}, f32[1,1,128,128]{3,2,1,0:T(8,128)S(1)}, u32[]{:S(2)}, u32[]{:S(2)}) collective-permute-start(f32[1,1,128,128]{3,2,1,0:T(8,128)S(1)} %get-tuple-element.676), channel_id=1, source_target_pairs={{8,0},{16,8},{24,16},{32,24},{40,32},{48,40},{56,48},{64,56},{72,6... | collective-permute-start | bytes 196616 | tf_op jit(solution)/shard_map/while/body/eval_jaxpr/ppermute | solution.py:21
  445.5 7.8 collective-permute-start.1
  470.0 7.8 collective-permute-start.1
  494.2 7.8 collective-permute-start.1
  518.7 7.8 collective-permute-start.1
  542.9 7.8 collective-permute-start.1
  567.4 7.8 collective-permute-start.1
  591.6 7.8 collective-permute-start.1
  616.1 7.8 collective-permute-start.1
  640.2 7.8 collective-permute-start.1
  664.8 7.8 collective-permute-start.1
  688.9 7.8 collective-permute-start.1
  713.5 7.8 collective-permute-start.1
  737.6 7.8 collective-permute-start.1
  762.1 7.8 collective-permute-start.1
  786.3 7.8 collective-permute-start.1
  810.8 7.8 collective-permute-start.1
  835.0 7.7 collective-permute-start.20
  840.2 8.3 collective-permute-start.19
  858.1 11.6 %collective-permute-start.23 = (f32[2,10,130,1]{2,0,3,1:T(2,128)S(1)}, f32[2,10,130,1]{2,0,3,1:T(2,128)S(1)}, u32[]{:S(2)}, u32[]{:S(2)}) collective-permute-start(f32[2,10,130,1]{2,0,3,1:T(2,128)S(1)} %copy.44), channel_id=1, source_target_pairs={{0,1},{1,0},{2,3},{3,2},{4,5},{5,4},{6,7},{7,6},{8,9},{9,8},{10,11... | collective-permute-start | bytes 31208 | tf_op jit(solution)/shard_map/ppermute | solution.py:19
  861.1 9.7 %collective-permute-start.24 = (f32[2,10,130,1]{2,0,3,1:T(2,128)S(1)}, f32[2,10,130,1]{2,0,3,1:T(2,128)S(1)}, u32[]{:S(2)}, u32[]{:S(2)}) collective-permute-start(f32[2,10,130,1]{2,0,3,1:T(2,128)S(1)} %copy.46), channel_id=1, source_target_pairs={{1,0},{0,1},{3,2},{2,3},{5,4},{4,5},{7,6},{6,7},{9,8},{8,9},{11,10... | collective-permute-start | bytes 31208 | tf_op jit(solution)/shard_map/ppermute | solution.py:21
  (197 other events, 954.1 us)
where the time goes:
time: 891 us; the launch traced here: 886 us
  starting transfers between devices  333 us (37%)
  waiting for transfers between devices  262 us (29%)
  other arithmetic  187 us (21%)
  local copies, waits for them, and re-layouts  98 us (11%)
    ppermute x102, starting transfers between devices, with_halo(): lax.ppermute(head, axis, [((i + 1) % count, i) for i in range(count)])  247 us
    ppermute x102, waiting for transfers between devices, with_halo(): lax.ppermute(tail, axis, [(i, (i + 1) % count) for i in range(count)])  199 us
    add x32, other arithmetic, sweep(): rho_next * rho_now * direction + 2.0 * rho_next / delta * residual  116 us
    ppermute x102, starting transfers between devices, with_halo(): lax.ppermute(tail, axis, [(i, (i + 1) % count) for i in range(count)])  83.5 us
    ppermute x102, waiting for transfers between devices, with_halo(): lax.ppermute(head, axis, [((i + 1) % count, i) for i in range(count)])  63.2 us
    while x128, local copies, waits for them, and re-layouts  34.6 us
    while x32, other arithmetic  32.5 us
    slice x99, local copies, waits for them, and re-layouts, with_halo(): lax.slice_in_dim(cells, cells.shape[dim] - width, cells.shape[dim], axis=...  23.8 us
  transfers between devices with their start and end apart: 205, of which 165 were waited for; matrix products, arithmetic and copies ran while one was open for 8% of the time, Pallas kernels for 0%

commit v1 on v0

v1 whole, which is shorter than its diff:
```python
import jax
import jax.numpy as jnp
from jax import lax
from jax.sharding import PartitionSpec as P

CHEB = 16


time_step = 8.0


def ring(x, axis, step):
    count = lax.axis_size(axis)
    return lax.ppermute(x, axis, [(i, (i + step) % count) for i in range(count)])


def halos(cells):
    nd = cells.ndim
    dx, dy, dz = nd - 3, nd - 2, nd - 1
    x_lo = ring(lax.slice_in_dim(cells, cells.shape[dx] - 1, cells.shape[dx], axis=dx), "gx", 1)
    x_hi = ring(lax.slice_in_dim(cells, 0, 1, axis=dx), "gx", -1)
    y_lo = ring(lax.slice_in_dim(cells, cells.shape[dy] - 1, cells.shape[dy], axis=dy), "gy", 1)
    y_hi = ring(lax.slice_in_dim(cells, 0, 1, axis=dy), "gy", -1)
    ends = jnp.concatenate(
        [lax.slice_in_dim(cells, 0, 1, axis=dz), lax.slice_in_dim(cells, cells.shape[dz] - 1, cells.shape[dz], axis=dz)],
        axis=dz,
    )
    got = ring(ends, "pa", 1)
    z_lo = lax.slice_in_dim(got, 1, 2, axis=dz)
    z_hi = lax.slice_in_dim(got, 0, 1, axis=dz)
    return (x_lo, x_hi, y_lo, y_hi, z_lo, z_hi)


def neighbours(cells, faces):
    nd = cells.ndim
    out = []
    for k, dim in enumerate((nd - 3, nd - 2, nd - 1)):
        lo, hi = faces[2 * k], faces[2 * k + 1]
        n = cells.shape[dim]
        out.append(jnp.concatenate([lo, lax.slice_in_dim(cells, 0, n - 1, axis=dim)], axis=dim))
        out.append(jnp.concatenate([lax.slice_in_dim(cells, 1, n, axis=dim), hi], axis=dim))
    return out


def apply_operator(direction, weights):
    near = neighbours(direction, halos(direction))
    summed = jnp.zeros_like(direction)
    for w, n in zip(weights, near):
        summed = summed + w * (direction - n)
    return direction + summed


def body(conductivity, stored_state, row_scales, cotangent, upper_bound):
    upper = upper_bound[0]
    weights = [(conductivity + kn) * (0.5 * time_step) for kn in neighbours(conductivity, halos(conductivity))]
    partner = ring(stored_state, "pa", 1)
    previous = partner.astype(jnp.float32) * row_scales[:, :, None]
    rhs = jnp.stack((previous, cotangent))

    theta = 0.5 * (upper + 1.0)
    delta = 0.5 * (upper - 1.0)
    sigma = theta / delta
    rho = 1.0 / sigma
    start = (jnp.zeros_like(rhs), rhs, rhs / theta, rho)

    def sweep(step, carry):
        solution, residual, direction, rho_now = carry
        solution = solution + direction
        residual = residual - apply_operator(direction, weights)
        rho_next = 1.0 / (2.0 * sigma - rho_now)
        direction = rho_next * rho_now * direction + 2.0 * rho_next / delta * residual
        return (solution, residual, direction, rho_next)

    solved, residuals, _, _ = lax.fori_loop(0, CHEB, sweep, start)
    near = neighbours(solved, halos(solved))
    summed = jnp.zeros_like(solved[0])
    for n in near:
        differ = solved - n
        summed = summed + differ[0] * differ[1]
    grad_conductivity = -0.5 * time_step * summed
    return (grad_conductivity, solved[1], solved[0], residuals)


def solution(mesh):
    return jax.shard_map(
        body,
        mesh=mesh,
        in_specs=(
            P("gx", "gy", "pa"),
            P("gx", "gy", "pa"),
            P("gx", "gy"),
            P("gx", "gy", "pa"),
            P(),
        ),
        out_specs=(
            P("gx", "gy", "pa"),
            P("gx", "gy", "pa"),
            P("gx", "gy", "pa"),
            P(None, "gx", "gy", "pa"),
        ),
        check_vma=False,
    )
```

time: 891 us -> 440 us (0.49)
  waiting for transfers between devices: 262 us -> 6.72 us
  starting transfers between devices: 333 us -> 148 us
  other arithmetic: 187 us -> 136 us
  local copies, waits for them, and re-layouts: 98 us -> 143 us
    ppermute x205 -> x91, waiting for transfers between devices: 262 us -> 6.72 us  [ring(): lax.ppermute(x, axis, [(i, (i + step) % count) for i in range(count)])]
    ppermute x205 -> x91, starting transfers between devices: 333 us -> 148 us  [ring(): lax.ppermute(x, axis, [(i, (i + step) % count) for i in range(count)])]
    slice x168 -> x162, local copies, waits for them, and re-layouts: 39.5 us -> 121 us  [the longest x51 77.1 us: neighbours(): lax.slice_in_dim(cells, 0, n - 1, axis=dim)]
    add x1 -> x16, other arithmetic: 1.95 us -> 36.1 us  [sweep(): solution = solution + direction]
    while x32 -> x0, other arithmetic: 32.5 us -> none
    add x32 -> x16, other arithmetic: 116 us -> 89 us  [sweep(): rho_next * rho_now * direction + 2.0 * rho_next / delta * residual]
    while x128 -> x18, local copies, waits for them, and re-layouts: 34.6 us -> 10.3 us
    ppermute x68 -> x0, local copies, waits for them, and re-layouts: 21.7 us -> none  [the longest x34 10.8 us: with_halo(): lax.ppermute(head, axis, [((i + 1) % count, i) for i in range(count)])]
  transfers between devices with their start and end apart: 205 -> 91, of which waited for: 165 -> 3; matrix products, arithmetic and copies ran while one was open for 8% -> 37% of each run, Pallas kernels for 0% -> 0%
where the time goes in v1:
time: 440 us; the launch traced here: 438 us
  starting transfers between devices  148 us (34%)
  local copies, waits for them, and re-layouts  143 us (32%)
  other arithmetic  136 us (31%)
  waiting for transfers between devices  6.72 us (2%)
    ppermute x91, starting transfers between devices, ring(): lax.ppermute(x, axis, [(i, (i + step) % count) for i in range(count)])  148 us
    add x16, other arithmetic, sweep(): rho_next * rho_now * direction + 2.0 * rho_next / delta * residual  89 us
    slice x51, local copies, waits for them, and re-layouts, neighbours(): lax.slice_in_dim(cells, 0, n - 1, axis=dim)  77.1 us
    add x16, other arithmetic, sweep(): solution = solution + direction  36.1 us
    slice x17, local copies, waits for them, and re-layouts, halos(): lax.slice_in_dim(cells, cells.shape[dx] - 1, cells.shape[dx], axis=dx)  13.7 us
    slice x17, local copies, waits for them, and re-layouts, halos(): lax.slice_in_dim(cells, cells.shape[dy] - 1, cells.shape[dy], axis=dy)  11 us
    unnamed x26, local copies, waits for them, and re-layouts  10 us
  transfers between devices with their start and end apart: 91, of which 3 were waited for; matrix products, arithmetic and copies ran while one was open for 37% of the time, Pallas kernels for 0%

profile of v1, /device:TPU:2, one launch (start us, length us, event | category | flops | bytes accessed | tf_op | source)
XLA Modules:
  0.0 437.6 jit_solution(16442508975838663968)
XLA Ops:
  21.3 6.8 %collective-permute-start.7 = (f32[1,128,128]{2,0,1:T(1,128)}, f32[1,128,128]{2,0,1:T(1,128)}, u32[]{:S(2)}, u32[]{:S(2)}) collective-permute-start(f32[1,128,128]{2,0,1:T(1,128)} %bitcast.5), channel_id=1, source_target_pairs={{0,248},{8,0},{16,8},{24,16},{32,24},{40,32},{48,40},{56,48},{64,5... | collective-permute-start | bytes 196616 | tf_op jit(solution)/shard_map/ppermute | solution.py:14
  30.4 4.0 fusion.25
  34.4 2.9 collective-permute-done.5
  38.6 370.4 %while.19 = (s32[]{:T(128)}, f32[2,8,128,128]{3,1,2,0:T(8,128)}, f32[2,8,128,128]{3,1,2,0:T(8,128)}, f32[2,8,128,128]{3,1,2,0:T(8,128)S(1)}, f32[]{:T(128)}, /*i...) while((s32[]{:T(128)}, f32[2,8,128,128]{3,1,2,0:T(8,128)}, ...), condition=%wide.region_1.0_spmd.clone, body=%wide.region_0.0_spmd.clone.sunk | while | flops 7868424 | bytes 32735676 | solution.py:74
  40.6 2.8 collective-permute-start.3
  52.8 5.5 %multiply_add_fusion.2 = (f32[2,8,128,128]{3,1,2,0:T(8,128)S(1)}, f32[2,8,128,128]{3,1,2,0:T(8,128)}) fusion(f32[2,8,128,128]{3,1,2,0:T(8,128)S(1)} %get-tuple-element.423, f32[]{:T(128)S(6)} %div.33, f32[]{:T(128)S(6)} %mul.324, f32[2,8,128,128]{3,1,2,0:T(8,128)} %get-tuple-element.422, f32[2,8,128,1]{3,1,2,0:T(8,128)S(1)} %copy.128, ...), kind=kLoop, calls=%fused_computation.20.clone.1 | loop fusion | flops 7340032 | bytes 13631496 | tf_op jit(solution)/shard_map/while/body/eval_jaxpr/add | solution.py:71
  60.3 5.0 %collective-permute-start.3 = (f32[2,1,128,128]{3,1,2,0:T(1,128)}, f32[2,1,128,128]{3,1,2,0:T(1,128)S(1)}, u32[]{:S(2)}, u32[]{:S(2)}) collective-permute-start(f32[2,1,128,128]{3,1,2,0:T(1,128)} %get-tuple-element.397), channel_id=1, source_target_pairs={{0,248},{8,0},{16,8},{24,16},{32,24},{40,32},{48,40},{56,48},{64,5... | collective-permute-start | bytes 393224 | tf_op jit(solution)/shard_map/while/body/eval_jaxpr/ppermute | solution.py:14
  70.6 2.3 select_add_fusion.2
  75.4 5.6 %multiply_add_fusion.2 = (f32[2,8,128,128]{3,1,2,0:T(8,128)S(1)}, f32[2,8,128,128]{3,1,2,0:T(8,128)}) fusion(f32[2,8,128,128]{3,1,2,0:T(8,128)S(1)} %get-tuple-element.423, f32[]{:T(128)S(6)} %div.33, f32[]{:T(128)S(6)} %mul.324, f32[2,8,128,128]{3,1,2,0:T(8,128)} %get-tuple-element.422, f32[2,8,128,1]{3,1,2,0:T(8,128)S(1)} %copy.128, ...), kind=kLoop, calls=%fused_computation.20.clone.1 | loop fusion | flops 7340032 | bytes 13631496 | tf_op jit(solution)/shard_map/while/body/eval_jaxpr/add | solution.py:71
  83.7 5.1 %collective-permute-start.3 = (f32[2,1,128,128]{3,1,2,0:T(1,128)}, f32[2,1,128,128]{3,1,2,0:T(1,128)S(1)}, u32[]{:S(2)}, u32[]{:S(2)}) collective-permute-start(f32[2,1,128,128]{3,1,2,0:T(1,128)} %get-tuple-element.397), channel_id=1, source_target_pairs={{0,248},{8,0},{16,8},{24,16},{32,24},{40,32},{48,40},{56,48},{64,5... | collective-permute-start | bytes 393224 | tf_op jit(solution)/shard_map/while/body/eval_jaxpr/ppermute | solution.py:14
  93.8 2.3 select_add_fusion.2
  98.6 5.6 %multiply_add_fusion.2 = (f32[2,8,128,128]{3,1,2,0:T(8,128)S(1)}, f32[2,8,128,128]{3,1,2,0:T(8,128)}) fusion(f32[2,8,128,128]{3,1,2,0:T(8,128)S(1)} %get-tuple-element.423, f32[]{:T(128)S(6)} %div.33, f32[]{:T(128)S(6)} %mul.324, f32[2,8,128,128]{3,1,2,0:T(8,128)} %get-tuple-element.422, f32[2,8,128,1]{3,1,2,0:T(8,128)S(1)} %copy.128, ...), kind=kLoop, calls=%fused_computation.20.clone.1 | loop fusion | flops 7340032 | bytes 13631496 | tf_op jit(solution)/shard_map/while/body/eval_jaxpr/add | solution.py:71
  107.1 5.1 %collective-permute-start.3 = (f32[2,1,128,128]{3,1,2,0:T(1,128)}, f32[2,1,128,128]{3,1,2,0:T(1,128)S(1)}, u32[]{:S(2)}, u32[]{:S(2)}) collective-permute-start(f32[2,1,128,128]{3,1,2,0:T(1,128)} %get-tuple-element.397), channel_id=1, source_target_pairs={{0,248},{8,0},{16,8},{24,16},{32,24},{40,32},{48,40},{56,48},{64,5... | collective-permute-start | bytes 393224 | tf_op jit(solution)/shard_map/while/body/eval_jaxpr/ppermute | solution.py:14
  117.2 2.3 select_add_fusion.2
  122.0 5.6 %multiply_add_fusion.2 = (f32[2,8,128,128]{3,1,2,0:T(8,128)S(1)}, f32[2,8,128,128]{3,1,2,0:T(8,128)}) fusion(f32[2,8,128,128]{3,1,2,0:T(8,128)S(1)} %get-tuple-element.423, f32[]{:T(128)S(6)} %div.33, f32[]{:T(128)S(6)} %mul.324, f32[2,8,128,128]{3,1,2,0:T(8,128)} %get-tuple-element.422, f32[2,8,128,1]{3,1,2,0:T(8,128)S(1)} %copy.128, ...), kind=kLoop, calls=%fused_computation.20.clone.1 | loop fusion | flops 7340032 | bytes 13631496 | tf_op jit(solution)/shard_map/while/body/eval_jaxpr/add | solution.py:71
  130.6 5.1 %collective-permute-start.3 = (f32[2,1,128,128]{3,1,2,0:T(1,128)}, f32[2,1,128,128]{3,1,2,0:T(1,128)S(1)}, u32[]{:S(2)}, u32[]{:S(2)}) collective-permute-start(f32[2,1,128,128]{3,1,2,0:T(1,128)} %get-tuple-element.397), channel_id=1, source_target_pairs={{0,248},{8,0},{16,8},{24,16},{32,24},{40,32},{48,40},{56,48},{64,5... | collective-permute-start | bytes 393224 | tf_op jit(solution)/shard_map/while/body/eval_jaxpr/ppermute | solution.py:14
  140.7 2.3 select_add_fusion.2
  145.5 5.6 %multiply_add_fusion.2 = (f32[2,8,128,128]{3,1,2,0:T(8,128)S(1)}, f32[2,8,128,128]{3,1,2,0:T(8,128)}) fusion(f32[2,8,128,128]{3,1,2,0:T(8,128)S(1)} %get-tuple-element.423, f32[]{:T(128)S(6)} %div.33, f32[]{:T(128)S(6)} %mul.324, f32[2,8,128,128]{3,1,2,0:T(8,128)} %get-tuple-element.422, f32[2,8,128,1]{3,1,2,0:T(8,128)S(1)} %copy.128, ...), kind=kLoop, calls=%fused_computation.20.clone.1 | loop fusion | flops 7340032 | bytes 13631496 | tf_op jit(solution)/shard_map/while/body/eval_jaxpr/add | solution.py:71
  154.1 5.1 %collective-permute-start.3 = (f32[2,1,128,128]{3,1,2,0:T(1,128)}, f32[2,1,128,128]{3,1,2,0:T(1,128)S(1)}, u32[]{:S(2)}, u32[]{:S(2)}) collective-permute-start(f32[2,1,128,128]{3,1,2,0:T(1,128)} %get-tuple-element.397), channel_id=1, source_target_pairs={{0,248},{8,0},{16,8},{24,16},{32,24},{40,32},{48,40},{56,48},{64,5... | collective-permute-start | bytes 393224 | tf_op jit(solution)/shard_map/while/body/eval_jaxpr/ppermute | solution.py:14
  164.2 2.3 select_add_fusion.2
  168.9 5.6 %multiply_add_fusion.2 = (f32[2,8,128,128]{3,1,2,0:T(8,128)S(1)}, f32[2,8,128,128]{3,1,2,0:T(8,128)}) fusion(f32[2,8,128,128]{3,1,2,0:T(8,128)S(1)} %get-tuple-element.423, f32[]{:T(128)S(6)} %div.33, f32[]{:T(128)S(6)} %mul.324, f32[2,8,128,128]{3,1,2,0:T(8,128)} %get-tuple-element.422, f32[2,8,128,1]{3,1,2,0:T(8,128)S(1)} %copy.128, ...), kind=kLoop, calls=%fused_computation.20.clone.1 | loop fusion | flops 7340032 | bytes 13631496 | tf_op jit(solution)/shard_map/while/body/eval_jaxpr/add | solution.py:71
  177.5 5.1 %collective-permute-start.3 = (f32[2,1,128,128]{3,1,2,0:T(1,128)}, f32[2,1,128,128]{3,1,2,0:T(1,128)S(1)}, u32[]{:S(2)}, u32[]{:S(2)}) collective-permute-start(f32[2,1,128,128]{3,1,2,0:T(1,128)} %get-tuple-element.397), channel_id=1, source_target_pairs={{0,248},{8,0},{16,8},{24,16},{32,24},{40,32},{48,40},{56,48},{64,5... | collective-permute-start | bytes 393224 | tf_op jit(solution)/shard_map/while/body/eval_jaxpr/ppermute | solution.py:14
  187.6 2.3 select_add_fusion.2
  192.4 5.6 %multiply_add_fusion.2 = (f32[2,8,128,128]{3,1,2,0:T(8,128)S(1)}, f32[2,8,128,128]{3,1,2,0:T(8,128)}) fusion(f32[2,8,128,128]{3,1,2,0:T(8,128)S(1)} %get-tuple-element.423, f32[]{:T(128)S(6)} %div.33, f32[]{:T(128)S(6)} %mul.324, f32[2,8,128,128]{3,1,2,0:T(8,128)} %get-tuple-element.422, f32[2,8,128,1]{3,1,2,0:T(8,128)S(1)} %copy.128, ...), kind=kLoop, calls=%fused_computation.20.clone.1 | loop fusion | flops 7340032 | bytes 13631496 | tf_op jit(solution)/shard_map/while/body/eval_jaxpr/add | solution.py:71
  201.0 5.1 %collective-permute-start.3 = (f32[2,1,128,128]{3,1,2,0:T(1,128)}, f32[2,1,128,128]{3,1,2,0:T(1,128)S(1)}, u32[]{:S(2)}, u32[]{:S(2)}) collective-permute-start(f32[2,1,128,128]{3,1,2,0:T(1,128)} %get-tuple-element.397), channel_id=1, source_target_pairs={{0,248},{8,0},{16,8},{24,16},{32,24},{40,32},{48,40},{56,48},{64,5... | collective-permute-start | bytes 393224 | tf_op jit(solution)/shard_map/while/body/eval_jaxpr/ppermute | solution.py:14
  211.1 2.3 select_add_fusion.2
  215.8 5.6 %multiply_add_fusion.2 = (f32[2,8,128,128]{3,1,2,0:T(8,128)S(1)}, f32[2,8,128,128]{3,1,2,0:T(8,128)}) fusion(f32[2,8,128,128]{3,1,2,0:T(8,128)S(1)} %get-tuple-element.423, f32[]{:T(128)S(6)} %div.33, f32[]{:T(128)S(6)} %mul.324, f32[2,8,128,128]{3,1,2,0:T(8,128)} %get-tuple-element.422, f32[2,8,128,1]{3,1,2,0:T(8,128)S(1)} %copy.128, ...), kind=kLoop, calls=%fused_computation.20.clone.1 | loop fusion | flops 7340032 | bytes 13631496 | tf_op jit(solution)/shard_map/while/body/eval_jaxpr/add | solution.py:71
  224.4 5.1 %collective-permute-start.3 = (f32[2,1,128,128]{3,1,2,0:T(1,128)}, f32[2,1,128,128]{3,1,2,0:T(1,128)S(1)}, u32[]{:S(2)}, u32[]{:S(2)}) collective-permute-start(f32[2,1,128,128]{3,1,2,0:T(1,128)} %get-tuple-element.397), channel_id=1, source_target_pairs={{0,248},{8,0},{16,8},{24,16},{32,24},{40,32},{48,40},{56,48},{64,5... | collective-permute-start | bytes 393224 | tf_op jit(solution)/shard_map/while/body/eval_jaxpr/ppermute | solution.py:14
  234.6 2.3 select_add_fusion.2
  239.3 5.6 %multiply_add_fusion.2 = (f32[2,8,128,128]{3,1,2,0:T(8,128)S(1)}, f32[2,8,128,128]{3,1,2,0:T(8,128)}) fusion(f32[2,8,128,128]{3,1,2,0:T(8,128)S(1)} %get-tuple-element.423, f32[]{:T(128)S(6)} %div.33, f32[]{:T(128)S(6)} %mul.324, f32[2,8,128,128]{3,1,2,0:T(8,128)} %get-tuple-element.422, f32[2,8,128,1]{3,1,2,0:T(8,128)S(1)} %copy.128, ...), kind=kLoop, calls=%fused_computation.20.clone.1 | loop fusion | flops 7340032 | bytes 13631496 | tf_op jit(solution)/shard_map/while/body/eval_jaxpr/add | solution.py:71
  247.9 5.1 %collective-permute-start.3 = (f32[2,1,128,128]{3,1,2,0:T(1,128)}, f32[2,1,128,128]{3,1,2,0:T(1,128)S(1)}, u32[]{:S(2)}, u32[]{:S(2)}) collective-permute-start(f32[2,1,128,128]{3,1,2,0:T(1,128)} %get-tuple-element.397), channel_id=1, source_target_pairs={{0,248},{8,0},{16,8},{24,16},{32,24},{40,32},{48,40},{56,48},{64,5... | collective-permute-start | bytes 393224 | tf_op jit(solution)/shard_map/while/body/eval_jaxpr/ppermute | solution.py:14
  262.7 5.6 %multiply_add_fusion.2 = (f32[2,8,128,128]{3,1,2,0:T(8,128)S(1)}, f32[2,8,128,128]{3,1,2,0:T(8,128)}) fusion(f32[2,8,128,128]{3,1,2,0:T(8,128)S(1)} %get-tuple-element.423, f32[]{:T(128)S(6)} %div.33, f32[]{:T(128)S(6)} %mul.324, f32[2,8,128,128]{3,1,2,0:T(8,128)} %get-tuple-element.422, f32[2,8,128,1]{3,1,2,0:T(8,128)S(1)} %copy.128, ...), kind=kLoop, calls=%fused_computation.20.clone.1 | loop fusion | flops 7340032 | bytes 13631496 | tf_op jit(solution)/shard_map/while/body/eval_jaxpr/add | solution.py:71
  271.3 5.1 %collective-permute-start.3 = (f32[2,1,128,128]{3,1,2,0:T(1,128)}, f32[2,1,128,128]{3,1,2,0:T(1,128)S(1)}, u32[]{:S(2)}, u32[]{:S(2)}) collective-permute-start(f32[2,1,128,128]{3,1,2,0:T(1,128)} %get-tuple-element.397), channel_id=1, source_target_pairs={{0,248},{8,0},{16,8},{24,16},{32,24},{40,32},{48,40},{56,48},{64,5... | collective-permute-start | bytes 393224 | tf_op jit(solution)/shard_map/while/body/eval_jaxpr/ppermute | solution.py:14
  286.2 5.6 %multiply_add_fusion.2 = (f32[2,8,128,128]{3,1,2,0:T(8,128)S(1)}, f32[2,8,128,128]{3,1,2,0:T(8,128)}) fusion(f32[2,8,128,128]{3,1,2,0:T(8,128)S(1)} %get-tuple-element.423, f32[]{:T(128)S(6)} %div.33, f32[]{:T(128)S(6)} %mul.324, f32[2,8,128,128]{3,1,2,0:T(8,128)} %get-tuple-element.422, f32[2,8,128,1]{3,1,2,0:T(8,128)S(1)} %copy.128, ...), kind=kLoop, calls=%fused_computation.20.clone.1 | loop fusion | flops 7340032 | bytes 13631496 | tf_op jit(solution)/shard_map/while/body/eval_jaxpr/add | solution.py:71
  294.8 5.1 %collective-permute-start.3 = (f32[2,1,128,128]{3,1,2,0:T(1,128)}, f32[2,1,128,128]{3,1,2,0:T(1,128)S(1)}, u32[]{:S(2)}, u32[]{:S(2)}) collective-permute-start(f32[2,1,128,128]{3,1,2,0:T(1,128)} %get-tuple-element.397), channel_id=1, source_target_pairs={{0,248},{8,0},{16,8},{24,16},{32,24},{40,32},{48,40},{56,48},{64,5... | collective-permute-start | bytes 393224 | tf_op jit(solution)/shard_map/while/body/eval_jaxpr/ppermute | solution.py:14
  309.7 5.6 %multiply_add_fusion.2 = (f32[2,8,128,128]{3,1,2,0:T(8,128)S(1)}, f32[2,8,128,128]{3,1,2,0:T(8,128)}) fusion(f32[2,8,128,128]{3,1,2,0:T(8,128)S(1)} %get-tuple-element.423, f32[]{:T(128)S(6)} %div.33, f32[]{:T(128)S(6)} %mul.324, f32[2,8,128,128]{3,1,2,0:T(8,128)} %get-tuple-element.422, f32[2,8,128,1]{3,1,2,0:T(8,128)S(1)} %copy.128, ...), kind=kLoop, calls=%fused_computation.20.clone.1 | loop fusion | flops 7340032 | bytes 13631496 | tf_op jit(solution)/shard_map/while/body/eval_jaxpr/add | solution.py:71
  318.2 5.1 %collective-permute-start.3 = (f32[2,1,128,128]{3,1,2,0:T(1,128)}, f32[2,1,128,128]{3,1,2,0:T(1,128)S(1)}, u32[]{:S(2)}, u32[]{:S(2)}) collective-permute-start(f32[2,1,128,128]{3,1,2,0:T(1,128)} %get-tuple-element.397), channel_id=1, source_target_pairs={{0,248},{8,0},{16,8},{24,16},{32,24},{40,32},{48,40},{56,48},{64,5... | collective-permute-start | bytes 393224 | tf_op jit(solution)/shard_map/while/body/eval_jaxpr/ppermute | solution.py:14
  333.1 5.6 %multiply_add_fusion.2 = (f32[2,8,128,128]{3,1,2,0:T(8,128)S(1)}, f32[2,8,128,128]{3,1,2,0:T(8,128)}) fusion(f32[2,8,128,128]{3,1,2,0:T(8,128)S(1)} %get-tuple-element.423, f32[]{:T(128)S(6)} %div.33, f32[]{:T(128)S(6)} %mul.324, f32[2,8,128,128]{3,1,2,0:T(8,128)} %get-tuple-element.422, f32[2,8,128,1]{3,1,2,0:T(8,128)S(1)} %copy.128, ...), kind=kLoop, calls=%fused_computation.20.clone.1 | loop fusion | flops 7340032 | bytes 13631496 | tf_op jit(solution)/shard_map/while/body/eval_jaxpr/add | solution.py:71
  341.7 5.1 %collective-permute-start.3 = (f32[2,1,128,128]{3,1,2,0:T(1,128)}, f32[2,1,128,128]{3,1,2,0:T(1,128)S(1)}, u32[]{:S(2)}, u32[]{:S(2)}) collective-permute-start(f32[2,1,128,128]{3,1,2,0:T(1,128)} %get-tuple-element.397), channel_id=1, source_target_pairs={{0,248},{8,0},{16,8},{24,16},{32,24},{40,32},{48,40},{56,48},{64,5... | collective-permute-start | bytes 393224 | tf_op jit(solution)/shard_map/while/body/eval_jaxpr/ppermute | solution.py:14
  356.6 5.6 %multiply_add_fusion.2 = (f32[2,8,128,128]{3,1,2,0:T(8,128)S(1)}, f32[2,8,128,128]{3,1,2,0:T(8,128)}) fusion(f32[2,8,128,128]{3,1,2,0:T(8,128)S(1)} %get-tuple-element.423, f32[]{:T(128)S(6)} %div.33, f32[]{:T(128)S(6)} %mul.324, f32[2,8,128,128]{3,1,2,0:T(8,128)} %get-tuple-element.422, f32[2,8,128,1]{3,1,2,0:T(8,128)S(1)} %copy.128, ...), kind=kLoop, calls=%fused_computation.20.clone.1 | loop fusion | flops 7340032 | bytes 13631496 | tf_op jit(solution)/shard_map/while/body/eval_jaxpr/add | solution.py:71
  365.2 5.1 %collective-permute-start.3 = (f32[2,1,128,128]{3,1,2,0:T(1,128)}, f32[2,1,128,128]{3,1,2,0:T(1,128)S(1)}, u32[]{:S(2)}, u32[]{:S(2)}) collective-permute-start(f32[2,1,128,128]{3,1,2,0:T(1,128)} %get-tuple-element.397), channel_id=1, source_target_pairs={{0,248},{8,0},{16,8},{24,16},{32,24},{40,32},{48,40},{56,48},{64,5... | collective-permute-start | bytes 393224 | tf_op jit(solution)/shard_map/while/body/eval_jaxpr/ppermute | solution.py:14
  380.1 5.6 %multiply_add_fusion.2 = (f32[2,8,128,128]{3,1,2,0:T(8,128)S(1)}, f32[2,8,128,128]{3,1,2,0:T(8,128)}) fusion(f32[2,8,128,128]{3,1,2,0:T(8,128)S(1)} %get-tuple-element.423, f32[]{:T(128)S(6)} %div.33, f32[]{:T(128)S(6)} %mul.324, f32[2,8,128,128]{3,1,2,0:T(8,128)} %get-tuple-element.422, f32[2,8,128,1]{3,1,2,0:T(8,128)S(1)} %copy.128, ...), kind=kLoop, calls=%fused_computation.20.clone.1 | loop fusion | flops 7340032 | bytes 13631496 | tf_op jit(solution)/shard_map/while/body/eval_jaxpr/add | solution.py:71
  388.6 5.1 %collective-permute-start.3 = (f32[2,1,128,128]{3,1,2,0:T(1,128)}, f32[2,1,128,128]{3,1,2,0:T(1,128)S(1)}, u32[]{:S(2)}, u32[]{:S(2)}) collective-permute-start(f32[2,1,128,128]{3,1,2,0:T(1,128)} %get-tuple-element.397), channel_id=1, source_target_pairs={{0,248},{8,0},{16,8},{24,16},{32,24},{40,32},{48,40},{56,48},{64,5... | collective-permute-start | bytes 393224 | tf_op jit(solution)/shard_map/while/body/eval_jaxpr/ppermute | solution.py:14
  398.7 2.3 select_add_fusion.2
  403.5 5.6 %multiply_add_fusion.2 = (f32[2,8,128,128]{3,1,2,0:T(8,128)S(1)}, f32[2,8,128,128]{3,1,2,0:T(8,128)}) fusion(f32[2,8,128,128]{3,1,2,0:T(8,128)S(1)} %get-tuple-element.423, f32[]{:T(128)S(6)} %div.33, f32[]{:T(128)S(6)} %mul.324, f32[2,8,128,128]{3,1,2,0:T(8,128)} %get-tuple-element.422, f32[2,8,128,1]{3,1,2,0:T(8,128)S(1)} %copy.128, ...), kind=kLoop, calls=%fused_computation.20.clone.1 | loop fusion | flops 7340032 | bytes 13631496 | tf_op jit(solution)/shard_map/while/body/eval_jaxpr/add | solution.py:71
  423.8 5.3 %collective-permute-start.12 = (f32[2,1,128,128]{3,2,1,0:T(8,128)S(1)}, f32[2,1,128,128]{3,2,1,0:T(8,128)S(1)}, u32[]{:S(2)}, u32[]{:S(2)}) collective-permute-start(f32[2,1,128,128]{3,2,1,0:T(8,128)S(1)} %get-tuple-element.257), channel_id=1, source_target_pairs={{0,248},{8,0},{16,8},{24,16},{32,24},{40,32},{48,40},{56,48},{64,5... | collective-permute-start | bytes 393224 | tf_op jit(solution)/shard_map/ppermute | solution.py:14
  429.9 2.7 collective-permute-done.11
  432.6 3.7 maximum_subtract_fusion.6
  (398 shorter events, 218.8 us)
Async XLA Ops:
  2.0 28.4 %collective-permute-start.8 = (f32[8,1,128]{2,0,1:T(8,128)}, f32[8,1,128]{2,0,1:T(8,128)S(1)}, u32[]{:S(2)}, u32[]{:S(2)}) collective-permute-start(f32[8,1,128]{2,0,1:T(8,128)} %copy.118), channel_id=1, source_target_pairs={{0,2},{2,4},{4,6},{6,0},{1,3},{3,5},{5,7},{7,1},{8,10},{10,12},{12... | collective-permute-start | bytes 12296 | tf_op jit(solution)/shard_map/ppermute | solution.py:14
  2.6 27.8 %collective-permute-start.9 = (f32[8,1,128]{2,0,1:T(8,128)}, f32[8,1,128]{2,0,1:T(8,128)}, u32[]{:S(2)}, u32[]{:S(2)}) collective-permute-start(f32[8,1,128]{2,0,1:T(8,128)} %copy.119), channel_id=1, source_target_pairs={{0,6},{2,0},{4,2},{6,4},{1,7},{3,1},{5,3},{7,5},{8,14},{10,8},{12,... | collective-permute-start | bytes 12296 | tf_op jit(solution)/shard_map/ppermute | solution.py:14
  5.9 24.5 %collective-permute-start.6 = (f32[1,128,128]{2,0,1:T(1,128)}, f32[1,128,128]{2,0,1:T(1,128)S(1)}, u32[]{:S(2)}, u32[]{:S(2)}) collective-permute-start(f32[1,128,128]{2,0,1:T(1,128)} %bitcast.4), channel_id=1, source_target_pairs={{0,8},{8,16},{16,24},{24,32},{32,40},{40,48},{48,56},{56,64},{64,7... | collective-permute-start | bytes 196616 | tf_op jit(solution)/shard_map/ppermute | solution.py:14
  9.8 18.3 %collective-permute-start.10 = (f32[8,128,2]{1,0,2:T(8,128)}, f32[8,128,2]{1,0,2:T(8,128)S(1)}, u32[]{:S(2)}, u32[]{:S(2)}) collective-permute-start(f32[8,128,2]{1,0,2:T(8,128)} %pad_maximum_fusion.3), channel_id=1, source_target_pairs={{0,1},{1,0},{2,3},{3,2},{4,5},{5,4},{6,7},{7,6},{8,9},{9,8},{10,11... | collective-permute-start | bytes 24584 | tf_op jit(solution)/shard_map/ppermute | solution.py:14
  59.0 16.4 %collective-permute-start.1 = (f32[2,8,1,128]{3,1,2,0:T(8,128)}, f32[2,8,1,128]{3,1,2,0:T(8,128)S(1)}, u32[]{:S(2)}, u32[]{:S(2)}) collective-permute-start(f32[2,8,1,128]{3,1,2,0:T(8,128)} %get-tuple-element.393), channel_id=1, source_target_pairs={{0,6},{2,0},{4,2},{6,4},{1,7},{3,1},{5,3},{7,5},{8,14},{10,8},{12,... | collective-permute-start | bytes 24584 | tf_op jit(solution)/shard_map/while/body/eval_jaxpr/ppermute | solution.py:14
  59.4 15.9 %collective-permute-start.2 = (f32[2,8,1,128]{3,1,2,0:T(8,128)}, f32[2,8,1,128]{3,1,2,0:T(8,128)}, u32[]{:S(2)}, u32[]{:S(2)}) collective-permute-start(f32[2,8,1,128]{3,1,2,0:T(8,128)} %get-tuple-element.396), channel_id=1, source_target_pairs={{0,2},{2,4},{4,6},{6,0},{1,3},{3,5},{5,7},{7,1},{8,10},{10,12},{12... | collective-permute-start | bytes 24584 | tf_op jit(solution)/shard_map/while/body/eval_jaxpr/ppermute | solution.py:14
  60.3 15.1 %collective-permute-start.3 = (f32[2,1,128,128]{3,1,2,0:T(1,128)}, f32[2,1,128,128]{3,1,2,0:T(1,128)S(1)}, u32[]{:S(2)}, u32[]{:S(2)}) collective-permute-start(f32[2,1,128,128]{3,1,2,0:T(1,128)} %get-tuple-element.397), channel_id=1, source_target_pairs={{0,248},{8,0},{16,8},{24,16},{32,24},{40,32},{48,40},{56,48},{64,5... | collective-permute-start | bytes 393224 | tf_op jit(solution)/shard_map/while/body/eval_jaxpr/ppermute | solution.py:14
  81.6 17.0 %collective-permute-start.1 = (f32[2,8,1,128]{3,1,2,0:T(8,128)}, f32[2,8,1,128]{3,1,2,0:T(8,128)S(1)}, u32[]{:S(2)}, u32[]{:S(2)}) collective-permute-start(f32[2,8,1,128]{3,1,2,0:T(8,128)} %get-tuple-element.393), channel_id=1, source_target_pairs={{0,6},{2,0},{4,2},{6,4},{1,7},{3,1},{5,3},{7,5},{8,14},{10,8},{12,... | collective-permute-start | bytes 24584 | tf_op jit(solution)/shard_map/while/body/eval_jaxpr/ppermute | solution.py:14
  82.8 15.7 %collective-permute-start.2 = (f32[2,8,1,128]{3,1,2,0:T(8,128)}, f32[2,8,1,128]{3,1,2,0:T(8,128)}, u32[]{:S(2)}, u32[]{:S(2)}) collective-permute-start(f32[2,8,1,128]{3,1,2,0:T(8,128)} %get-tuple-element.396), channel_id=1, source_target_pairs={{0,2},{2,4},{4,6},{6,0},{1,3},{3,5},{5,7},{7,1},{8,10},{10,12},{12... | collective-permute-start | bytes 24584 | tf_op jit(solution)/shard_map/while/body/eval_jaxpr/ppermute | solution.py:14
  83.7 14.9 %collective-permute-start.3 = (f32[2,1,128,128]{3,1,2,0:T(1,128)}, f32[2,1,128,128]{3,1,2,0:T(1,128)S(1)}, u32[]{:S(2)}, u32[]{:S(2)}) collective-permute-start(f32[2,1,128,128]{3,1,2,0:T(1,128)} %get-tuple-element.397), channel_id=1, source_target_pairs={{0,248},{8,0},{16,8},{24,16},{32,24},{40,32},{48,40},{56,48},{64,5... | collective-permute-start | bytes 393224 | tf_op jit(solution)/shard_map/while/body/eval_jaxpr/ppermute | solution.py:14
  104.8 17.2 %collective-permute-start.1 = (f32[2,8,1,128]{3,1,2,0:T(8,128)}, f32[2,8,1,128]{3,1,2,0:T(8,128)S(1)}, u32[]{:S(2)}, u32[]{:S(2)}) collective-permute-start(f32[2,8,1,128]{3,1,2,0:T(8,128)} %get-tuple-element.393), channel_id=1, source_target_pairs={{0,6},{2,0},{4,2},{6,4},{1,7},{3,1},{5,3},{7,5},{8,14},{10,8},{12,... | collective-permute-start | bytes 24584 | tf_op jit(solution)/shard_map/while/body/eval_jaxpr/ppermute | solution.py:14
  106.3 15.6 %collective-permute-start.2 = (f32[2,8,1,128]{3,1,2,0:T(8,128)}, f32[2,8,1,128]{3,1,2,0:T(8,128)}, u32[]{:S(2)}, u32[]{:S(2)}) collective-permute-start(f32[2,8,1,128]{3,1,2,0:T(8,128)} %get-tuple-element.396), channel_id=1, source_target_pairs={{0,2},{2,4},{4,6},{6,0},{1,3},{3,5},{5,7},{7,1},{8,10},{10,12},{12... | collective-permute-start | bytes 24584 | tf_op jit(solution)/shard_map/while/body/eval_jaxpr/ppermute | solution.py:14
  128.2 17.3 %collective-permute-start.1 = (f32[2,8,1,128]{3,1,2,0:T(8,128)}, f32[2,8,1,128]{3,1,2,0:T(8,128)S(1)}, u32[]{:S(2)}, u32[]{:S(2)}) collective-permute-start(f32[2,8,1,128]{3,1,2,0:T(8,128)} %get-tuple-element.393), channel_id=1, source_target_pairs={{0,6},{2,0},{4,2},{6,4},{1,7},{3,1},{5,3},{7,5},{8,14},{10,8},{12,... | collective-permute-start | bytes 24584 | tf_op jit(solution)/shard_map/while/body/eval_jaxpr/ppermute | solution.py:14
  129.8 15.7 %collective-permute-start.2 = (f32[2,8,1,128]{3,1,2,0:T(8,128)}, f32[2,8,1,128]{3,1,2,0:T(8,128)}, u32[]{:S(2)}, u32[]{:S(2)}) collective-permute-start(f32[2,8,1,128]{3,1,2,0:T(8,128)} %get-tuple-element.396), channel_id=1, source_target_pairs={{0,2},{2,4},{4,6},{6,0},{1,3},{3,5},{5,7},{7,1},{8,10},{10,12},{12... | collective-permute-start | bytes 24584 | tf_op jit(solution)/shard_map/while/body/eval_jaxpr/ppermute | solution.py:14
  130.6 14.9 %collective-permute-start.3 = (f32[2,1,128,128]{3,1,2,0:T(1,128)}, f32[2,1,128,128]{3,1,2,0:T(1,128)S(1)}, u32[]{:S(2)}, u32[]{:S(2)}) collective-permute-start(f32[2,1,128,128]{3,1,2,0:T(1,128)} %get-tuple-element.397), channel_id=1, source_target_pairs={{0,248},{8,0},{16,8},{24,16},{32,24},{40,32},{48,40},{56,48},{64,5... | collective-permute-start | bytes 393224 | tf_op jit(solution)/shard_map/while/body/eval_jaxpr/ppermute | solution.py:14
  151.7 17.2 %collective-permute-start.1 = (f32[2,8,1,128]{3,1,2,0:T(8,128)}, f32[2,8,1,128]{3,1,2,0:T(8,128)S(1)}, u32[]{:S(2)}, u32[]{:S(2)}) collective-permute-start(f32[2,8,1,128]{3,1,2,0:T(8,128)} %get-tuple-element.393), channel_id=1, source_target_pairs={{0,6},{2,0},{4,2},{6,4},{1,7},{3,1},{5,3},{7,5},{8,14},{10,8},{12,... | collective-permute-start | bytes 24584 | tf_op jit(solution)/shard_map/while/body/eval_jaxpr/ppermute | solution.py:14
  153.2 15.6 %collective-permute-start.2 = (f32[2,8,1,128]{3,1,2,0:T(8,128)}, f32[2,8,1,128]{3,1,2,0:T(8,128)}, u32[]{:S(2)}, u32[]{:S(2)}) collective-permute-start(f32[2,8,1,128]{3,1,2,0:T(8,128)} %get-tuple-element.396), channel_id=1, source_target_pairs={{0,2},{2,4},{4,6},{6,0},{1,3},{3,5},{5,7},{7,1},{8,10},{10,12},{12... | collective-permute-start | bytes 24584 | tf_op jit(solution)/shard_map/while/body/eval_jaxpr/ppermute | solution.py:14
  154.1 14.8 %collective-permute-start.3 = (f32[2,1,128,128]{3,1,2,0:T(1,128)}, f32[2,1,128,128]{3,1,2,0:T(1,128)S(1)}, u32[]{:S(2)}, u32[]{:S(2)}) collective-permute-start(f32[2,1,128,128]{3,1,2,0:T(1,128)} %get-tuple-element.397), channel_id=1, source_target_pairs={{0,248},{8,0},{16,8},{24,16},{32,24},{40,32},{48,40},{56,48},{64,5... | collective-permute-start | bytes 393224 | tf_op jit(solution)/shard_map/while/body/eval_jaxpr/ppermute | solution.py:14
  175.1 17.3 %collective-permute-start.1 = (f32[2,8,1,128]{3,1,2,0:T(8,128)}, f32[2,8,1,128]{3,1,2,0:T(8,128)S(1)}, u32[]{:S(2)}, u32[]{:S(2)}) collective-permute-start(f32[2,8,1,128]{3,1,2,0:T(8,128)} %get-tuple-element.393), channel_id=1, source_target_pairs={{0,6},{2,0},{4,2},{6,4},{1,7},{3,1},{5,3},{7,5},{8,14},{10,8},{12,... | collective-permute-start | bytes 24584 | tf_op jit(solution)/shard_map/while/body/eval_jaxpr/ppermute | solution.py:14
  176.7 15.7 %collective-permute-start.2 = (f32[2,8,1,128]{3,1,2,0:T(8,128)}, f32[2,8,1,128]{3,1,2,0:T(8,128)}, u32[]{:S(2)}, u32[]{:S(2)}) collective-permute-start(f32[2,8,1,128]{3,1,2,0:T(8,128)} %get-tuple-element.396), channel_id=1, source_target_pairs={{0,2},{2,4},{4,6},{6,0},{1,3},{3,5},{5,7},{7,1},{8,10},{10,12},{12... | collective-permute-start | bytes 24584 | tf_op jit(solution)/shard_map/while/body/eval_jaxpr/ppermute | solution.py:14
  177.5 14.9 %collective-permute-start.3 = (f32[2,1,128,128]{3,1,2,0:T(1,128)}, f32[2,1,128,128]{3,1,2,0:T(1,128)S(1)}, u32[]{:S(2)}, u32[]{:S(2)}) collective-permute-start(f32[2,1,128,128]{3,1,2,0:T(1,128)} %get-tuple-element.397), channel_id=1, source_target_pairs={{0,248},{8,0},{16,8},{24,16},{32,24},{40,32},{48,40},{56,48},{64,5... | collective-permute-start | bytes 393224 | tf_op jit(solution)/shard_map/while/body/eval_jaxpr/ppermute | solution.py:14
  198.6 17.2 %collective-permute-start.1 = (f32[2,8,1,128]{3,1,2,0:T(8,128)}, f32[2,8,1,128]{3,1,2,0:T(8,128)S(1)}, u32[]{:S(2)}, u32[]{:S(2)}) collective-permute-start(f32[2,8,1,128]{3,1,2,0:T(8,128)} %get-tuple-element.393), channel_id=1, source_target_pairs={{0,6},{2,0},{4,2},{6,4},{1,7},{3,1},{5,3},{7,5},{8,14},{10,8},{12,... | collective-permute-start | bytes 24584 | tf_op jit(solution)/shard_map/while/body/eval_jaxpr/ppermute | solution.py:14
  200.2 15.6 %collective-permute-start.2 = (f32[2,8,1,128]{3,1,2,0:T(8,128)}, f32[2,8,1,128]{3,1,2,0:T(8,128)}, u32[]{:S(2)}, u32[]{:S(2)}) collective-permute-start(f32[2,8,1,128]{3,1,2,0:T(8,128)} %get-tuple-element.396), channel_id=1, source_target_pairs={{0,2},{2,4},{4,6},{6,0},{1,3},{3,5},{5,7},{7,1},{8,10},{10,12},{12... | collective-permute-start | bytes 24584 | tf_op jit(solution)/shard_map/while/body/eval_jaxpr/ppermute | solution.py:14
  201.0 14.8 %collective-permute-start.3 = (f32[2,1,128,128]{3,1,2,0:T(1,128)}, f32[2,1,128,128]{3,1,2,0:T(1,128)S(1)}, u32[]{:S(2)}, u32[]{:S(2)}) collective-permute-start(f32[2,1,128,128]{3,1,2,0:T(1,128)} %get-tuple-element.397), channel_id=1, source_target_pairs={{0,248},{8,0},{16,8},{24,16},{32,24},{40,32},{48,40},{56,48},{64,5... | collective-permute-start | bytes 393224 | tf_op jit(solution)/shard_map/while/body/eval_jaxpr/ppermute | solution.py:14
  222.0 17.3 %collective-permute-start.1 = (f32[2,8,1,128]{3,1,2,0:T(8,128)}, f32[2,8,1,128]{3,1,2,0:T(8,128)S(1)}, u32[]{:S(2)}, u32[]{:S(2)}) collective-permute-start(f32[2,8,1,128]{3,1,2,0:T(8,128)} %get-tuple-element.393), channel_id=1, source_target_pairs={{0,6},{2,0},{4,2},{6,4},{1,7},{3,1},{5,3},{7,5},{8,14},{10,8},{12,... | collective-permute-start | bytes 24584 | tf_op jit(solution)/shard_map/while/body/eval_jaxpr/ppermute | solution.py:14
  223.6 15.7 %collective-permute-start.2 = (f32[2,8,1,128]{3,1,2,0:T(8,128)}, f32[2,8,1,128]{3,1,2,0:T(8,128)}, u32[]{:S(2)}, u32[]{:S(2)}) collective-permute-start(f32[2,8,1,128]{3,1,2,0:T(8,128)} %get-tuple-element.396), channel_id=1, source_target_pairs={{0,2},{2,4},{4,6},{6,0},{1,3},{3,5},{5,7},{7,1},{8,10},{10,12},{12... | collective-permute-start | bytes 24584 | tf_op jit(solution)/shard_map/while/body/eval_jaxpr/ppermute | solution.py:14
  224.4 14.9 %collective-permute-start.3 = (f32[2,1,128,128]{3,1,2,0:T(1,128)}, f32[2,1,128,128]{3,1,2,0:T(1,128)S(1)}, u32[]{:S(2)}, u32[]{:S(2)}) collective-permute-start(f32[2,1,128,128]{3,1,2,0:T(1,128)} %get-tuple-element.397), channel_id=1, source_target_pairs={{0,248},{8,0},{16,8},{24,16},{32,24},{40,32},{48,40},{56,48},{64,5... | collective-permute-start | bytes 393224 | tf_op jit(solution)/shard_map/while/body/eval_jaxpr/ppermute | solution.py:14
  245.5 17.2 %collective-permute-start.1 = (f32[2,8,1,128]{3,1,2,0:T(8,128)}, f32[2,8,1,128]{3,1,2,0:T(8,128)S(1)}, u32[]{:S(2)}, u32[]{:S(2)}) collective-permute-start(f32[2,8,1,128]{3,1,2,0:T(8,128)} %get-tuple-element.393), channel_id=1, source_target_pairs={{0,6},{2,0},{4,2},{6,4},{1,7},{3,1},{5,3},{7,5},{8,14},{10,8},{12,... | collective-permute-start | bytes 24584 | tf_op jit(solution)/shard_map/while/body/eval_jaxpr/ppermute | solution.py:14
  247.1 15.6 %collective-permute-start.2 = (f32[2,8,1,128]{3,1,2,0:T(8,128)}, f32[2,8,1,128]{3,1,2,0:T(8,128)}, u32[]{:S(2)}, u32[]{:S(2)}) collective-permute-start(f32[2,8,1,128]{3,1,2,0:T(8,128)} %get-tuple-element.396), channel_id=1, source_target_pairs={{0,2},{2,4},{4,6},{6,0},{1,3},{3,5},{5,7},{7,1},{8,10},{10,12},{12... | collective-permute-start | bytes 24584 | tf_op jit(solution)/shard_map/while/body/eval_jaxpr/ppermute | solution.py:14
  247.9 14.8 %collective-permute-start.3 = (f32[2,1,128,128]{3,1,2,0:T(1,128)}, f32[2,1,128,128]{3,1,2,0:T(1,128)S(1)}, u32[]{:S(2)}, u32[]{:S(2)}) collective-permute-start(f32[2,1,128,128]{3,1,2,0:T(1,128)} %get-tuple-element.397), channel_id=1, source_target_pairs={{0,248},{8,0},{16,8},{24,16},{32,24},{40,32},{48,40},{56,48},{64,5... | collective-permute-start | bytes 393224 | tf_op jit(solution)/shard_map/while/body/eval_jaxpr/ppermute | solution.py:14
  268.9 17.3 %collective-permute-start.1 = (f32[2,8,1,128]{3,1,2,0:T(8,128)}, f32[2,8,1,128]{3,1,2,0:T(8,128)S(1)}, u32[]{:S(2)}, u32[]{:S(2)}) collective-permute-start(f32[2,8,1,128]{3,1,2,0:T(8,128)} %get-tuple-element.393), channel_id=1, source_target_pairs={{0,6},{2,0},{4,2},{6,4},{1,7},{3,1},{5,3},{7,5},{8,14},{10,8},{12,... | collective-permute-start | bytes 24584 | tf_op jit(solution)/shard_map/while/body/eval_jaxpr/ppermute | solution.py:14
  270.5 15.7 %collective-permute-start.2 = (f32[2,8,1,128]{3,1,2,0:T(8,128)}, f32[2,8,1,128]{3,1,2,0:T(8,128)}, u32[]{:S(2)}, u32[]{:S(2)}) collective-permute-start(f32[2,8,1,128]{3,1,2,0:T(8,128)} %get-tuple-element.396), channel_id=1, source_target_pairs={{0,2},{2,4},{4,6},{6,0},{1,3},{3,5},{5,7},{7,1},{8,10},{10,12},{12... | collective-permute-start | bytes 24584 | tf_op jit(solution)/shard_map/while/body/eval_jaxpr/ppermute | solution.py:14
  271.3 14.9 %collective-permute-start.3 = (f32[2,1,128,128]{3,1,2,0:T(1,128)}, f32[2,1,128,128]{3,1,2,0:T(1,128)S(1)}, u32[]{:S(2)}, u32[]{:S(2)}) collective-permute-start(f32[2,1,128,128]{3,1,2,0:T(1,128)} %get-tuple-element.397), channel_id=1, source_target_pairs={{0,248},{8,0},{16,8},{24,16},{32,24},{40,32},{48,40},{56,48},{64,5... | collective-permute-start | bytes 393224 | tf_op jit(solution)/shard_map/while/body/eval_jaxpr/ppermute | solution.py:14
  292.4 17.2 %collective-permute-start.1 = (f32[2,8,1,128]{3,1,2,0:T(8,128)}, f32[2,8,1,128]{3,1,2,0:T(8,128)S(1)}, u32[]{:S(2)}, u32[]{:S(2)}) collective-permute-start(f32[2,8,1,128]{3,1,2,0:T(8,128)} %get-tuple-element.393), channel_id=1, source_target_pairs={{0,6},{2,0},{4,2},{6,4},{1,7},{3,1},{5,3},{7,5},{8,14},{10,8},{12,... | collective-permute-start | bytes 24584 | tf_op jit(solution)/shard_map/while/body/eval_jaxpr/ppermute | solution.py:14
  294.0 15.6 %collective-permute-start.2 = (f32[2,8,1,128]{3,1,2,0:T(8,128)}, f32[2,8,1,128]{3,1,2,0:T(8,128)}, u32[]{:S(2)}, u32[]{:S(2)}) collective-permute-start(f32[2,8,1,128]{3,1,2,0:T(8,128)} %get-tuple-element.396), channel_id=1, source_target_pairs={{0,2},{2,4},{4,6},{6,0},{1,3},{3,5},{5,7},{7,1},{8,10},{10,12},{12... | collective-permute-start | bytes 24584 | tf_op jit(solution)/shard_map/while/body/eval_jaxpr/ppermute | solution.py:14
  294.8 14.8 %collective-permute-start.3 = (f32[2,1,128,128]{3,1,2,0:T(1,128)}, f32[2,1,128,128]{3,1,2,0:T(1,128)S(1)}, u32[]{:S(2)}, u32[]{:S(2)}) collective-permute-start(f32[2,1,128,128]{3,1,2,0:T(1,128)} %get-tuple-element.397), channel_id=1, source_target_pairs={{0,248},{8,0},{16,8},{24,16},{32,24},{40,32},{48,40},{56,48},{64,5... | collective-permute-start | bytes 393224 | tf_op jit(solution)/shard_map/while/body/eval_jaxpr/ppermute | solution.py:14
  315.9 17.3 %collective-permute-start.1 = (f32[2,8,1,128]{3,1,2,0:T(8,128)}, f32[2,8,1,128]{3,1,2,0:T(8,128)S(1)}, u32[]{:S(2)}, u32[]{:S(2)}) collective-permute-start(f32[2,8,1,128]{3,1,2,0:T(8,128)} %get-tuple-element.393), channel_id=1, source_target_pairs={{0,6},{2,0},{4,2},{6,4},{1,7},{3,1},{5,3},{7,5},{8,14},{10,8},{12,... | collective-permute-start | bytes 24584 | tf_op jit(solution)/shard_map/while/body/eval_jaxpr/ppermute | solution.py:14
  317.4 15.7 %collective-permute-start.2 = (f32[2,8,1,128]{3,1,2,0:T(8,128)}, f32[2,8,1,128]{3,1,2,0:T(8,128)}, u32[]{:S(2)}, u32[]{:S(2)}) collective-permute-start(f32[2,8,1,128]{3,1,2,0:T(8,128)} %get-tuple-element.396), channel_id=1, source_target_pairs={{0,2},{2,4},{4,6},{6,0},{1,3},{3,5},{5,7},{7,1},{8,10},{10,12},{12... | collective-permute-start | bytes 24584 | tf_op jit(solution)/shard_map/while/body/eval_jaxpr/ppermute | solution.py:14
  318.2 14.9 %collective-permute-start.3 = (f32[2,1,128,128]{3,1,2,0:T(1,128)}, f32[2,1,128,128]{3,1,2,0:T(1,128)S(1)}, u32[]{:S(2)}, u32[]{:S(2)}) collective-permute-start(f32[2,1,128,128]{3,1,2,0:T(1,128)} %get-tuple-element.397), channel_id=1, source_target_pairs={{0,248},{8,0},{16,8},{24,16},{32,24},{40,32},{48,40},{56,48},{64,5... | collective-permute-start | bytes 393224 | tf_op jit(solution)/shard_map/while/body/eval_jaxpr/ppermute | solution.py:14
  339.3 17.2 %collective-permute-start.1 = (f32[2,8,1,128]{3,1,2,0:T(8,128)}, f32[2,8,1,128]{3,1,2,0:T(8,128)S(1)}, u32[]{:S(2)}, u32[]{:S(2)}) collective-permute-start(f32[2,8,1,128]{3,1,2,0:T(8,128)} %get-tuple-element.393), channel_id=1, source_target_pairs={{0,6},{2,0},{4,2},{6,4},{1,7},{3,1},{5,3},{7,5},{8,14},{10,8},{12,... | collective-permute-start | bytes 24584 | tf_op jit(solution)/shard_map/while/body/eval_jaxpr/ppermute | solution.py:14
  340.9 15.6 %collective-permute-start.2 = (f32[2,8,1,128]{3,1,2,0:T(8,128)}, f32[2,8,1,128]{3,1,2,0:T(8,128)}, u32[]{:S(2)}, u32[]{:S(2)}) collective-permute-start(f32[2,8,1,128]{3,1,2,0:T(8,128)} %get-tuple-element.396), channel_id=1, source_target_pairs={{0,2},{2,4},{4,6},{6,0},{1,3},{3,5},{5,7},{7,1},{8,10},{10,12},{12... | collective-permute-start | bytes 24584 | tf_op jit(solution)/shard_map/while/body/eval_jaxpr/ppermute | solution.py:14
  341.7 14.8 %collective-permute-start.3 = (f32[2,1,128,128]{3,1,2,0:T(1,128)}, f32[2,1,128,128]{3,1,2,0:T(1,128)S(1)}, u32[]{:S(2)}, u32[]{:S(2)}) collective-permute-start(f32[2,1,128,128]{3,1,2,0:T(1,128)} %get-tuple-element.397), channel_id=1, source_target_pairs={{0,248},{8,0},{16,8},{24,16},{32,24},{40,32},{48,40},{56,48},{64,5... | collective-permute-start | bytes 393224 | tf_op jit(solution)/shard_map/while/body/eval_jaxpr/ppermute | solution.py:14
  362.8 17.3 %collective-permute-start.1 = (f32[2,8,1,128]{3,1,2,0:T(8,128)}, f32[2,8,1,128]{3,1,2,0:T(8,128)S(1)}, u32[]{:S(2)}, u32[]{:S(2)}) collective-permute-start(f32[2,8,1,128]{3,1,2,0:T(8,128)} %get-tuple-element.393), channel_id=1, source_target_pairs={{0,6},{2,0},{4,2},{6,4},{1,7},{3,1},{5,3},{7,5},{8,14},{10,8},{12,... | collective-permute-start | bytes 24584 | tf_op jit(solution)/shard_map/while/body/eval_jaxpr/ppermute | solution.py:14
  364.3 15.7 %collective-permute-start.2 = (f32[2,8,1,128]{3,1,2,0:T(8,128)}, f32[2,8,1,128]{3,1,2,0:T(8,128)}, u32[]{:S(2)}, u32[]{:S(2)}) collective-permute-start(f32[2,8,1,128]{3,1,2,0:T(8,128)} %get-tuple-element.396), channel_id=1, source_target_pairs={{0,2},{2,4},{4,6},{6,0},{1,3},{3,5},{5,7},{7,1},{8,10},{10,12},{12... | collective-permute-start | bytes 24584 | tf_op jit(solution)/shard_map/while/body/eval_jaxpr/ppermute | solution.py:14
  365.2 14.9 %collective-permute-start.3 = (f32[2,1,128,128]{3,1,2,0:T(1,128)}, f32[2,1,128,128]{3,1,2,0:T(1,128)S(1)}, u32[]{:S(2)}, u32[]{:S(2)}) collective-permute-start(f32[2,1,128,128]{3,1,2,0:T(1,128)} %get-tuple-element.397), channel_id=1, source_target_pairs={{0,248},{8,0},{16,8},{24,16},{32,24},{40,32},{48,40},{56,48},{64,5... | collective-permute-start | bytes 393224 | tf_op jit(solution)/shard_map/while/body/eval_jaxpr/ppermute | solution.py:14
  386.2 17.2 %collective-permute-start.1 = (f32[2,8,1,128]{3,1,2,0:T(8,128)}, f32[2,8,1,128]{3,1,2,0:T(8,128)S(1)}, u32[]{:S(2)}, u32[]{:S(2)}) collective-permute-start(f32[2,8,1,128]{3,1,2,0:T(8,128)} %get-tuple-element.393), channel_id=1, source_target_pairs={{0,6},{2,0},{4,2},{6,4},{1,7},{3,1},{5,3},{7,5},{8,14},{10,8},{12,... | collective-permute-start | bytes 24584 | tf_op jit(solution)/shard_map/while/body/eval_jaxpr/ppermute | solution.py:14
  387.8 15.6 %collective-permute-start.2 = (f32[2,8,1,128]{3,1,2,0:T(8,128)}, f32[2,8,1,128]{3,1,2,0:T(8,128)}, u32[]{:S(2)}, u32[]{:S(2)}) collective-permute-start(f32[2,8,1,128]{3,1,2,0:T(8,128)} %get-tuple-element.396), channel_id=1, source_target_pairs={{0,2},{2,4},{4,6},{6,0},{1,3},{3,5},{5,7},{7,1},{8,10},{10,12},{12... | collective-permute-start | bytes 24584 | tf_op jit(solution)/shard_map/while/body/eval_jaxpr/ppermute | solution.py:14
  388.6 14.8 %collective-permute-start.3 = (f32[2,1,128,128]{3,1,2,0:T(1,128)}, f32[2,1,128,128]{3,1,2,0:T(1,128)S(1)}, u32[]{:S(2)}, u32[]{:S(2)}) collective-permute-start(f32[2,1,128,128]{3,1,2,0:T(1,128)} %get-tuple-element.397), channel_id=1, source_target_pairs={{0,248},{8,0},{16,8},{24,16},{32,24},{40,32},{48,40},{56,48},{64,5... | collective-permute-start | bytes 393224 | tf_op jit(solution)/shard_map/while/body/eval_jaxpr/ppermute | solution.py:14
  (49 other events, 415.5 us)

commit v2 on v1

--- a/solution.py
+++ b/solution.py
@@ -1,10 +1,15 @@
+import functools
+
 import jax
 import jax.numpy as jnp
 from jax import lax
+from jax.experimental import pallas as pl
+from jax.experimental.pallas import tpu as pltpu
 from jax.sharding import PartitionSpec as P
 
 CHEB = 16
 
+MESH = pl.DeviceIdType.MESH
 
 time_step = 8.0
 
@@ -42,17 +47,142 @@
     return out
 
 
-def apply_operator(direction, weights):
-    near = neighbours(direction, halos(direction))
-    summed = jnp.zeros_like(direction)
-    for w, n in zip(weights, near):
-        summed = summed + w * (direction - n)
-    return direction + summed
+def solve_kernel(ngx, ngy, ab_ref, w_ref, rhs_ref, d0_ref, x_ref, r_ref,
+                 dbuf, sx, sy, sz, rx, ry, rz, send_sem, recv_sem):
+    S, X, Y, Z = rhs_ref.shape
+    gx = lax.axis_index("gx")
+    gy = lax.axis_index("gy")
+    pa = lax.axis_index("pa")
+    gx_prev = lax.rem(gx + ngx - 1, ngx)
+    gx_next = lax.rem(gx + 1, ngx)
+    gy_prev = lax.rem(gy + ngy - 1, ngy)
+    gy_next = lax.rem(gy + 1, ngy)
+    partner = 1 - pa
+    peers = ((gx_prev, gy, pa), (gx_next, gy, pa), (gx, gy_prev, pa), (gx, gy_next, pa), (gx, gy, partner))
+
+    barrier = pltpu.get_barrier_semaphore()
+    for dev in peers:
+        pl.semaphore_signal(barrier, inc=1, device_id=dev, device_id_type=MESH)
+    pl.semaphore_wait(barrier, len(peers))
+
+    def copies(slot):
+        plan = (
+            (sx.at[0], rx.at[slot, 1], peers[0]),
+            (sx.at[1], rx.at[slot, 0], peers[1]),
+            (sy.at[0], ry.at[slot, 1], peers[2]),
+            (sy.at[1], ry.at[slot, 0], peers[3]),
+            (sz, rz.at[slot], peers[4]),
+        )
+        return [
+            pltpu.make_async_remote_copy(
+                src_ref=src, dst_ref=dst, send_sem=send_sem.at[i, slot], recv_sem=recv_sem.at[i, slot],
+                device_id=dev, device_id_type=MESH,
+            )
+            for i, (src, dst, dev) in enumerate(plan)
+        ]
+
+    def put_faces(s, xi, plane):
+        if xi == 0:
+            sx[0, s] = plane
+        if xi == X - 1:
+            sx[1, s] = plane
+        sy[0, s, pl.ds(xi, 1), :] = plane[0:1, :]
+        sy[1, s, pl.ds(xi, 1), :] = plane[Y - 1:Y, :]
+        t = plane.T
+        sz[0, s, pl.ds(xi, 1), :] = t[0:1, :]
+        sz[1, s, pl.ds(xi, 1), :] = t[Z - 1:Z, :]
+
+    row = lax.broadcasted_iota(jnp.int32, (Y, Z), 0)
+    lane = lax.broadcasted_iota(jnp.int32, (Y, Z), 1)
+
+    for s in range(S):
+        for xi in range(X):
+            plane = d0_ref[s, xi]
+            dbuf[0, s, xi] = plane
+            x_ref[s, xi] = jnp.zeros((Y, Z), jnp.float32)
+            r_ref[s, xi] = rhs_ref[s, xi]
+            put_faces(s, xi, plane)
+    for c in copies(0):
+        c.start()
+
+    def step(k, carry):
+        slot = lax.rem(k, 2)
+        nslot = 1 - slot
+        for c in copies(slot):
+            c.wait()
+        a = ab_ref[0, k]
+        b = ab_ref[1, k]
+        last = k == CHEB - 1
+        for s in range(S):
+            for xi in range(X):
+                c = dbuf[slot, s, xi]
+                xm = dbuf[slot, s, xi - 1] if xi > 0 else rx[slot, 0, s]
+                xp = dbuf[slot, s, xi + 1] if xi < X - 1 else rx[slot, 1, s]
+                ym = jnp.where(row == 0, jnp.broadcast_to(ry[slot, 0, s, pl.ds(xi, 1), :], (Y, Z)),
+                               pltpu.roll(c, 1, 0))
+                yp = jnp.where(row == Y - 1, jnp.broadcast_to(ry[slot, 1, s, pl.ds(xi, 1), :], (Y, Z)),
+                               pltpu.roll(c, Y - 1, 0))
+                zpair = jnp.where(
+                    row < Y // 2,
+                    jnp.broadcast_to(rz[slot, 1, s, pl.ds(xi, 1), :], (Y, Z)),
+                    jnp.broadcast_to(rz[slot, 0, s, pl.ds(xi, 1), :], (Y, Z)),
+                ).T
+                zm = jnp.where(lane == 0, zpair, pltpu.roll(c, 1, 1))
+                zp = jnp.where(lane == Z - 1, zpair, pltpu.roll(c, Z - 1, 1))
+                summed = w_ref[0, xi] * (c - xm)
+                summed = summed + w_ref[1, xi] * (c - xp)
+                summed = summed + w_ref[2, xi] * (c - ym)
+                summed = summed + w_ref[3, xi] * (c - yp)
+                summed = summed + w_ref[4, xi] * (c - zm)
+                summed = summed + w_ref[5, xi] * (c - zp)
+                x_ref[s, xi] = x_ref[s, xi] + c
+                res = r_ref[s, xi] - (c + summed)
+                r_ref[s, xi] = res
+                nd = a * c + b * res
+                dbuf[nslot, s, xi] = nd
+                put_faces(s, xi, nd)
+
+        @pl.when(jnp.logical_not(last))
+        def _():
+            for c in copies(nslot):
+                c.start()
+
+        return carry
+
+    lax.fori_loop(0, CHEB, step, 0)
+
+
+def chebyshev_solve(weights, rhs, d0, ab):
+    S, X, Y, Z = rhs.shape
+    ngx = lax.axis_size("gx")
+    ngy = lax.axis_size("gy")
+    f32 = jnp.float32
+    vmem = pl.BlockSpec(memory_space=pltpu.VMEM)
+    return pl.pallas_call(
+        functools.partial(solve_kernel, ngx, ngy),
+        out_shape=(jax.ShapeDtypeStruct(rhs.shape, f32), jax.ShapeDtypeStruct(rhs.shape, f32)),
+        in_specs=[pl.BlockSpec(memory_space=pltpu.SMEM), vmem, vmem, vmem],
+        out_specs=(vmem, vmem),
+        scratch_shapes=[
+            pltpu.VMEM((2, S, X, Y, Z), f32),
+            pltpu.VMEM((2, S, Y, Z), f32),
+            pltpu.VMEM((2, S, X, Z), f32),
+            pltpu.VMEM((2, S, X, Y), f32),
+            pltpu.VMEM((2, 2, S, Y, Z), f32),
+            pltpu.VMEM((2, 2, S, X, Z), f32),
+            pltpu.VMEM((2, 2, S, X, Y), f32),
+            pltpu.SemaphoreType.DMA((5, 2)),
+            pltpu.SemaphoreType.DMA((5, 2)),
+        ],
+        compiler_params=pltpu.CompilerParams(
+            collective_id=0, has_side_effects=True, vmem_limit_bytes=60 * 1024 * 1024
+        ),
+    )(ab, weights, rhs, d0)
 
 
 def body(conductivity, stored_state, row_scales, cotangent, upper_bound):
     upper = upper_bound[0]
-    weights = [(conductivity + kn) * (0.5 * time_step) for kn in neighbours(conductivity, halos(conductivity))]
+    weights = jnp.stack([(conductivity + kn) * (0.5 * time_step) for kn in neighbours(conductivity, halos(conductivity))])
     partner = ring(stored_state, "pa", 1)
     previous = partner.astype(jnp.float32) * row_scales[:, :, None]
     rhs = jnp.stack((previous, cotangent))
@@ -61,17 +191,14 @@
     delta = 0.5 * (upper - 1.0)
     sigma = theta / delta
     rho = 1.0 / sigma
-    start = (jnp.zeros_like(rhs), rhs, rhs / theta, rho)
-
-    def sweep(step, carry):
-        solution, residual, direction, rho_now = carry
-        solution = solution + direction
-        residual = residual - apply_operator(direction, weights)
-        rho_next = 1.0 / (2.0 * sigma - rho_now)
-        direction = rho_next * rho_now * direction + 2.0 * rho_next / delta * residual
-        return (solution, residual, direction, rho_next)
-
-    solved, residuals, _, _ = lax.fori_loop(0, CHEB, sweep, start)
+    coefs = []
+    for _ in range(CHEB):
+        rho_next = 1.0 / (2.0 * sigma - rho)
+        coefs.append((rho_next * rho, 2.0 * rho_next / delta))
+        rho = rho_next
+    ab = jnp.stack([jnp.stack([c[0] for c in coefs]), jnp.stack([c[1] for c in coefs])])
+
+    solved, residuals = chebyshev_solve(weights, rhs, rhs / theta, ab)
     near = neighbours(solved, halos(solved))
     summed = jnp.zeros_like(solved[0])
     for n in near:

time: 440 us -> 197 us (0.45)
  Pallas kernels: 0 us -> 128 us
  other arithmetic: 136 us -> 8.81 us
  starting transfers between devices: 148 us -> 23.7 us
  local copies, waits for them, and re-layouts: 143 us -> 19.3 us
    pallas_call x0 -> x1, Pallas kernels: none -> 128 us  [chebyshev_solve(): pl.pallas_call(functools.partial(solve_kernel, ngx, ngy), out_shape=(jax....]
    add x32 -> x0, other arithmetic: 125 us -> none  [the longest x16 89 us: sweep(): rho_next * rho_now * direction + 2.0 * rho_next / delta * residual]
    ppermute x91 -> x11, starting transfers between devices: 148 us -> 23.7 us  [ring(): lax.ppermute(x, axis, [(i, (i + step) % count) for i in range(count)])]
    slice x51 -> x3, local copies, waits for them, and re-layouts: 77.1 us -> 4.68 us  [neighbours(): lax.slice_in_dim(cells, 0, n - 1, axis=dim)]
    slice x17 -> x1, local copies, waits for them, and re-layouts: 13.7 us -> 0.67 us  [halos(): lax.slice_in_dim(cells, cells.shape[dx] - 1, cells.shape[dx], axis=dx)]
    while x18 -> x0, local copies, waits for them, and re-layouts: 10.3 us -> none
    slice x17 -> x1, local copies, waits for them, and re-layouts: 11 us -> 0.62 us  [halos(): lax.slice_in_dim(cells, cells.shape[dy] - 1, cells.shape[dy], axis=dy)]
    unnamed x26 -> x17, local copies, waits for them, and re-layouts: 10 us -> 3 us
  transfers between devices with their start and end apart: 91 -> 11, of which waited for: 3 -> 3; matrix products, arithmetic and copies ran while one was open for 37% -> 5% of each run, Pallas kernels for 0% -> 0%
where the time goes in v2:
time: 197 us; the launch traced here: 194 us
  Pallas kernels  128 us (65%)
  starting transfers between devices  23.7 us (12%)
  local copies, waits for them, and re-layouts  19.3 us (10%)
  waiting for transfers between devices  11.1 us (6%)
  other arithmetic  8.81 us (4%)
  between operations  2.92 us (1%)
    pallas_call x1, Pallas kernels, chebyshev_solve(): pl.pallas_call(functools.partial(solve_kernel, ngx, ngy), out_shape=(jax....  128 us
    ppermute x11, starting transfers between devices, ring(): lax.ppermute(x, axis, [(i, (i + step) % count) for i in range(count)])  23.7 us
    ppermute x11, waiting for transfers between devices, ring(): lax.ppermute(x, axis, [(i, (i + step) % count) for i in range(count)])  11.1 us
    slice x3, local copies, waits for them, and re-layouts, neighbours(): lax.slice_in_dim(cells, 0, n - 1, axis=dim)  4.68 us
  transfers between devices with their start and end apart: 11, of which 3 were waited for; matrix products, arithmetic and copies ran while one was open for 5% of the time, Pallas kernels for 0%

profile of v2, /device:TPU:2, one launch (start us, length us, event | category | flops | bytes accessed | tf_op | source)
XLA Modules:
  0.0 193.8 jit_solution(17512361684268028157)
XLA Ops:
  0.6 0.9 fusion.37
  1.6 1.7 collective-permute-start
  3.2 6.8 %collective-permute-start.1 = (f32[1,128,128]{2,1,0:T(8,128)S(1)}, f32[1,128,128]{2,1,0:T(8,128)S(1)}, u32[]{:S(2)}, u32[]{:S(2)}) collective-permute-start(f32[1,128,128]{2,1,0:T(8,128)S(1)} %get-tuple-element.42), channel_id=1, source_target_pairs={{0,248},{8,0},{16,8},{24,16},{32,24},{40,32},{48,40},{56,48},{64,5... | collective-permute-start | bytes 196616 | tf_op jit(solution)/shard_map/ppermute | solution.py:19
  10.1 0.8 fusion.35
  10.8 0.1 collective-permute-start.2
  10.9 1.7 collective-permute-start.3
  12.6 1.4 fusion.33
  14.1 0.2 copy.16
  14.2 0.2 copy.17
  14.4 1.0 copy.11
  15.5 2.1 %collective-permute-start.4 = (f32[8,128,2]{2,1,0:T(8,128)}, f32[8,128,2]{2,1,0:T(8,128)S(1)}, u32[]{:S(2)}, u32[]{:S(2)}) collective-permute-start(f32[8,128,2]{2,1,0:T(8,128)} %copy.11), channel_id=1, source_target_pairs={{0,1},{1,0},{2,3},{3,2},{4,5},{5,4},{6,7},{7,6},{8,9},{9,8},{10,11... | collective-permute-start | bytes 24584 | tf_op jit(solution)/shard_map/ppermute | solution.py:19
  19.0 1.0 fusion.36
  20.0 0.1 fusion.34
  20.1 0.2 fusion.31
  21.0 0.1 stack.157
  21.1 0.1 stack.175
  21.2 0.5 pad_maximum_fusion.3.ab_ref
  21.7 8.2 %collective-permute-done.4 = f32[8,128,2]{2,1,0:T(8,128)S(1)} collective-permute-done((f32[8,128,2]{2,1,0:T(8,128)}, f32[8,128,2]{2,1,0:T(8,128)S(1)}, u32[]{:S(2)}, u32[]{:S(2)}) %collective-permute-start.4) | collective-permute-done | bytes 8224 | tf_op jit(solution)/shard_map/ppermute | solution.py:19
  29.9 2.4 %collective-permute-start.5 = (bf16[8,128,128]{2,1,0:T(8,128)(2,1)}, bf16[8,128,128]{2,1,0:T(8,128)(2,1)S(1)}, u32[]{:S(2)}, u32[]{:S(2)}) collective-permute-start(bf16[8,128,128]{2,1,0:T(8,128)(2,1)} %param.6), channel_id=1, source_target_pairs={{0,1},{1,0},{2,3},{3,2},{4,5},{5,4},{6,7},{7,6},{8,9},{9,8},{10,11... | collective-permute-start | bytes 786440 | tf_op jit(solution)/shard_map/ppermute | solution.py:19
  32.4 0.2 fusion.32
  32.6 1.1 fusion.9
  33.7 0.1 fusion.15
  33.9 0.1 fusion.18
  33.9 0.2 fusion.21
  34.1 0.2 fusion.24.w_ref
  34.4 1.6 copy-done.2
  36.0 2.0 %collective-permute-done.5 = bf16[8,128,128]{2,1,0:T(8,128)(2,1)S(1)} collective-permute-done((bf16[8,128,128]{2,1,0:T(8,128)(2,1)}, bf16[8,128,128]{2,1,0:T(8,128)(2,1)S(1)}, u32[]{:S(2)}, u32[]{:S(2)}) %collective-permute-start.5) | collective-permute-done | bytes 262176 | tf_op jit(solution)/shard_map/ppermute | solution.py:19
  38.0 0.2 multiply_bitcast_fusion
  38.2 1.5 broadcast_divide_fusion
  39.8 128.1 %shard_map.84 = (f32[2,8,128,128]{3,2,1,0:T(8,128)}, f32[2,8,128,128]{3,2,1,0:T(8,128)}) custom-call(f32[2,16]{1,0:T(2,128)} %pad_maximum_fusion.3.ab_ref, f32[6,8,128,128]{3,2,1,0:T(8,128)} %copy-done.2, f32[2,8,128,128]{3,2,1,0:T(8,128)} %get-tuple-element.29.rhs_ref, f32[2,8,128,128]{3,2,1,0:T(8,128)} %get-tuple-element.28.d0_ref), custom_call_target="tpu_custom_call" | custom-call | tf_op jit(solution)/shard_map/pallas_call | solution.py:161
  167.8 2.0 %fusion.30 = (f32[2,8,128,1]{3,2,1,0:T(8,128)S(1)}, f32[2,8,128,1]{3,2,1,0:T(8,128)S(1)}) fusion(f32[2,8,128,128]{3,2,1,0:T(8,128)} %get-tuple-element.6), kind=kLoop, calls=%fused_computation.56 | loop fusion | bytes 32768 | tf_op jit(solution)/shard_map/slice | solution.py:30
  169.8 1.5 fusion.28
  171.3 1.7 fusion.29
  173.0 1.5 fusion.26
  174.5 0.7 fusion.25
  175.2 1.0 slice_bitcast_fusion
  176.2 0.3 copy.12
  176.6 0.3 copy.13
  176.9 1.8 collective-permute-start.10
  178.7 0.6 fusion.27
  179.3 5.3 %collective-permute-start.7 = (f32[2,1,128,128]{3,2,1,0:T(8,128)S(1)}, f32[2,1,128,128]{3,2,1,0:T(8,128)S(1)}, u32[]{:S(2)}, u32[]{:S(2)}) collective-permute-start(f32[2,1,128,128]{3,2,1,0:T(8,128)S(1)} %get-tuple-element.17), channel_id=1, source_target_pairs={{0,248},{8,0},{16,8},{24,16},{32,24},{40,32},{48,40},{56,48},{64,5... | collective-permute-start | bytes 393224 | tf_op jit(solution)/shard_map/ppermute | solution.py:19
  184.7 1.7 collective-permute-start.9
  186.4 0.4 copy.14
  186.8 0.4 copy.15
  187.2 0.8 collective-permute-done.8
  188.0 3.5 %maximum_subtract_fusion = (f32[2,8,128,128]{3,2,1,0:T(8,128)S(1)}, f32[2,8,128,128]{3,2,1,0:T(8,128)S(1)}, f32[2,8,128,128]{3,2,1,0:T(8,128)S(1)}, f32[2,8,128,...) fusion(f32[2,8,128,128]{3,2,1,0:T(8,128)S(1)} %copy-done, ...), kind=kLoop, calls=%fused_computation.1 | loop fusion | flops 3145728 | bytes 13631488 | tf_op jit(solution)/shard_map/sub | solution.py:205
  191.5 1.3 fusion.2
  192.9 1.0 copy.25
  (27 shorter events, 0.2 us)
Async XLA Ops:
  0.6 18.4 %copy-start.1 = (f32[8,128,128]{2,1,0:T(8,128)S(1)}, f32[8,128,128]{2,1,0:T(8,128)}, u32[]{:S(2)}) copy-start(f32[8,128,128]{2,1,0:T(8,128)} %param.5) | copy-start | bytes 1572868
  1.6 31.0 %collective-permute-start = (f32[1,128,128]{2,1,0:T(8,128)S(1)}, f32[1,128,128]{2,1,0:T(8,128)S(1)}, u32[]{:S(2)}, u32[]{:S(2)}) collective-permute-start(f32[1,128,128]{2,1,0:T(8,128)S(1)} %get-tuple-element.43), channel_id=1, source_target_pairs={{0,8},{8,16},{16,24},{24,32},{32,40},{40,48},{48,56},{56,64},{64,7... | collective-permute-start | bytes 196616 | tf_op jit(solution)/shard_map/ppermute | solution.py:19
  3.2 30.4 %collective-permute-start.1 = (f32[1,128,128]{2,1,0:T(8,128)S(1)}, f32[1,128,128]{2,1,0:T(8,128)S(1)}, u32[]{:S(2)}, u32[]{:S(2)}) collective-permute-start(f32[1,128,128]{2,1,0:T(8,128)S(1)} %get-tuple-element.42), channel_id=1, source_target_pairs={{0,248},{8,0},{16,8},{24,16},{32,24},{40,32},{48,40},{56,48},{64,5... | collective-permute-start | bytes 196616 | tf_op jit(solution)/shard_map/ppermute | solution.py:19
  10.8 22.9 %collective-permute-start.2 = (f32[8,1,128]{2,1,0:T(1,128)S(1)}, f32[8,1,128]{2,1,0:T(1,128)S(1)}, u32[]{:S(2)}, u32[]{:S(2)}) collective-permute-start(f32[8,1,128]{2,1,0:T(1,128)S(1)} %get-tuple-element.39), channel_id=1, source_target_pairs={{0,2},{2,4},{4,6},{6,0},{1,3},{3,5},{5,7},{7,1},{8,10},{10,12},{12... | collective-permute-start | bytes 12296 | tf_op jit(solution)/shard_map/ppermute | solution.py:19
  10.9 22.9 %collective-permute-start.3 = (f32[8,1,128]{2,1,0:T(1,128)S(1)}, f32[8,1,128]{2,1,0:T(1,128)S(1)}, u32[]{:S(2)}, u32[]{:S(2)}) collective-permute-start(f32[8,1,128]{2,1,0:T(1,128)S(1)} %get-tuple-element.38), channel_id=1, source_target_pairs={{0,6},{2,0},{4,2},{6,4},{1,7},{3,1},{5,3},{7,5},{8,14},{10,8},{12,... | collective-permute-start | bytes 12296 | tf_op jit(solution)/shard_map/ppermute | solution.py:19
  15.5 14.5 %collective-permute-start.4 = (f32[8,128,2]{2,1,0:T(8,128)}, f32[8,128,2]{2,1,0:T(8,128)S(1)}, u32[]{:S(2)}, u32[]{:S(2)}) collective-permute-start(f32[8,128,2]{2,1,0:T(8,128)} %copy.11), channel_id=1, source_target_pairs={{0,1},{1,0},{2,3},{3,2},{4,5},{5,4},{6,7},{7,6},{8,9},{9,8},{10,11... | collective-permute-start | bytes 24584 | tf_op jit(solution)/shard_map/ppermute | solution.py:19
  21.2 12.5 %copy-start.3 = (f32[7,128,128]{2,1,0:T(8,128)S(1)}, f32[7,128,128]{2,1,0:T(8,128)}, u32[]{:S(2)}) copy-start(f32[7,128,128]{2,1,0:T(8,128)} %get-tuple-element.40) | copy-start | bytes 1376260
  29.9 8.1 %collective-permute-start.5 = (bf16[8,128,128]{2,1,0:T(8,128)(2,1)}, bf16[8,128,128]{2,1,0:T(8,128)(2,1)S(1)}, u32[]{:S(2)}, u32[]{:S(2)}) collective-permute-start(bf16[8,128,128]{2,1,0:T(8,128)(2,1)} %param.6), channel_id=1, source_target_pairs={{0,1},{1,0},{2,3},{3,2},{4,5},{5,4},{6,7},{7,6},{8,9},{9,8},{10,11... | collective-permute-start | bytes 786440 | tf_op jit(solution)/shard_map/ppermute | solution.py:19
  33.8 4.2 %copy-start.6 = (f32[8,128]{1,0:T(8,128)S(1)}, f32[8,128]{1,0:T(8,128)}, u32[]{:S(2)}) copy-start(f32[8,128]{1,0:T(8,128)} %param.7) | copy-start | bytes 12292
  33.8 4.4 %copy-start.5 = (f32[8,128,128]{2,1,0:T(8,128)S(1)}, f32[8,128,128]{2,1,0:T(8,128)}, u32[]{:S(2)}) copy-start(f32[8,128,128]{2,1,0:T(8,128)} %param.8) | copy-start | bytes 1572868
  34.4 1.6 copy-start.2
  167.8 2.0 %copy-start = (f32[2,8,128,128]{3,2,1,0:T(8,128)S(1)}, f32[2,8,128,128]{3,2,1,0:T(8,128)}, u32[]{:S(2)}) copy-start(f32[2,8,128,128]{3,2,1,0:T(8,128)} %get-tuple-element.6) | copy-start | bytes 3145732
  176.9 9.5 %collective-permute-start.10 = (f32[2,8,128,2]{2,1,3,0:T(8,128)S(1)}, f32[2,8,128,2]{2,1,3,0:T(8,128)S(1)}, u32[]{:S(2)}, u32[]{:S(2)}) collective-permute-start(f32[2,8,128,2]{2,1,3,0:T(8,128)S(1)} %pad_maximum_fusion.1), channel_id=1, source_target_pairs={{0,1},{1,0},{2,3},{3,2},{4,5},{5,4},{6,7},{7,6},{8,9},{9,8},{10,11... | collective-permute-start | bytes 49160 | tf_op jit(solution)/shard_map/ppermute | solution.py:19
  179.3 8.7 %collective-permute-start.6 = (f32[2,1,128,128]{3,2,1,0:T(8,128)}, f32[2,1,128,128]{3,2,1,0:T(8,128)S(1)}, u32[]{:S(2)}, u32[]{:S(2)}) collective-permute-start(f32[2,1,128,128]{3,2,1,0:T(8,128)} %get-tuple-element.16), channel_id=1, source_target_pairs={{0,8},{8,16},{16,24},{24,32},{32,40},{40,48},{48,56},{56,64},{64,7... | collective-permute-start | bytes 393224 | tf_op jit(solution)/shard_map/ppermute | solution.py:19
  179.3 8.7 %collective-permute-start.7 = (f32[2,1,128,128]{3,2,1,0:T(8,128)S(1)}, f32[2,1,128,128]{3,2,1,0:T(8,128)S(1)}, u32[]{:S(2)}, u32[]{:S(2)}) collective-permute-start(f32[2,1,128,128]{3,2,1,0:T(8,128)S(1)} %get-tuple-element.17), channel_id=1, source_target_pairs={{0,248},{8,0},{16,8},{24,16},{32,24},{40,32},{48,40},{56,48},{64,5... | collective-permute-start | bytes 393224 | tf_op jit(solution)/shard_map/ppermute | solution.py:19
  184.7 3.3 %collective-permute-start.8 = (f32[2,8,1,128]{3,2,1,0:T(1,128)}, f32[2,8,1,128]{3,2,1,0:T(1,128)S(1)}, u32[]{:S(2)}, u32[]{:S(2)}) collective-permute-start(f32[2,8,1,128]{3,2,1,0:T(1,128)} %get-tuple-element.20), channel_id=1, source_target_pairs={{0,2},{2,4},{4,6},{6,0},{1,3},{3,5},{5,7},{7,1},{8,10},{10,12},{12... | collective-permute-start | bytes 24584 | tf_op jit(solution)/shard_map/ppermute | solution.py:19
  184.7 3.3 %collective-permute-start.9 = (f32[2,8,1,128]{3,2,1,0:T(1,128)}, f32[2,8,1,128]{3,2,1,0:T(1,128)}, u32[]{:S(2)}, u32[]{:S(2)}) collective-permute-start(f32[2,8,1,128]{3,2,1,0:T(1,128)} %get-tuple-element.21), channel_id=1, source_target_pairs={{0,6},{2,0},{4,2},{6,4},{1,7},{3,1},{5,3},{7,5},{8,14},{10,8},{12,... | collective-permute-start | bytes 24584 | tf_op jit(solution)/shard_map/ppermute | solution.py:19
  191.5 1.3 copy-start.4

commit v3 on v2

--- a/solution.py
+++ b/solution.py
@@ -47,9 +47,10 @@
     return out
 
 
-def solve_kernel(ngx, ngy, ab_ref, w_ref, rhs_ref, d0_ref, x_ref, r_ref,
+def solve_kernel(ngx, ngy, ab_ref, w_ref, rhs_ref, d0_ref, g_ref, adj_ref, state_ref, r_ref,
                  dbuf, sx, sy, sz, rx, ry, rz, send_sem, recv_sem):
     S, X, Y, Z = rhs_ref.shape
+    xo = (state_ref, adj_ref)
     gx = lax.axis_index("gx")
     gy = lax.axis_index("gy")
     pa = lax.axis_index("pa")
@@ -95,61 +96,74 @@
     row = lax.broadcasted_iota(jnp.int32, (Y, Z), 0)
     lane = lax.broadcasted_iota(jnp.int32, (Y, Z), 1)
 
+    def near(plane, slot, s, xi):
+        c = plane(xi)
+        xm = plane(xi - 1) if xi > 0 else rx[slot, 0, s]
+        xp = plane(xi + 1) if xi < X - 1 else rx[slot, 1, s]
+        ym = jnp.where(row == 0, jnp.broadcast_to(ry[slot, 0, s, pl.ds(xi, 1), :], (Y, Z)), pltpu.roll(c, 1, 0))
+        yp = jnp.where(row == Y - 1, jnp.broadcast_to(ry[slot, 1, s, pl.ds(xi, 1), :], (Y, Z)),
+                       pltpu.roll(c, Y - 1, 0))
+        zpair = jnp.where(
+            row < Y // 2,
+            jnp.broadcast_to(rz[slot, 1, s, pl.ds(xi, 1), :], (Y, Z)),
+            jnp.broadcast_to(rz[slot, 0, s, pl.ds(xi, 1), :], (Y, Z)),
+        ).T
+        zm = jnp.where(lane == 0, zpair, pltpu.roll(c, 1, 1))
+        zp = jnp.where(lane == Z - 1, zpair, pltpu.roll(c, Z - 1, 1))
+        return c, (xm, xp, ym, yp, zm, zp)
+
     for s in range(S):
         for xi in range(X):
             plane = d0_ref[s, xi]
             dbuf[0, s, xi] = plane
-            x_ref[s, xi] = jnp.zeros((Y, Z), jnp.float32)
+            xo[s][xi] = jnp.zeros((Y, Z), jnp.float32)
             r_ref[s, xi] = rhs_ref[s, xi]
             put_faces(s, xi, plane)
     for c in copies(0):
         c.start()
 
-    def step(k, carry):
-        slot = lax.rem(k, 2)
+    def step(k, slot, final):
         nslot = 1 - slot
         for c in copies(slot):
             c.wait()
         a = ab_ref[0, k]
         b = ab_ref[1, k]
-        last = k == CHEB - 1
         for s in range(S):
             for xi in range(X):
-                c = dbuf[slot, s, xi]
-                xm = dbuf[slot, s, xi - 1] if xi > 0 else rx[slot, 0, s]
-                xp = dbuf[slot, s, xi + 1] if xi < X - 1 else rx[slot, 1, s]
-                ym = jnp.where(row == 0, jnp.broadcast_to(ry[slot, 0, s, pl.ds(xi, 1), :], (Y, Z)),
-                               pltpu.roll(c, 1, 0))
-                yp = jnp.where(row == Y - 1, jnp.broadcast_to(ry[slot, 1, s, pl.ds(xi, 1), :], (Y, Z)),
-                               pltpu.roll(c, Y - 1, 0))
-                zpair = jnp.where(
-                    row < Y // 2,
-                    jnp.broadcast_to(rz[slot, 1, s, pl.ds(xi, 1), :], (Y, Z)),
-                    jnp.broadcast_to(rz[slot, 0, s, pl.ds(xi, 1), :], (Y, Z)),
-                ).T
-                zm = jnp.where(lane == 0, zpair, pltpu.roll(c, 1, 1))
-                zp = jnp.where(lane == Z - 1, zpair, pltpu.roll(c, Z - 1, 1))
-                summed = w_ref[0, xi] * (c - xm)
-                summed = summed + w_ref[1, xi] * (c - xp)
-                summed = summed + w_ref[2, xi] * (c - ym)
-                summed = summed + w_ref[3, xi] * (c - yp)
-                summed = summed + w_ref[4, xi] * (c - zm)
-                summed = summed + w_ref[5, xi] * (c - zp)
-                x_ref[s, xi] = x_ref[s, xi] + c
+                c, nb = near(lambda i: dbuf[slot, s, i], slot, s, xi)
+                summed = w_ref[0, xi] * (c - nb[0])
+                for j in range(1, 6):
+                    summed = summed + w_ref[j, xi] * (c - nb[j])
+                xn = xo[s][xi] + c
+                xo[s][xi] = xn
                 res = r_ref[s, xi] - (c + summed)
                 r_ref[s, xi] = res
-                nd = a * c + b * res
-                dbuf[nslot, s, xi] = nd
-                put_faces(s, xi, nd)
-
-        @pl.when(jnp.logical_not(last))
-        def _():
-            for c in copies(nslot):
-                c.start()
-
+                if final:
+                    put_faces(s, xi, xn)
+                else:
+                    nd = a * c + b * res
+                    dbuf[nslot, s, xi] = nd
+                    put_faces(s, xi, nd)
+        for c in copies(nslot):
+            c.start()
+
+    def loop_step(k, carry):
+        step(k, lax.rem(k, 2), False)
         return carry
 
-    lax.fori_loop(0, CHEB, step, 0)
+    lax.fori_loop(0, CHEB - 1, loop_step, 0)
+    step(CHEB - 1, (CHEB - 1) % 2, True)
+
+    gslot = CHEB % 2
+    for c in copies(gslot):
+        c.wait()
+    for xi in range(X):
+        c0, n0 = near(lambda i: xo[0][i], gslot, 0, xi)
+        c1, n1 = near(lambda i: xo[1][i], gslot, 1, xi)
+        summed = (c0 - n0[0]) * (c1 - n1[0])
+        for j in range(1, 6):
+            summed = summed + (c0 - n0[j]) * (c1 - n1[j])
+        g_ref[xi] = (-0.5 * time_step) * summed
 
 
 def chebyshev_solve(weights, rhs, d0, ab):
@@ -158,11 +172,12 @@
     ngy = lax.axis_size("gy")
     f32 = jnp.float32
     vmem = pl.BlockSpec(memory_space=pltpu.VMEM)
+    field = jax.ShapeDtypeStruct((X, Y, Z), f32)
     return pl.pallas_call(
         functools.partial(solve_kernel, ngx, ngy),
-        out_shape=(jax.ShapeDtypeStruct(rhs.shape, f32), jax.ShapeDtypeStruct(rhs.shape, f32)),
+        out_shape=(field, field, field, jax.ShapeDtypeStruct(rhs.shape, f32)),
         in_specs=[pl.BlockSpec(memory_space=pltpu.SMEM), vmem, vmem, vmem],
-        out_specs=(vmem, vmem),
+        out_specs=(vmem, vmem, vmem, vmem),
         scratch_shapes=[
             pltpu.VMEM((2, S, X, Y, Z), f32),
             pltpu.VMEM((2, S, Y, Z), f32),
@@ -198,14 +213,7 @@
         rho = rho_next
     ab = jnp.stack([jnp.stack([c[0] for c in coefs]), jnp.stack([c[1] for c in coefs])])
 
-    solved, residuals = chebyshev_solve(weights, rhs, rhs / theta, ab)
-    near = neighbours(solved, halos(solved))
-    summed = jnp.zeros_like(solved[0])
-    for n in near:
-        differ = solved - n
-        summed = summed + differ[0] * differ[1]
-    grad_conductivity = -0.5 * time_step * summed
-    return (grad_conductivity, solved[1], solved[0], residuals)
+    return chebyshev_solve(weights, rhs, rhs / theta, ab)
 
 
 def solution(mesh):

time: 197 us -> 182 us (0.924)
  starting transfers between devices: 23.7 us -> 14.8 us
  Pallas kernels: 128 us -> 134 us
  other arithmetic: 8.81 us -> 4.04 us
  local copies, waits for them, and re-layouts: 19.3 us -> 14.6 us
    ppermute x11 -> x6, starting transfers between devices: 23.7 us -> 14.8 us  [ring(): lax.ppermute(x, axis, [(i, (i + step) % count) for i in range(count)])]
    slice x8 -> x0, local copies, waits for them, and re-layouts: 6.68 us -> none  [the longest x3 4.68 us: neighbours(): lax.slice_in_dim(cells, 0, n - 1, axis=dim)]
    unnamed x17 -> x18, local copies, waits for them, and re-layouts: 3 us -> 8.73 us
    pallas_call x1, Pallas kernels: 128 us -> 134 us  [chebyshev_solve(): pl.pallas_call(functools.partial(solve_kernel, ngx, ngy), out_shape=(fiel...]
    sub x1 -> x0, other arithmetic: 3.54 us -> none  [body(): differ = solved - n]
    slice x3 -> x1, local copies, waits for them, and re-layouts: 3.72 us -> 1.4 us  [halos(): lax.slice_in_dim(cells, 0, 1, axis=dz)]
    ppermute x11 -> x6, waiting for transfers between devices: 11.1 us -> 10.2 us  [ring(): lax.ppermute(x, axis, [(i, (i + step) % count) for i in range(count)])]
  transfers between devices with their start and end apart: 11 -> 6, of which waited for: 3 -> 2; matrix products, arithmetic and copies ran while one was open for 5% -> 4% of each run, Pallas kernels for 0% -> 0%
where the time goes in v3:
time: 182 us; the launch traced here: 180 us
  Pallas kernels  134 us (74%)
  starting transfers between devices  14.8 us (8%)
  local copies, waits for them, and re-layouts  14.6 us (8%)
  waiting for transfers between devices  10.2 us (6%)
  other arithmetic  4.04 us (2%)
  between operations  2.86 us (2%)
    pallas_call x1, Pallas kernels, chebyshev_solve(): pl.pallas_call(functools.partial(solve_kernel, ngx, ngy), out_shape=(fiel...  134 us
    ppermute x6, starting transfers between devices, ring(): lax.ppermute(x, axis, [(i, (i + step) % count) for i in range(count)])  14.8 us
    ppermute x6, waiting for transfers between devices, ring(): lax.ppermute(x, axis, [(i, (i + step) % count) for i in range(count)])  10.2 us
    unnamed x18, local copies, waits for them, and re-layouts  8.73 us
  transfers between devices with their start and end apart: 6, of which 2 were waited for; matrix products, arithmetic and copies ran while one was open for 4% of the time, Pallas kernels for 0%

profile of v3, /device:TPU:2, one launch (start us, length us, event | category | flops | bytes accessed | tf_op | source)
XLA Modules:
  0.0 180.0 jit_solution(1054021754337085254)
XLA Ops:
  0.6 0.0 copy-start
  0.6 0.9 fusion.24
  1.6 1.7 collective-permute-start
  3.2 6.8 %collective-permute-start.1 = (f32[1,128,128]{2,1,0:T(8,128)S(1)}, f32[1,128,128]{2,1,0:T(8,128)S(1)}, u32[]{:S(2)}, u32[]{:S(2)}) collective-permute-start(f32[1,128,128]{2,1,0:T(8,128)S(1)} %get-tuple-element.18), channel_id=1, source_target_pairs={{0,248},{8,0},{16,8},{24,16},{32,24},{40,32},{48,40},{56,48},{64,5... | collective-permute-start | bytes 196616 | tf_op jit(solution)/shard_map/ppermute | solution.py:19
  10.1 0.8 fusion.22
  10.8 0.1 collective-permute-start.2
  10.9 1.7 collective-permute-start.3
  12.6 1.4 fusion.20
  14.1 0.2 copy.12
  14.2 0.2 copy.13
  14.4 1.0 copy.11
  15.5 2.1 %collective-permute-start.4 = (f32[8,128,2]{2,1,0:T(8,128)}, f32[8,128,2]{2,1,0:T(8,128)S(1)}, u32[]{:S(2)}, u32[]{:S(2)}) collective-permute-start(f32[8,128,2]{2,1,0:T(8,128)} %copy.11), channel_id=1, source_target_pairs={{0,1},{1,0},{2,3},{3,2},{4,5},{5,4},{6,7},{7,6},{8,9},{9,8},{10,11... | collective-permute-start | bytes 24584 | tf_op jit(solution)/shard_map/ppermute | solution.py:19
  19.0 0.0 copy-done
  19.0 1.0 fusion.23
  20.0 0.1 fusion.21
  20.1 0.2 fusion.18
  21.0 0.1 stack.157
  21.1 0.1 stack.175
  21.2 0.0 copy-start.2
  21.2 0.6 pad_maximum_fusion.2.ab_ref
  21.8 8.2 %collective-permute-done.4 = f32[8,128,2]{2,1,0:T(8,128)S(1)} collective-permute-done((f32[8,128,2]{2,1,0:T(8,128)}, f32[8,128,2]{2,1,0:T(8,128)S(1)}, u32[]{:S(2)}, u32[]{:S(2)}) %collective-permute-start.4) | collective-permute-done | bytes 8224 | tf_op jit(solution)/shard_map/ppermute | solution.py:19
  29.9 2.4 %collective-permute-start.5 = (bf16[8,128,128]{2,1,0:T(8,128)(2,1)}, bf16[8,128,128]{2,1,0:T(8,128)(2,1)S(1)}, u32[]{:S(2)}, u32[]{:S(2)}) collective-permute-start(bf16[8,128,128]{2,1,0:T(8,128)(2,1)} %param.6), channel_id=1, source_target_pairs={{0,1},{1,0},{2,3},{3,2},{4,5},{5,4},{6,7},{7,6},{8,9},{9,8},{10,11... | collective-permute-start | bytes 786440 | tf_op jit(solution)/shard_map/ppermute | solution.py:19
  32.4 0.2 fusion.19
  32.6 0.0 collective-permute-done
  32.6 1.1 fusion.2
  33.6 0.0 collective-permute-done.1
  33.7 0.0 copy-done.2
  33.7 0.1 fusion.5
  33.7 0.0 collective-permute-done.2
  33.7 0.1 fusion.8
  33.8 0.0 copy-start.5
  33.8 0.0 collective-permute-done.3
  33.9 0.0 copy-start.4
  33.9 0.1 fusion.11
  33.9 0.2 fusion.14
  34.1 0.2 fusion.17.w_ref
  34.4 0.0 copy-start.1
  34.4 1.6 copy-done.1
  36.0 2.0 %collective-permute-done.5 = bf16[8,128,128]{2,1,0:T(8,128)(2,1)S(1)} collective-permute-done((bf16[8,128,128]{2,1,0:T(8,128)(2,1)}, bf16[8,128,128]{2,1,0:T(8,128)(2,1)S(1)}, u32[]{:S(2)}, u32[]{:S(2)}) %collective-permute-start.5) | collective-permute-done | bytes 262176 | tf_op jit(solution)/shard_map/ppermute | solution.py:19
  38.0 0.0 copy-done.5
  38.0 0.2 multiply_bitcast_fusion
  38.2 0.0 copy-done.4
  38.2 1.5 broadcast_divide_fusion
  39.8 133.5 %shard_map.84 = (f32[8,128,128]{2,1,0:T(8,128)}, f32[8,128,128]{2,1,0:T(8,128)}, f32[8,128,128]{2,1,0:T(8,128)}, f32[2,8,128,128]{3,2,1,0:T(8,128)}) custom-call(f32[2,16]{1,0:T(2,128)} %pad_maximum_fusion.2.ab_ref, f32[6,8,128,128]{3,2,1,0:T(8,128)} %copy-done.1, f32[2,8,128,128]{3,2,1,0:T(8,128)} %get-tuple-element.5.rhs_ref, ...), custom_call_target="tpu_custom_call" | custom-call | tf_op jit(solution)/shard_map/pallas_call | solution.py:176
  173.3 2.0 %copy.24 = f32[8,128,128]{2,1,0:T(8,128)} copy(f32[8,128,128]{2,1,0:T(8,128)} %get-tuple-element.24) | data formatting | bytes 1048576
  175.3 1.9 %copy.25 = f32[8,128,128]{2,1,0:T(8,128)} copy(f32[8,128,128]{2,1,0:T(8,128)} %get-tuple-element.25) | data formatting | bytes 1048576
  177.2 1.9 %copy.26 = f32[8,128,128]{2,1,0:T(8,128)} copy(f32[8,128,128]{2,1,0:T(8,128)} %get-tuple-element.26) | data formatting | bytes 1048576
  179.0 1.0 copy.27
  (3 shorter events, 0.0 us)
Async XLA Ops:
  0.6 18.4 %copy-start = (f32[8,128,128]{2,1,0:T(8,128)S(1)}, f32[8,128,128]{2,1,0:T(8,128)}, u32[]{:S(2)}) copy-start(f32[8,128,128]{2,1,0:T(8,128)} %param.5) | copy-start | bytes 1572868
  1.6 31.0 %collective-permute-start = (f32[1,128,128]{2,1,0:T(8,128)S(1)}, f32[1,128,128]{2,1,0:T(8,128)S(1)}, u32[]{:S(2)}, u32[]{:S(2)}) collective-permute-start(f32[1,128,128]{2,1,0:T(8,128)S(1)} %get-tuple-element.19), channel_id=1, source_target_pairs={{0,8},{8,16},{16,24},{24,32},{32,40},{40,48},{48,56},{56,64},{64,7... | collective-permute-start | bytes 196616 | tf_op jit(solution)/shard_map/ppermute | solution.py:19
  3.2 30.4 %collective-permute-start.1 = (f32[1,128,128]{2,1,0:T(8,128)S(1)}, f32[1,128,128]{2,1,0:T(8,128)S(1)}, u32[]{:S(2)}, u32[]{:S(2)}) collective-permute-start(f32[1,128,128]{2,1,0:T(8,128)S(1)} %get-tuple-element.18), channel_id=1, source_target_pairs={{0,248},{8,0},{16,8},{24,16},{32,24},{40,32},{48,40},{56,48},{64,5... | collective-permute-start | bytes 196616 | tf_op jit(solution)/shard_map/ppermute | solution.py:19
  10.8 22.9 %collective-permute-start.2 = (f32[8,1,128]{2,1,0:T(1,128)S(1)}, f32[8,1,128]{2,1,0:T(1,128)S(1)}, u32[]{:S(2)}, u32[]{:S(2)}) collective-permute-start(f32[8,1,128]{2,1,0:T(1,128)S(1)} %get-tuple-element.15), channel_id=1, source_target_pairs={{0,2},{2,4},{4,6},{6,0},{1,3},{3,5},{5,7},{7,1},{8,10},{10,12},{12... | collective-permute-start | bytes 12296 | tf_op jit(solution)/shard_map/ppermute | solution.py:19
  10.9 22.9 %collective-permute-start.3 = (f32[8,1,128]{2,1,0:T(1,128)S(1)}, f32[8,1,128]{2,1,0:T(1,128)S(1)}, u32[]{:S(2)}, u32[]{:S(2)}) collective-permute-start(f32[8,1,128]{2,1,0:T(1,128)S(1)} %get-tuple-element.14), channel_id=1, source_target_pairs={{0,6},{2,0},{4,2},{6,4},{1,7},{3,1},{5,3},{7,5},{8,14},{10,8},{12,... | collective-permute-start | bytes 12296 | tf_op jit(solution)/shard_map/ppermute | solution.py:19
  15.5 14.5 %collective-permute-start.4 = (f32[8,128,2]{2,1,0:T(8,128)}, f32[8,128,2]{2,1,0:T(8,128)S(1)}, u32[]{:S(2)}, u32[]{:S(2)}) collective-permute-start(f32[8,128,2]{2,1,0:T(8,128)} %copy.11), channel_id=1, source_target_pairs={{0,1},{1,0},{2,3},{3,2},{4,5},{5,4},{6,7},{7,6},{8,9},{9,8},{10,11... | collective-permute-start | bytes 24584 | tf_op jit(solution)/shard_map/ppermute | solution.py:19
  21.2 12.5 %copy-start.2 = (f32[7,128,128]{2,1,0:T(8,128)S(1)}, f32[7,128,128]{2,1,0:T(8,128)}, u32[]{:S(2)}) copy-start(f32[7,128,128]{2,1,0:T(8,128)} %get-tuple-element.16) | copy-start | bytes 1376260
  29.9 8.1 %collective-permute-start.5 = (bf16[8,128,128]{2,1,0:T(8,128)(2,1)}, bf16[8,128,128]{2,1,0:T(8,128)(2,1)S(1)}, u32[]{:S(2)}, u32[]{:S(2)}) collective-permute-start(bf16[8,128,128]{2,1,0:T(8,128)(2,1)} %param.6), channel_id=1, source_target_pairs={{0,1},{1,0},{2,3},{3,2},{4,5},{5,4},{6,7},{7,6},{8,9},{9,8},{10,11... | collective-permute-start | bytes 786440 | tf_op jit(solution)/shard_map/ppermute | solution.py:19
  33.8 4.2 %copy-start.5 = (f32[8,128]{1,0:T(8,128)S(1)}, f32[8,128]{1,0:T(8,128)}, u32[]{:S(2)}) copy-start(f32[8,128]{1,0:T(8,128)} %param.7) | copy-start | bytes 12292
  33.9 4.4 %copy-start.4 = (f32[8,128,128]{2,1,0:T(8,128)S(1)}, f32[8,128,128]{2,1,0:T(8,128)}, u32[]{:S(2)}) copy-start(f32[8,128,128]{2,1,0:T(8,128)} %param.8) | copy-start | bytes 1572868
  34.4 1.7 copy-start.1
  173.3 5.7 %copy-start.3 = (f32[2,8,128,128]{3,2,1,0:T(8,128)S(1)}, f32[2,8,128,128]{3,2,1,0:T(8,128)}, u32[]{:S(2)}) copy-start(f32[2,8,128,128]{3,2,1,0:T(8,128)} %get-tuple-element.27) | copy-start | bytes 3145732

commit v4 on v3

--- a/solution.py
+++ b/solution.py
@@ -128,23 +128,27 @@
             c.wait()
         a = ab_ref[0, k]
         b = ab_ref[1, k]
-        for s in range(S):
-            for xi in range(X):
-                c, nb = near(lambda i: dbuf[slot, s, i], slot, s, xi)
-                summed = w_ref[0, xi] * (c - nb[0])
-                for j in range(1, 6):
-                    summed = summed + w_ref[j, xi] * (c - nb[j])
-                xn = xo[s][xi] + c
-                xo[s][xi] = xn
-                res = r_ref[s, xi] - (c + summed)
-                r_ref[s, xi] = res
-                if final:
-                    put_faces(s, xi, xn)
-                else:
-                    nd = a * c + b * res
-                    dbuf[nslot, s, xi] = nd
-                    put_faces(s, xi, nd)
-        for c in copies(nslot):
+        outgoing = copies(nslot)
+        order = [(s, xi) for xi in (0, X - 1) for s in range(S)] + [(s, xi) for xi in range(1, X - 1) for s in range(S)]
+        for n, (s, xi) in enumerate(order):
+            if n == 2 * S:
+                for c in outgoing[:2]:
+                    c.start()
+            c, nb = near(lambda i: dbuf[slot, s, i], slot, s, xi)
+            summed = w_ref[0, xi] * (c - nb[0])
+            for j in range(1, 6):
+                summed = summed + w_ref[j, xi] * (c - nb[j])
+            xn = xo[s][xi] + c
+            xo[s][xi] = xn
+            res = r_ref[s, xi] - (c + summed)
+            r_ref[s, xi] = res
+            if final:
+                put_faces(s, xi, xn)
+            else:
+                nd = a * c + b * res
+                dbuf[nslot, s, xi] = nd
+                put_faces(s, xi, nd)
+        for c in outgoing[2:]:
             c.start()
 
     def loop_step(k, carry):

time: 182 us -> 159 us (0.87)
  Pallas kernels: 134 us -> 112 us
    pallas_call x1, Pallas kernels: 134 us -> 112 us  [chebyshev_solve(): pl.pallas_call(functools.partial(solve_kernel, ngx, ngy), out_shape=(fiel...]
  transfers between devices with their start and end apart: 6 -> 6, of which waited for: 2 -> 2; matrix products, arithmetic and copies ran while one was open for 4% -> 5% of each run, Pallas kernels for 0% -> 0%
where the time goes in v4:
time: 159 us
  Pallas kernels  112 us (70%)
  starting transfers between devices  14.8 us (9%)
  local copies, waits for them, and re-layouts  14.6 us (9%)
  waiting for transfers between devices  10.2 us (6%)
  other arithmetic  4.04 us (3%)
  between operations  2.86 us (2%)
    pallas_call x1, Pallas kernels, chebyshev_solve(): pl.pallas_call(functools.partial(solve_kernel, ngx, ngy), out_shape=(fiel...  112 us
    ppermute x6, starting transfers between devices, ring(): lax.ppermute(x, axis, [(i, (i + step) % count) for i in range(count)])  14.8 us
    ppermute x6, waiting for transfers between devices, ring(): lax.ppermute(x, axis, [(i, (i + step) % count) for i in range(count)])  10.2 us
    unnamed x18, local copies, waits for them, and re-layouts  8.73 us
  transfers between devices with their start and end apart: 6, of which 2 were waited for; matrix products, arithmetic and copies ran while one was open for 5% of the time, Pallas kernels for 0%

profile of v4, /device:TPU:2, one launch (start us, length us, event | category | flops | bytes accessed | tf_op | source)
XLA Modules:
  0.0 158.5 jit_solution(4056492263878876042)
XLA Ops:
  0.6 0.0 copy-start
  0.6 0.9 fusion.24
  1.6 1.7 %collective-permute-start = (f32[1,128,128]{2,1,0:T(8,128)S(1)}, f32[1,128,128]{2,1,0:T(8,128)S(1)}, u32[]{:S(2)}, u32[]{:S(2)}) collective-permute-start(f32[1,128,128]{2,1,0:T(8,128)S(1)} %get-tuple-element.19), channel_id=1, source_target_pairs={{0,8},{8,16},{16,24},{24,32},{32,40},{40,48},{48,56},{56,64},{64,7... | collective-permute-start | bytes 196616 | tf_op jit(solution)/shard_map/ppermute | solution.py:19
  3.2 6.8 %collective-permute-start.1 = (f32[1,128,128]{2,1,0:T(8,128)S(1)}, f32[1,128,128]{2,1,0:T(8,128)S(1)}, u32[]{:S(2)}, u32[]{:S(2)}) collective-permute-start(f32[1,128,128]{2,1,0:T(8,128)S(1)} %get-tuple-element.18), channel_id=1, source_target_pairs={{0,248},{8,0},{16,8},{24,16},{32,24},{40,32},{48,40},{56,48},{64,5... | collective-permute-start | bytes 196616 | tf_op jit(solution)/shard_map/ppermute | solution.py:19
  10.1 0.8 fusion.22
  10.8 0.1 collective-permute-start.2
  10.9 1.7 %collective-permute-start.3 = (f32[8,1,128]{2,1,0:T(1,128)S(1)}, f32[8,1,128]{2,1,0:T(1,128)S(1)}, u32[]{:S(2)}, u32[]{:S(2)}) collective-permute-start(f32[8,1,128]{2,1,0:T(1,128)S(1)} %get-tuple-element.14), channel_id=1, source_target_pairs={{0,6},{2,0},{4,2},{6,4},{1,7},{3,1},{5,3},{7,5},{8,14},{10,8},{12,... | collective-permute-start | bytes 12296 | tf_op jit(solution)/shard_map/ppermute | solution.py:19
  12.6 1.4 fusion.20
  14.1 0.2 copy.12
  14.2 0.2 copy.13
  14.4 1.0 copy.11
  15.5 2.1 %collective-permute-start.4 = (f32[8,128,2]{2,1,0:T(8,128)}, f32[8,128,2]{2,1,0:T(8,128)S(1)}, u32[]{:S(2)}, u32[]{:S(2)}) collective-permute-start(f32[8,128,2]{2,1,0:T(8,128)} %copy.11), channel_id=1, source_target_pairs={{0,1},{1,0},{2,3},{3,2},{4,5},{5,4},{6,7},{7,6},{8,9},{9,8},{10,11... | collective-permute-start | bytes 24584 | tf_op jit(solution)/shard_map/ppermute | solution.py:19
  19.0 0.0 copy-done
  19.0 1.0 fusion.23
  20.0 0.1 fusion.21
  20.1 0.2 fusion.18
  21.0 0.1 stack.157
  21.1 0.1 stack.175
  21.2 0.0 copy-start.2
  21.2 0.6 pad_maximum_fusion.2.ab_ref
  21.8 8.2 %collective-permute-done.4 = f32[8,128,2]{2,1,0:T(8,128)S(1)} collective-permute-done((f32[8,128,2]{2,1,0:T(8,128)}, f32[8,128,2]{2,1,0:T(8,128)S(1)}, u32[]{:S(2)}, u32[]{:S(2)}) %collective-permute-start.4) | collective-permute-done | bytes 8224 | tf_op jit(solution)/shard_map/ppermute | solution.py:19
  29.9 2.4 %collective-permute-start.5 = (bf16[8,128,128]{2,1,0:T(8,128)(2,1)}, bf16[8,128,128]{2,1,0:T(8,128)(2,1)S(1)}, u32[]{:S(2)}, u32[]{:S(2)}) collective-permute-start(bf16[8,128,128]{2,1,0:T(8,128)(2,1)} %param.6), channel_id=1, source_target_pairs={{0,1},{1,0},{2,3},{3,2},{4,5},{5,4},{6,7},{7,6},{8,9},{9,8},{10,11... | collective-permute-start | bytes 786440 | tf_op jit(solution)/shard_map/ppermute | solution.py:19
  32.4 0.2 fusion.19
  32.6 0.0 collective-permute-done
  32.6 1.1 fusion.2
  33.6 0.0 collective-permute-done.1
  33.7 0.0 copy-done.2
  33.7 0.1 fusion.5
  33.7 0.0 collective-permute-done.2
  33.7 0.1 fusion.8
  33.8 0.0 copy-start.5
  33.8 0.0 collective-permute-done.3
  33.9 0.0 copy-start.4
  33.9 0.1 fusion.11
  33.9 0.2 fusion.14
  34.1 0.2 fusion.17.w_ref
  34.4 0.0 copy-start.1
  34.4 1.6 %copy-done.1 = f32[6,8,128,128]{3,2,1,0:T(8,128)} copy-done((f32[6,8,128,128]{3,2,1,0:T(8,128)}, f32[6,8,128,128]{3,2,1,0:T(8,128)S(1)}, u32[]{:S(2)}) %copy-start.1) | copy-done | bytes 3145752
  36.0 2.0 %collective-permute-done.5 = bf16[8,128,128]{2,1,0:T(8,128)(2,1)S(1)} collective-permute-done((bf16[8,128,128]{2,1,0:T(8,128)(2,1)}, bf16[8,128,128]{2,1,0:T(8,128)(2,1)S(1)}, u32[]{:S(2)}, u32[]{:S(2)}) %collective-permute-start.5) | collective-permute-done | bytes 262176 | tf_op jit(solution)/shard_map/ppermute | solution.py:19
  38.0 0.2 multiply_bitcast_fusion
  38.2 0.0 copy-done.4
  38.2 1.5 broadcast_divide_fusion
  39.8 112.1 %shard_map.84 = (f32[8,128,128]{2,1,0:T(8,128)}, f32[8,128,128]{2,1,0:T(8,128)}, f32[8,128,128]{2,1,0:T(8,128)}, f32[2,8,128,128]{3,2,1,0:T(8,128)}) custom-call(f32[2,16]{1,0:T(2,128)} %pad_maximum_fusion.2.ab_ref, f32[6,8,128,128]{3,2,1,0:T(8,128)} %copy-done.1, f32[2,8,128,128]{3,2,1,0:T(8,128)} %get-tuple-element.5.rhs_ref, ...), custom_call_target="tpu_custom_call" | custom-call | tf_op jit(solution)/shard_map/pallas_call | solution.py:180
  151.9 0.0 copy-start.3
  151.9 2.0 %copy.24 = f32[8,128,128]{2,1,0:T(8,128)} copy(f32[8,128,128]{2,1,0:T(8,128)} %get-tuple-element.24) | data formatting | bytes 1048576
  153.8 1.9 %copy.25 = f32[8,128,128]{2,1,0:T(8,128)} copy(f32[8,128,128]{2,1,0:T(8,128)} %get-tuple-element.25) | data formatting | bytes 1048576
  155.7 1.9 %copy.26 = f32[8,128,128]{2,1,0:T(8,128)} copy(f32[8,128,128]{2,1,0:T(8,128)} %get-tuple-element.26) | data formatting | bytes 1048576
  157.6 1.0 copy.27
  (3 shorter events, 0.0 us)
Async XLA Ops:
  0.6 18.4 %copy-start = (f32[8,128,128]{2,1,0:T(8,128)S(1)}, f32[8,128,128]{2,1,0:T(8,128)}, u32[]{:S(2)}) copy-start(f32[8,128,128]{2,1,0:T(8,128)} %param.5) | copy-start | bytes 1572868
  1.6 31.0 %collective-permute-start = (f32[1,128,128]{2,1,0:T(8,128)S(1)}, f32[1,128,128]{2,1,0:T(8,128)S(1)}, u32[]{:S(2)}, u32[]{:S(2)}) collective-permute-start(f32[1,128,128]{2,1,0:T(8,128)S(1)} %get-tuple-element.19), channel_id=1, source_target_pairs={{0,8},{8,16},{16,24},{24,32},{32,40},{40,48},{48,56},{56,64},{64,7... | collective-permute-start | bytes 196616 | tf_op jit(solution)/shard_map/ppermute | solution.py:19
  3.2 30.4 %collective-permute-start.1 = (f32[1,128,128]{2,1,0:T(8,128)S(1)}, f32[1,128,128]{2,1,0:T(8,128)S(1)}, u32[]{:S(2)}, u32[]{:S(2)}) collective-permute-start(f32[1,128,128]{2,1,0:T(8,128)S(1)} %get-tuple-element.18), channel_id=1, source_target_pairs={{0,248},{8,0},{16,8},{24,16},{32,24},{40,32},{48,40},{56,48},{64,5... | collective-permute-start | bytes 196616 | tf_op jit(solution)/shard_map/ppermute | solution.py:19
  10.8 22.9 %collective-permute-start.2 = (f32[8,1,128]{2,1,0:T(1,128)S(1)}, f32[8,1,128]{2,1,0:T(1,128)S(1)}, u32[]{:S(2)}, u32[]{:S(2)}) collective-permute-start(f32[8,1,128]{2,1,0:T(1,128)S(1)} %get-tuple-element.15), channel_id=1, source_target_pairs={{0,2},{2,4},{4,6},{6,0},{1,3},{3,5},{5,7},{7,1},{8,10},{10,12},{12... | collective-permute-start | bytes 12296 | tf_op jit(solution)/shard_map/ppermute | solution.py:19
  10.9 22.9 %collective-permute-start.3 = (f32[8,1,128]{2,1,0:T(1,128)S(1)}, f32[8,1,128]{2,1,0:T(1,128)S(1)}, u32[]{:S(2)}, u32[]{:S(2)}) collective-permute-start(f32[8,1,128]{2,1,0:T(1,128)S(1)} %get-tuple-element.14), channel_id=1, source_target_pairs={{0,6},{2,0},{4,2},{6,4},{1,7},{3,1},{5,3},{7,5},{8,14},{10,8},{12,... | collective-permute-start | bytes 12296 | tf_op jit(solution)/shard_map/ppermute | solution.py:19
  15.5 14.5 %collective-permute-start.4 = (f32[8,128,2]{2,1,0:T(8,128)}, f32[8,128,2]{2,1,0:T(8,128)S(1)}, u32[]{:S(2)}, u32[]{:S(2)}) collective-permute-start(f32[8,128,2]{2,1,0:T(8,128)} %copy.11), channel_id=1, source_target_pairs={{0,1},{1,0},{2,3},{3,2},{4,5},{5,4},{6,7},{7,6},{8,9},{9,8},{10,11... | collective-permute-start | bytes 24584 | tf_op jit(solution)/shard_map/ppermute | solution.py:19
  21.2 12.5 %copy-start.2 = (f32[7,128,128]{2,1,0:T(8,128)S(1)}, f32[7,128,128]{2,1,0:T(8,128)}, u32[]{:S(2)}) copy-start(f32[7,128,128]{2,1,0:T(8,128)} %get-tuple-element.16) | copy-start | bytes 1376260
  29.9 8.1 %collective-permute-start.5 = (bf16[8,128,128]{2,1,0:T(8,128)(2,1)}, bf16[8,128,128]{2,1,0:T(8,128)(2,1)S(1)}, u32[]{:S(2)}, u32[]{:S(2)}) collective-permute-start(bf16[8,128,128]{2,1,0:T(8,128)(2,1)} %param.6), channel_id=1, source_target_pairs={{0,1},{1,0},{2,3},{3,2},{4,5},{5,4},{6,7},{7,6},{8,9},{9,8},{10,11... | collective-permute-start | bytes 786440 | tf_op jit(solution)/shard_map/ppermute | solution.py:19
  33.8 4.2 %copy-start.5 = (f32[8,128]{1,0:T(8,128)S(1)}, f32[8,128]{1,0:T(8,128)}, u32[]{:S(2)}) copy-start(f32[8,128]{1,0:T(8,128)} %param.7) | copy-start | bytes 12292
  33.9 4.4 %copy-start.4 = (f32[8,128,128]{2,1,0:T(8,128)S(1)}, f32[8,128,128]{2,1,0:T(8,128)}, u32[]{:S(2)}) copy-start(f32[8,128,128]{2,1,0:T(8,128)} %param.8) | copy-start | bytes 1572868
  34.4 1.7 %copy-start.1 = (f32[6,8,128,128]{3,2,1,0:T(8,128)}, f32[6,8,128,128]{3,2,1,0:T(8,128)S(1)}, u32[]{:S(2)}) copy-start(f32[6,8,128,128]{3,2,1,0:T(8,128)S(1)} %fusion.17.w_ref) | copy-start | bytes 9437188
  151.9 5.7 %copy-start.3 = (f32[2,8,128,128]{3,2,1,0:T(8,128)S(1)}, f32[2,8,128,128]{3,2,1,0:T(8,128)}, u32[]{:S(2)}) copy-start(f32[2,8,128,128]{3,2,1,0:T(8,128)} %get-tuple-element.27) | copy-start | bytes 3145732

commit v5 on v3

--- a/solution.py
+++ b/solution.py
@@ -66,17 +66,17 @@
         pl.semaphore_signal(barrier, inc=1, device_id=dev, device_id_type=MESH)
     pl.semaphore_wait(barrier, len(peers))
 
-    def copies(slot):
+    def copies(slot, s):
         plan = (
-            (sx.at[0], rx.at[slot, 1], peers[0]),
-            (sx.at[1], rx.at[slot, 0], peers[1]),
-            (sy.at[0], ry.at[slot, 1], peers[2]),
-            (sy.at[1], ry.at[slot, 0], peers[3]),
-            (sz, rz.at[slot], peers[4]),
+            (sx.at[0, s], rx.at[slot, 1, s], peers[0]),
+            (sx.at[1, s], rx.at[slot, 0, s], peers[1]),
+            (sy.at[0, s], ry.at[slot, 1, s], peers[2]),
+            (sy.at[1, s], ry.at[slot, 0, s], peers[3]),
+            (sz.at[s], rz.at[slot, s], peers[4]),
         )
         return [
             pltpu.make_async_remote_copy(
-                src_ref=src, dst_ref=dst, send_sem=send_sem.at[i, slot], recv_sem=recv_sem.at[i, slot],
+                src_ref=src, dst_ref=dst, send_sem=send_sem.at[i, s, slot], recv_sem=recv_sem.at[i, s, slot],
                 device_id=dev, device_id_type=MESH,
             )
             for i, (src, dst, dev) in enumerate(plan)
@@ -90,8 +90,8 @@
         sy[0, s, pl.ds(xi, 1), :] = plane[0:1, :]
         sy[1, s, pl.ds(xi, 1), :] = plane[Y - 1:Y, :]
         t = plane.T
-        sz[0, s, pl.ds(xi, 1), :] = t[0:1, :]
-        sz[1, s, pl.ds(xi, 1), :] = t[Z - 1:Z, :]
+        sz[s, 0, pl.ds(xi, 1), :] = t[0:1, :]
+        sz[s, 1, pl.ds(xi, 1), :] = t[Z - 1:Z, :]
 
     row = lax.broadcasted_iota(jnp.int32, (Y, Z), 0)
     lane = lax.broadcasted_iota(jnp.int32, (Y, Z), 1)
@@ -105,8 +105,8 @@
                        pltpu.roll(c, Y - 1, 0))
         zpair = jnp.where(
             row < Y // 2,
-            jnp.broadcast_to(rz[slot, 1, s, pl.ds(xi, 1), :], (Y, Z)),
-            jnp.broadcast_to(rz[slot, 0, s, pl.ds(xi, 1), :], (Y, Z)),
+            jnp.broadcast_to(rz[slot, s, 1, pl.ds(xi, 1), :], (Y, Z)),
+            jnp.broadcast_to(rz[slot, s, 0, pl.ds(xi, 1), :], (Y, Z)),
         ).T
         zm = jnp.where(lane == 0, zpair, pltpu.roll(c, 1, 1))
         zp = jnp.where(lane == Z - 1, zpair, pltpu.roll(c, Z - 1, 1))
@@ -119,17 +119,21 @@
             xo[s][xi] = jnp.zeros((Y, Z), jnp.float32)
             r_ref[s, xi] = rhs_ref[s, xi]
             put_faces(s, xi, plane)
-    for c in copies(0):
-        c.start()
+        for c in copies(0, s):
+            c.start()
 
     def step(k, slot, final):
         nslot = 1 - slot
-        for c in copies(slot):
-            c.wait()
         a = ab_ref[0, k]
         b = ab_ref[1, k]
         for s in range(S):
-            for xi in range(X):
+            for c in copies(slot, s):
+                c.wait()
+            outgoing = copies(nslot, s)
+            for xi in [0, X - 1] + list(range(1, X - 1)):
+                if xi == 1:
+                    for c in outgoing[:2]:
+                        c.start()
                 c, nb = near(lambda i: dbuf[slot, s, i], slot, s, xi)
                 summed = w_ref[0, xi] * (c - nb[0])
                 for j in range(1, 6):
@@ -144,8 +148,8 @@
                     nd = a * c + b * res
                     dbuf[nslot, s, xi] = nd
                     put_faces(s, xi, nd)
-        for c in copies(nslot):
-            c.start()
+            for c in outgoing[2:]:
+                c.start()
 
     def loop_step(k, carry):
         step(k, lax.rem(k, 2), False)
@@ -155,8 +159,9 @@
     step(CHEB - 1, (CHEB - 1) % 2, True)
 
     gslot = CHEB % 2
-    for c in copies(gslot):
-        c.wait()
+    for s in range(S):
+        for c in copies(gslot, s):
+            c.wait()
     for xi in range(X):
         c0, n0 = near(lambda i: xo[0][i], gslot, 0, xi)
         c1, n1 = near(lambda i: xo[1][i], gslot, 1, xi)
@@ -182,12 +187,12 @@
             pltpu.VMEM((2, S, X, Y, Z), f32),
             pltpu.VMEM((2, S, Y, Z), f32),
             pltpu.VMEM((2, S, X, Z), f32),
-            pltpu.VMEM((2, S, X, Y), f32),
+            pltpu.VMEM((S, 2, X, Y), f32),
             pltpu.VMEM((2, 2, S, Y, Z), f32),
             pltpu.VMEM((2, 2, S, X, Z), f32),
-            pltpu.VMEM((2, 2, S, X, Y), f32),
-            pltpu.SemaphoreType.DMA((5, 2)),
-            pltpu.SemaphoreType.DMA((5, 2)),
+            pltpu.VMEM((2, S, 2, X, Y), f32),
+            pltpu.SemaphoreType.DMA((5, S, 2)),
+            pltpu.SemaphoreType.DMA((5, S, 2)),
         ],
         compiler_params=pltpu.CompilerParams(
             collective_id=0, has_side_effects=True, vmem_limit_bytes=60 * 1024 * 1024

time: 182 us -> 146 us (0.80)
  Pallas kernels: 134 us -> 98.9 us
    pallas_call x1, Pallas kernels: 134 us -> 98.9 us  [chebyshev_solve(): pl.pallas_call(functools.partial(solve_kernel, ngx, ngy), out_shape=(fiel...]
  transfers between devices with their start and end apart: 6 -> 6, of which waited for: 2 -> 2; matrix products, arithmetic and copies ran while one was open for 4% -> 5% of each run, Pallas kernels for 0% -> 0%
where the time goes in v5:
time: 146 us; the launch traced here: 145 us
  Pallas kernels  98.9 us (68%)
  starting transfers between devices  14.8 us (10%)
  local copies, waits for them, and re-layouts  14.6 us (10%)
  waiting for transfers between devices  10.2 us (7%)
  other arithmetic  4.04 us (3%)
  between operations  2.86 us (2%)
    pallas_call x1, Pallas kernels, chebyshev_solve(): pl.pallas_call(functools.partial(solve_kernel, ngx, ngy), out_shape=(fiel...  98.9 us
    ppermute x6, starting transfers between devices, ring(): lax.ppermute(x, axis, [(i, (i + step) % count) for i in range(count)])  14.8 us
    ppermute x6, waiting for transfers between devices, ring(): lax.ppermute(x, axis, [(i, (i + step) % count) for i in range(count)])  10.2 us
    unnamed x18, local copies, waits for them, and re-layouts  8.73 us
  transfers between devices with their start and end apart: 6, of which 2 were waited for; matrix products, arithmetic and copies ran while one was open for 5% of the time, Pallas kernels for 0%

profile of v5, /device:TPU:2, one launch (start us, length us, event | category | flops | bytes accessed | tf_op | source)
XLA Modules:
  0.0 145.4 jit_solution(9579131047084393009)
XLA Ops:
  0.6 0.0 copy-start
  0.6 0.9 fusion.24
  1.6 1.7 %collective-permute-start = (f32[1,128,128]{2,1,0:T(8,128)S(1)}, f32[1,128,128]{2,1,0:T(8,128)S(1)}, u32[]{:S(2)}, u32[]{:S(2)}) collective-permute-start(f32[1,128,128]{2,1,0:T(8,128)S(1)} %get-tuple-element.19), channel_id=1, source_target_pairs={{0,8},{8,16},{16,24},{24,32},{32,40},{40,48},{48,56},{56,64},{64,7... | collective-permute-start | bytes 196616 | tf_op jit(solution)/shard_map/ppermute | solution.py:19
  3.2 6.8 %collective-permute-start.1 = (f32[1,128,128]{2,1,0:T(8,128)S(1)}, f32[1,128,128]{2,1,0:T(8,128)S(1)}, u32[]{:S(2)}, u32[]{:S(2)}) collective-permute-start(f32[1,128,128]{2,1,0:T(8,128)S(1)} %get-tuple-element.18), channel_id=1, source_target_pairs={{0,248},{8,0},{16,8},{24,16},{32,24},{40,32},{48,40},{56,48},{64,5... | collective-permute-start | bytes 196616 | tf_op jit(solution)/shard_map/ppermute | solution.py:19
  10.1 0.8 fusion.22
  10.8 0.1 collective-permute-start.2
  10.9 1.7 %collective-permute-start.3 = (f32[8,1,128]{2,1,0:T(1,128)S(1)}, f32[8,1,128]{2,1,0:T(1,128)S(1)}, u32[]{:S(2)}, u32[]{:S(2)}) collective-permute-start(f32[8,1,128]{2,1,0:T(1,128)S(1)} %get-tuple-element.14), channel_id=1, source_target_pairs={{0,6},{2,0},{4,2},{6,4},{1,7},{3,1},{5,3},{7,5},{8,14},{10,8},{12,... | collective-permute-start | bytes 12296 | tf_op jit(solution)/shard_map/ppermute | solution.py:19
  12.6 1.4 fusion.20
  14.1 0.2 copy.12
  14.2 0.2 copy.13
  14.4 1.0 copy.11
  15.5 2.1 %collective-permute-start.4 = (f32[8,128,2]{2,1,0:T(8,128)}, f32[8,128,2]{2,1,0:T(8,128)S(1)}, u32[]{:S(2)}, u32[]{:S(2)}) collective-permute-start(f32[8,128,2]{2,1,0:T(8,128)} %copy.11), channel_id=1, source_target_pairs={{0,1},{1,0},{2,3},{3,2},{4,5},{5,4},{6,7},{7,6},{8,9},{9,8},{10,11... | collective-permute-start | bytes 24584 | tf_op jit(solution)/shard_map/ppermute | solution.py:19
  19.0 0.0 copy-done
  19.0 1.0 fusion.23
  20.0 0.1 fusion.21
  20.1 0.2 fusion.18
  21.0 0.1 stack.157
  21.1 0.1 stack.175
  21.2 0.0 copy-start.2
  21.2 0.6 pad_maximum_fusion.2.ab_ref
  21.8 8.2 %collective-permute-done.4 = f32[8,128,2]{2,1,0:T(8,128)S(1)} collective-permute-done((f32[8,128,2]{2,1,0:T(8,128)}, f32[8,128,2]{2,1,0:T(8,128)S(1)}, u32[]{:S(2)}, u32[]{:S(2)}) %collective-permute-start.4) | collective-permute-done | bytes 8224 | tf_op jit(solution)/shard_map/ppermute | solution.py:19
  29.9 2.4 %collective-permute-start.5 = (bf16[8,128,128]{2,1,0:T(8,128)(2,1)}, bf16[8,128,128]{2,1,0:T(8,128)(2,1)S(1)}, u32[]{:S(2)}, u32[]{:S(2)}) collective-permute-start(bf16[8,128,128]{2,1,0:T(8,128)(2,1)} %param.6), channel_id=1, source_target_pairs={{0,1},{1,0},{2,3},{3,2},{4,5},{5,4},{6,7},{7,6},{8,9},{9,8},{10,11... | collective-permute-start | bytes 786440 | tf_op jit(solution)/shard_map/ppermute | solution.py:19
  32.4 0.2 fusion.19
  32.6 0.0 collective-permute-done
  32.6 1.1 fusion.2
  33.6 0.0 collective-permute-done.1
  33.7 0.0 copy-done.2
  33.7 0.1 fusion.5
  33.7 0.0 collective-permute-done.2
  33.7 0.1 fusion.8
  33.8 0.0 copy-start.5
  33.8 0.0 collective-permute-done.3
  33.9 0.0 copy-start.4
  33.9 0.1 fusion.11
  33.9 0.2 fusion.14
  34.1 0.2 fusion.17.w_ref
  34.4 0.0 copy-start.1
  34.4 1.6 %copy-done.1 = f32[6,8,128,128]{3,2,1,0:T(8,128)} copy-done((f32[6,8,128,128]{3,2,1,0:T(8,128)}, f32[6,8,128,128]{3,2,1,0:T(8,128)S(1)}, u32[]{:S(2)}) %copy-start.1) | copy-done | bytes 3145752
  36.0 2.0 %collective-permute-done.5 = bf16[8,128,128]{2,1,0:T(8,128)(2,1)S(1)} collective-permute-done((bf16[8,128,128]{2,1,0:T(8,128)(2,1)}, bf16[8,128,128]{2,1,0:T(8,128)(2,1)S(1)}, u32[]{:S(2)}, u32[]{:S(2)}) %collective-permute-start.5) | collective-permute-done | bytes 262176 | tf_op jit(solution)/shard_map/ppermute | solution.py:19
  38.0 0.2 multiply_bitcast_fusion
  38.2 0.0 copy-done.4
  38.2 1.5 %broadcast_divide_fusion = (f32[2,8,128,128]{3,2,1,0:T(8,128)}, f32[2,8,128,128]{3,2,1,0:T(8,128)}) fusion(f32[]{:T(128)} %bitcast, f32[1,8,128,128]{3,2,1,0:T(8,128)S(1)} %bitcast.63, f32[1,8,128,128]{3,2,1,0:T(8,128)S(1)} %multiply_bitcast_fusion), kind=kLoop, calls=%fused_computation.25 | loop fusion | flops 524288 | bytes 3145732 | tf_op jit(solution)/shard_map/div | solution.py:221
  39.8 98.9 %shard_map.84 = (f32[8,128,128]{2,1,0:T(8,128)}, f32[8,128,128]{2,1,0:T(8,128)}, f32[8,128,128]{2,1,0:T(8,128)}, f32[2,8,128,128]{3,2,1,0:T(8,128)}) custom-call(f32[2,16]{1,0:T(2,128)} %pad_maximum_fusion.2.ab_ref, f32[6,8,128,128]{3,2,1,0:T(8,128)} %copy-done.1, f32[2,8,128,128]{3,2,1,0:T(8,128)} %get-tuple-element.5.rhs_ref, ...), custom_call_target="tpu_custom_call" | custom-call | tf_op jit(solution)/shard_map/pallas_call | solution.py:181
  138.7 2.0 %copy.24 = f32[8,128,128]{2,1,0:T(8,128)} copy(f32[8,128,128]{2,1,0:T(8,128)} %get-tuple-element.24) | data formatting | bytes 1048576
  140.7 1.9 %copy.25 = f32[8,128,128]{2,1,0:T(8,128)} copy(f32[8,128,128]{2,1,0:T(8,128)} %get-tuple-element.25) | data formatting | bytes 1048576
  142.6 1.9 %copy.26 = f32[8,128,128]{2,1,0:T(8,128)} copy(f32[8,128,128]{2,1,0:T(8,128)} %get-tuple-element.26) | data formatting | bytes 1048576
  144.4 0.0 copy-done.3
  144.4 1.0 copy.27
  (3 shorter events, 0.0 us)
Async XLA Ops:
  0.6 18.4 %copy-start = (f32[8,128,128]{2,1,0:T(8,128)S(1)}, f32[8,128,128]{2,1,0:T(8,128)}, u32[]{:S(2)}) copy-start(f32[8,128,128]{2,1,0:T(8,128)} %param.5) | copy-start | bytes 1572868
  1.6 31.0 %collective-permute-start = (f32[1,128,128]{2,1,0:T(8,128)S(1)}, f32[1,128,128]{2,1,0:T(8,128)S(1)}, u32[]{:S(2)}, u32[]{:S(2)}) collective-permute-start(f32[1,128,128]{2,1,0:T(8,128)S(1)} %get-tuple-element.19), channel_id=1, source_target_pairs={{0,8},{8,16},{16,24},{24,32},{32,40},{40,48},{48,56},{56,64},{64,7... | collective-permute-start | bytes 196616 | tf_op jit(solution)/shard_map/ppermute | solution.py:19
  3.2 30.4 %collective-permute-start.1 = (f32[1,128,128]{2,1,0:T(8,128)S(1)}, f32[1,128,128]{2,1,0:T(8,128)S(1)}, u32[]{:S(2)}, u32[]{:S(2)}) collective-permute-start(f32[1,128,128]{2,1,0:T(8,128)S(1)} %get-tuple-element.18), channel_id=1, source_target_pairs={{0,248},{8,0},{16,8},{24,16},{32,24},{40,32},{48,40},{56,48},{64,5... | collective-permute-start | bytes 196616 | tf_op jit(solution)/shard_map/ppermute | solution.py:19
  10.8 22.9 %collective-permute-start.2 = (f32[8,1,128]{2,1,0:T(1,128)S(1)}, f32[8,1,128]{2,1,0:T(1,128)S(1)}, u32[]{:S(2)}, u32[]{:S(2)}) collective-permute-start(f32[8,1,128]{2,1,0:T(1,128)S(1)} %get-tuple-element.15), channel_id=1, source_target_pairs={{0,2},{2,4},{4,6},{6,0},{1,3},{3,5},{5,7},{7,1},{8,10},{10,12},{12... | collective-permute-start | bytes 12296 | tf_op jit(solution)/shard_map/ppermute | solution.py:19
  10.9 22.9 %collective-permute-start.3 = (f32[8,1,128]{2,1,0:T(1,128)S(1)}, f32[8,1,128]{2,1,0:T(1,128)S(1)}, u32[]{:S(2)}, u32[]{:S(2)}) collective-permute-start(f32[8,1,128]{2,1,0:T(1,128)S(1)} %get-tuple-element.14), channel_id=1, source_target_pairs={{0,6},{2,0},{4,2},{6,4},{1,7},{3,1},{5,3},{7,5},{8,14},{10,8},{12,... | collective-permute-start | bytes 12296 | tf_op jit(solution)/shard_map/ppermute | solution.py:19
  15.5 14.5 %collective-permute-start.4 = (f32[8,128,2]{2,1,0:T(8,128)}, f32[8,128,2]{2,1,0:T(8,128)S(1)}, u32[]{:S(2)}, u32[]{:S(2)}) collective-permute-start(f32[8,128,2]{2,1,0:T(8,128)} %copy.11), channel_id=1, source_target_pairs={{0,1},{1,0},{2,3},{3,2},{4,5},{5,4},{6,7},{7,6},{8,9},{9,8},{10,11... | collective-permute-start | bytes 24584 | tf_op jit(solution)/shard_map/ppermute | solution.py:19
  21.2 12.5 %copy-start.2 = (f32[7,128,128]{2,1,0:T(8,128)S(1)}, f32[7,128,128]{2,1,0:T(8,128)}, u32[]{:S(2)}) copy-start(f32[7,128,128]{2,1,0:T(8,128)} %get-tuple-element.16) | copy-start | bytes 1376260
  29.9 8.1 %collective-permute-start.5 = (bf16[8,128,128]{2,1,0:T(8,128)(2,1)}, bf16[8,128,128]{2,1,0:T(8,128)(2,1)S(1)}, u32[]{:S(2)}, u32[]{:S(2)}) collective-permute-start(bf16[8,128,128]{2,1,0:T(8,128)(2,1)} %param.6), channel_id=1, source_target_pairs={{0,1},{1,0},{2,3},{3,2},{4,5},{5,4},{6,7},{7,6},{8,9},{9,8},{10,11... | collective-permute-start | bytes 786440 | tf_op jit(solution)/shard_map/ppermute | solution.py:19
  33.8 4.2 %copy-start.5 = (f32[8,128]{1,0:T(8,128)S(1)}, f32[8,128]{1,0:T(8,128)}, u32[]{:S(2)}) copy-start(f32[8,128]{1,0:T(8,128)} %param.7) | copy-start | bytes 12292
  33.9 4.4 %copy-start.4 = (f32[8,128,128]{2,1,0:T(8,128)S(1)}, f32[8,128,128]{2,1,0:T(8,128)}, u32[]{:S(2)}) copy-start(f32[8,128,128]{2,1,0:T(8,128)} %param.8) | copy-start | bytes 1572868
  34.4 1.7 %copy-start.1 = (f32[6,8,128,128]{3,2,1,0:T(8,128)}, f32[6,8,128,128]{3,2,1,0:T(8,128)S(1)}, u32[]{:S(2)}) copy-start(f32[6,8,128,128]{3,2,1,0:T(8,128)S(1)} %fusion.17.w_ref) | copy-start | bytes 9437188
  138.7 5.7 %copy-start.3 = (f32[2,8,128,128]{3,2,1,0:T(8,128)S(1)}, f32[2,8,128,128]{3,2,1,0:T(8,128)}, u32[]{:S(2)}) copy-start(f32[2,8,128,128]{3,2,1,0:T(8,128)} %get-tuple-element.27) | copy-start | bytes 3145732

commit v6 on v5

--- a/solution.py
+++ b/solution.py
@@ -14,42 +14,10 @@
 time_step = 8.0
 
 
-def ring(x, axis, step):
-    count = lax.axis_size(axis)
-    return lax.ppermute(x, axis, [(i, (i + step) % count) for i in range(count)])
-
-
-def halos(cells):
-    nd = cells.ndim
-    dx, dy, dz = nd - 3, nd - 2, nd - 1
-    x_lo = ring(lax.slice_in_dim(cells, cells.shape[dx] - 1, cells.shape[dx], axis=dx), "gx", 1)
-    x_hi = ring(lax.slice_in_dim(cells, 0, 1, axis=dx), "gx", -1)
-    y_lo = ring(lax.slice_in_dim(cells, cells.shape[dy] - 1, cells.shape[dy], axis=dy), "gy", 1)
-    y_hi = ring(lax.slice_in_dim(cells, 0, 1, axis=dy), "gy", -1)
-    ends = jnp.concatenate(
-        [lax.slice_in_dim(cells, 0, 1, axis=dz), lax.slice_in_dim(cells, cells.shape[dz] - 1, cells.shape[dz], axis=dz)],
-        axis=dz,
-    )
-    got = ring(ends, "pa", 1)
-    z_lo = lax.slice_in_dim(got, 1, 2, axis=dz)
-    z_hi = lax.slice_in_dim(got, 0, 1, axis=dz)
-    return (x_lo, x_hi, y_lo, y_hi, z_lo, z_hi)
-
-
-def neighbours(cells, faces):
-    nd = cells.ndim
-    out = []
-    for k, dim in enumerate((nd - 3, nd - 2, nd - 1)):
-        lo, hi = faces[2 * k], faces[2 * k + 1]
-        n = cells.shape[dim]
-        out.append(jnp.concatenate([lo, lax.slice_in_dim(cells, 0, n - 1, axis=dim)], axis=dim))
-        out.append(jnp.concatenate([lax.slice_in_dim(cells, 1, n, axis=dim), hi], axis=dim))
-    return out
-
-
-def solve_kernel(ngx, ngy, ab_ref, w_ref, rhs_ref, d0_ref, g_ref, adj_ref, state_ref, r_ref,
-                 dbuf, sx, sy, sz, rx, ry, rz, send_sem, recv_sem):
-    S, X, Y, Z = rhs_ref.shape
+def solve_kernel(ngx, ngy, ab_ref, kap_ref, st_ref, rs_ref, cot_ref, g_ref, adj_ref, state_ref, r_ref,
+                 w_ref, prev, dbuf, sx, sy, sz, rx, ry, rz, send_sem, recv_sem, st_sem):
+    S = 2
+    X, Y, Z = kap_ref.shape
     xo = (state_ref, adj_ref)
     gx = lax.axis_index("gx")
     gy = lax.axis_index("gy")
@@ -112,12 +80,36 @@
         zp = jnp.where(lane == Z - 1, zpair, pltpu.roll(c, Z - 1, 1))
         return c, (xm, xp, ym, yp, zm, zp)
 
+    swap = pltpu.make_async_remote_copy(
+        src_ref=st_ref, dst_ref=prev, send_sem=st_sem.at[0], recv_sem=st_sem.at[1],
+        device_id=peers[4], device_id_type=MESH,
+    )
+    swap.start()
+
+    for xi in range(X):
+        put_faces(0, xi, kap_ref[xi])
+    for c in copies(1, 0):
+        c.start()
+    for c in copies(1, 0):
+        c.wait()
+    for xi in range(X):
+        kc, nb = near(lambda i: kap_ref[i], 1, 0, xi)
+        for j in range(6):
+            w_ref[j, xi] = (kc + nb[j]) * (0.5 * time_step)
+
+    swap.wait()
+    theta = ab_ref[2, 0]
     for s in range(S):
         for xi in range(X):
-            plane = d0_ref[s, xi]
+            if s == 0:
+                scale = jnp.broadcast_to(rs_ref[pl.ds(xi, 1), :], (Z, Y)).T
+                rhs = prev[xi].astype(jnp.float32) * scale
+            else:
+                rhs = cot_ref[xi]
+            plane = rhs / theta
             dbuf[0, s, xi] = plane
             xo[s][xi] = jnp.zeros((Y, Z), jnp.float32)
-            r_ref[s, xi] = rhs_ref[s, xi]
+            r_ref[s, xi] = rhs
             put_faces(s, xi, plane)
         for c in copies(0, s):
             c.start()
@@ -171,8 +163,25 @@
         g_ref[xi] = (-0.5 * time_step) * summed
 
 
-def chebyshev_solve(weights, rhs, d0, ab):
-    S, X, Y, Z = rhs.shape
+def body(conductivity, stored_state, row_scales, cotangent, upper_bound):
+    X, Y, Z = conductivity.shape
+    S = 2
+    upper = upper_bound[0]
+    theta = 0.5 * (upper + 1.0)
+    delta = 0.5 * (upper - 1.0)
+    sigma = theta / delta
+    rho = 1.0 / sigma
+    coefs = []
+    for _ in range(CHEB):
+        rho_next = 1.0 / (2.0 * sigma - rho)
+        coefs.append((rho_next * rho, 2.0 * rho_next / delta))
+        rho = rho_next
+    ab = jnp.stack([
+        jnp.stack([c[0] for c in coefs]),
+        jnp.stack([c[1] for c in coefs]),
+        jnp.broadcast_to(theta, (CHEB,)),
+    ])
+
     ngx = lax.axis_size("gx")
     ngy = lax.axis_size("gy")
     f32 = jnp.float32
@@ -180,10 +189,12 @@
     field = jax.ShapeDtypeStruct((X, Y, Z), f32)
     return pl.pallas_call(
         functools.partial(solve_kernel, ngx, ngy),
-        out_shape=(field, field, field, jax.ShapeDtypeStruct(rhs.shape, f32)),
-        in_specs=[pl.BlockSpec(memory_space=pltpu.SMEM), vmem, vmem, vmem],
+        out_shape=(field, field, field, jax.ShapeDtypeStruct((S, X, Y, Z), f32)),
+        in_specs=[pl.BlockSpec(memory_space=pltpu.SMEM), vmem, vmem, vmem, vmem],
         out_specs=(vmem, vmem, vmem, vmem),
         scratch_shapes=[
+            pltpu.VMEM((6, X, Y, Z), f32),
+            pltpu.VMEM((X, Y, Z), stored_state.dtype),
             pltpu.VMEM((2, S, X, Y, Z), f32),
             pltpu.VMEM((2, S, Y, Z), f32),
             pltpu.VMEM((2, S, X, Z), f32),
@@ -193,32 +204,12 @@
             pltpu.VMEM((2, S, 2, X, Y), f32),
             pltpu.SemaphoreType.DMA((5, S, 2)),
             pltpu.SemaphoreType.DMA((5, S, 2)),
+            pltpu.SemaphoreType.DMA((2,)),
         ],
         compiler_params=pltpu.CompilerParams(
             collective_id=0, has_side_effects=True, vmem_limit_bytes=60 * 1024 * 1024
         ),
-    )(ab, weights, rhs, d0)
-
-
-def body(conductivity, stored_state, row_scales, cotangent, upper_bound):
-    upper = upper_bound[0]
-    weights = jnp.stack([(conductivity + kn) * (0.5 * time_step) for kn in neighbours(conductivity, halos(conductivity))])
-    partner = ring(stored_state, "pa", 1)
-    previous = partner.astype(jnp.float32) * row_scales[:, :, None]
-    rhs = jnp.stack((previous, cotangent))
-
-    theta = 0.5 * (upper + 1.0)
-    delta = 0.5 * (upper - 1.0)
-    sigma = theta / delta
-    rho = 1.0 / sigma
-    coefs = []
-    for _ in range(CHEB):
-        rho_next = 1.0 / (2.0 * sigma - rho)
-        coefs.append((rho_next * rho, 2.0 * rho_next / delta))
-        rho = rho_next
-    ab = jnp.stack([jnp.stack([c[0] for c in coefs]), jnp.stack([c[1] for c in coefs])])
-
-    return chebyshev_solve(weights, rhs, rhs / theta, ab)
+    )(ab, conductivity, stored_state, row_scales, cotangent)
 
 
 def solution(mesh):

time: 146 us -> 120 us (0.82)
  starting transfers between devices: 14.8 us -> 0 us
  Pallas kernels: 98.9 us -> 112 us
  waiting for transfers between devices: 10.2 us -> 0 us
  local copies, waits for them, and re-layouts: 14.6 us -> 4.79 us
  other arithmetic: 4.04 us -> 0.65 us
    ppermute x6 -> x0, starting transfers between devices: 14.8 us -> none  [ring(): lax.ppermute(x, axis, [(i, (i + step) % count) for i in range(count)])]
    pallas_call x1, Pallas kernels: 98.9 us -> 112 us  [body(): pl.pallas_call(functools.partial(solve_kernel, ngx, ngy), out_shape=(fiel...]
    ppermute x6 -> x0, waiting for transfers between devices: 10.2 us -> none  [ring(): lax.ppermute(x, axis, [(i, (i + step) % count) for i in range(count)])]
    slice x7 -> x0, local copies, waits for them, and re-layouts: 4.62 us -> none  [the longest x1 1.4 us: halos(): lax.slice_in_dim(cells, 0, 1, axis=dz)]
    unnamed x18 -> x10, local copies, waits for them, and re-layouts: 8.73 us -> 4.53 us
    div x1 -> x0, other arithmetic: 1.53 us -> none  [body(): return chebyshev_solve(weights, rhs, rhs / theta, ab)]
    unnamed x5 -> x0, other arithmetic: 1.49 us -> none
  transfers between devices with their start and end apart: 6 -> 0, of which waited for: 2 -> 0; matrix products, arithmetic and copies ran while one was open for 5% -> 0% of each run, Pallas kernels for 0% -> 0%
where the time goes in v6:
time: 120 us
  Pallas kernels  112 us (93%)
  local copies, waits for them, and re-layouts  4.79 us (4%)
  between operations  2.72 us (2%)
    pallas_call x1, Pallas kernels, body(): pl.pallas_call(functools.partial(solve_kernel, ngx, ngy), out_shape=(fiel...  112 us
    unnamed x10, local copies, waits for them, and re-layouts  4.53 us

profile of v6, /device:TPU:2, one launch (start us, length us, event | category | flops | bytes accessed | tf_op | source)
XLA Modules:
  0.0 119.8 jit_solution(8019047307099824624)
XLA Ops:
  2.7 0.1 stack.127
  2.8 0.1 stack.145
  2.9 0.1 pad.2.clone
  3.0 0.7 maximum_maximum_fusion.ab_ref
  3.6 111.7 %shard_map.84 = (f32[8,128,128]{2,1,0:T(8,128)}, f32[8,128,128]{2,1,0:T(8,128)}, f32[8,128,128]{2,1,0:T(8,128)}, f32[2,8,128,128]{3,2,1,0:T(8,128)}) custom-call(f32[3,16]{1,0:T(4,128)} %maximum_maximum_fusion.ab_ref, f32[8,128,128]{2,1,0:T(8,128)} %kap_ref.1, bf16[8,128,128]{2,1,0:T(8,128)(2,1)} %st_ref.1, f32[8,128]{1,0:T(8,128)} %rs_ref.1, ...), custom_call_target="tpu_custom_call" | custom-call | tf_op jit(solution)/shard_map/pallas_call | solution.py:190
  115.3 0.0 copy-start.2
  115.3 0.0 copy-start.1
  115.3 2.0 %copy.14 = f32[8,128,128]{2,1,0:T(8,128)} copy(f32[8,128,128]{2,1,0:T(8,128)} %get-tuple-element.8) | data formatting | bytes 1048576
  117.2 0.0 copy-done.2
  117.3 0.0 copy-start
  117.3 0.8 copy.15
  118.0 0.0 copy-done.1
  118.0 0.8 copy.16
  118.8 0.0 copy-done
  118.8 1.0 copy.17
Async XLA Ops:
  115.3 2.0 %copy-start.2 = (f32[8,128,128]{2,1,0:T(8,128)S(1)}, f32[8,128,128]{2,1,0:T(8,128)}, u32[]{:S(2)}) copy-start(f32[8,128,128]{2,1,0:T(8,128)} %get-tuple-element.9) | copy-start | bytes 1572868
  115.3 2.8 %copy-start.1 = (f32[8,128,128]{2,1,0:T(8,128)S(1)}, f32[8,128,128]{2,1,0:T(8,128)}, u32[]{:S(2)}) copy-start(f32[8,128,128]{2,1,0:T(8,128)} %get-tuple-element.10) | copy-start | bytes 1572868
  117.3 1.6 %copy-start = (f32[2,8,128,128]{3,2,1,0:T(8,128)S(1)}, f32[2,8,128,128]{3,2,1,0:T(8,128)}, u32[]{:S(2)}) copy-start(f32[2,8,128,128]{3,2,1,0:T(8,128)} %get-tuple-element.11) | copy-start | bytes 3145732

commit v7 on v6

--- a/solution.py
+++ b/solution.py
@@ -15,7 +15,7 @@
 
 
 def solve_kernel(ngx, ngy, ab_ref, kap_ref, st_ref, rs_ref, cot_ref, g_ref, adj_ref, state_ref, r_ref,
-                 w_ref, prev, dbuf, sx, sy, sz, rx, ry, rz, send_sem, recv_sem, st_sem):
+                 w_ref, prev, dbuf, sx, sy, sz, rx, ry, rz, ax, ay, az, send_sem, recv_sem, st_sem):
     S = 2
     X, Y, Z = kap_ref.shape
     xo = (state_ref, adj_ref)
@@ -64,17 +64,17 @@
     row = lax.broadcasted_iota(jnp.int32, (Y, Z), 0)
     lane = lax.broadcasted_iota(jnp.int32, (Y, Z), 1)
 
-    def near(plane, slot, s, xi):
+    def near(plane, hx, hy, hz, s, xi):
         c = plane(xi)
-        xm = plane(xi - 1) if xi > 0 else rx[slot, 0, s]
-        xp = plane(xi + 1) if xi < X - 1 else rx[slot, 1, s]
-        ym = jnp.where(row == 0, jnp.broadcast_to(ry[slot, 0, s, pl.ds(xi, 1), :], (Y, Z)), pltpu.roll(c, 1, 0))
-        yp = jnp.where(row == Y - 1, jnp.broadcast_to(ry[slot, 1, s, pl.ds(xi, 1), :], (Y, Z)),
+        xm = plane(xi - 1) if xi > 0 else hx[0, s]
+        xp = plane(xi + 1) if xi < X - 1 else hx[1, s]
+        ym = jnp.where(row == 0, jnp.broadcast_to(hy[0, s, pl.ds(xi, 1), :], (Y, Z)), pltpu.roll(c, 1, 0))
+        yp = jnp.where(row == Y - 1, jnp.broadcast_to(hy[1, s, pl.ds(xi, 1), :], (Y, Z)),
                        pltpu.roll(c, Y - 1, 0))
         zpair = jnp.where(
             row < Y // 2,
-            jnp.broadcast_to(rz[slot, s, 1, pl.ds(xi, 1), :], (Y, Z)),
-            jnp.broadcast_to(rz[slot, s, 0, pl.ds(xi, 1), :], (Y, Z)),
+            jnp.broadcast_to(hz[s, 1, pl.ds(xi, 1), :], (Y, Z)),
+            jnp.broadcast_to(hz[s, 0, pl.ds(xi, 1), :], (Y, Z)),
         ).T
         zm = jnp.where(lane == 0, zpair, pltpu.roll(c, 1, 1))
         zp = jnp.where(lane == Z - 1, zpair, pltpu.roll(c, Z - 1, 1))
@@ -85,21 +85,9 @@
         device_id=peers[4], device_id_type=MESH,
     )
     swap.start()
-
-    for xi in range(X):
-        put_faces(0, xi, kap_ref[xi])
-    for c in copies(1, 0):
-        c.start()
-    for c in copies(1, 0):
-        c.wait()
-    for xi in range(X):
-        kc, nb = near(lambda i: kap_ref[i], 1, 0, xi)
-        for j in range(6):
-            w_ref[j, xi] = (kc + nb[j]) * (0.5 * time_step)
-
-    swap.wait()
     theta = ab_ref[2, 0]
-    for s in range(S):
+
+    def start_solve(s):
         for xi in range(X):
             if s == 0:
                 scale = jnp.broadcast_to(rs_ref[pl.ds(xi, 1), :], (Z, Y)).T
@@ -114,34 +102,53 @@
         for c in copies(0, s):
             c.start()
 
+    start_solve(1)
+
+    for xi in range(X):
+        put_faces(0, xi, kap_ref[xi])
+    for c in copies(1, 0):
+        c.start()
+    for c in copies(1, 0):
+        c.wait()
+    for xi in range(X):
+        kc, nb = near(lambda i: kap_ref[i], rx.at[1], ry.at[1], rz.at[1], 0, xi)
+        for j in range(6):
+            w_ref[j, xi] = (kc + nb[j]) * (0.5 * time_step)
+
+    swap.wait()
+    start_solve(0)
+    for q in (ax, ay, az):
+        q[...] = jnp.zeros(q.shape, jnp.float32)
+
     def step(k, slot, final):
         nslot = 1 - slot
         a = ab_ref[0, k]
         b = ab_ref[1, k]
-        for s in range(S):
+        for s in (1, 0):
             for c in copies(slot, s):
                 c.wait()
+            ax[:, s] = ax[:, s] + rx[slot, :, s]
+            ay[:, s] = ay[:, s] + ry[slot, :, s]
+            az[s] = az[s] + rz[slot, s]
             outgoing = copies(nslot, s)
             for xi in [0, X - 1] + list(range(1, X - 1)):
-                if xi == 1:
+                if xi == 1 and not final:
                     for c in outgoing[:2]:
                         c.start()
-                c, nb = near(lambda i: dbuf[slot, s, i], slot, s, xi)
+                c, nb = near(lambda i: dbuf[slot, s, i], rx.at[slot], ry.at[slot], rz.at[slot], s, xi)
                 summed = w_ref[0, xi] * (c - nb[0])
                 for j in range(1, 6):
                     summed = summed + w_ref[j, xi] * (c - nb[j])
-                xn = xo[s][xi] + c
-                xo[s][xi] = xn
+                xo[s][xi] = xo[s][xi] + c
                 res = r_ref[s, xi] - (c + summed)
                 r_ref[s, xi] = res
-                if final:
-                    put_faces(s, xi, xn)
-                else:
+                if not final:
                     nd = a * c + b * res
                     dbuf[nslot, s, xi] = nd
                     put_faces(s, xi, nd)
-            for c in outgoing[2:]:
-                c.start()
+            if not final:
+                for c in outgoing[2:]:
+                    c.start()
 
     def loop_step(k, carry):
         step(k, lax.rem(k, 2), False)
@@ -150,13 +157,9 @@
     lax.fori_loop(0, CHEB - 1, loop_step, 0)
     step(CHEB - 1, (CHEB - 1) % 2, True)
 
-    gslot = CHEB % 2
-    for s in range(S):
-        for c in copies(gslot, s):
-            c.wait()
     for xi in range(X):
-        c0, n0 = near(lambda i: xo[0][i], gslot, 0, xi)
-        c1, n1 = near(lambda i: xo[1][i], gslot, 1, xi)
+        c0, n0 = near(lambda i: xo[0][i], ax, ay, az, 0, xi)
+        c1, n1 = near(lambda i: xo[1][i], ax, ay, az, 1, xi)
         summed = (c0 - n0[0]) * (c1 - n1[0])
         for j in range(1, 6):
             summed = summed + (c0 - n0[j]) * (c1 - n1[j])
@@ -202,6 +205,9 @@
             pltpu.VMEM((2, 2, S, Y, Z), f32),
             pltpu.VMEM((2, 2, S, X, Z), f32),
             pltpu.VMEM((2, S, 2, X, Y), f32),
+            pltpu.VMEM((2, S, Y, Z), f32),
+            pltpu.VMEM((2, S, X, Z), f32),
+            pltpu.VMEM((S, 2, X, Y), f32),
             pltpu.SemaphoreType.DMA((5, S, 2)),
             pltpu.SemaphoreType.DMA((5, S, 2)),
             pltpu.SemaphoreType.DMA((2,)),

time: 120 us -> 114 us (0.950)
  Pallas kernels: 112 us -> 106 us
    pallas_call x1, Pallas kernels: 112 us -> 106 us  [body(): pl.pallas_call(functools.partial(solve_kernel, ngx, ngy), out_shape=(fiel...]
where the time goes in v7:
time: 114 us
  Pallas kernels  106 us (93%)
  local copies, waits for them, and re-layouts  4.79 us (4%)
  between operations  2.72 us (2%)
    pallas_call x1, Pallas kernels, body(): pl.pallas_call(functools.partial(solve_kernel, ngx, ngy), out_shape=(fiel...  106 us
    unnamed x10, local copies, waits for them, and re-layouts  4.53 us

profile of v7, /device:TPU:2, one launch (start us, length us, event | category | flops | bytes accessed | tf_op | source)
XLA Modules:
  0.0 113.8 jit_solution(873825730424581665)
XLA Ops:
  2.7 0.1 stack.127
  2.8 0.1 stack.145
  2.9 0.1 pad.2.clone
  3.0 0.7 maximum_maximum_fusion.ab_ref
  3.6 105.7 %shard_map.84 = (f32[8,128,128]{2,1,0:T(8,128)}, f32[8,128,128]{2,1,0:T(8,128)}, f32[8,128,128]{2,1,0:T(8,128)}, f32[2,8,128,128]{3,2,1,0:T(8,128)}) custom-call(f32[3,16]{1,0:T(4,128)} %maximum_maximum_fusion.ab_ref, f32[8,128,128]{2,1,0:T(8,128)} %kap_ref.1, bf16[8,128,128]{2,1,0:T(8,128)(2,1)} %st_ref.1, f32[8,128]{1,0:T(8,128)} %rs_ref.1, ...), custom_call_target="tpu_custom_call" | custom-call | tf_op jit(solution)/shard_map/pallas_call | solution.py:193
  109.3 0.0 copy-start.2
  109.3 0.0 copy-start.1
  109.3 2.0 %copy.14 = f32[8,128,128]{2,1,0:T(8,128)} copy(f32[8,128,128]{2,1,0:T(8,128)} %get-tuple-element.8) | data formatting | bytes 1048576
  111.3 0.0 copy-done.2
  111.3 0.0 copy-start
  111.3 0.8 copy.15
  112.1 0.0 copy-done.1
  112.1 0.8 copy.16
  112.9 0.0 copy-done
  112.9 1.0 copy.17
Async XLA Ops:
  109.3 2.0 %copy-start.2 = (f32[8,128,128]{2,1,0:T(8,128)S(1)}, f32[8,128,128]{2,1,0:T(8,128)}, u32[]{:S(2)}) copy-start(f32[8,128,128]{2,1,0:T(8,128)} %get-tuple-element.9) | copy-start | bytes 1572868
  109.3 2.8 %copy-start.1 = (f32[8,128,128]{2,1,0:T(8,128)S(1)}, f32[8,128,128]{2,1,0:T(8,128)}, u32[]{:S(2)}) copy-start(f32[8,128,128]{2,1,0:T(8,128)} %get-tuple-element.10) | copy-start | bytes 1572868
  111.3 1.6 %copy-start = (f32[2,8,128,128]{3,2,1,0:T(8,128)S(1)}, f32[2,8,128,128]{3,2,1,0:T(8,128)}, u32[]{:S(2)}) copy-start(f32[2,8,128,128]{3,2,1,0:T(8,128)} %get-tuple-element.11) | copy-start | bytes 3145732

commit v8 on v7

--- a/solution.py
+++ b/solution.py
@@ -125,16 +125,16 @@
         a = ab_ref[0, k]
         b = ab_ref[1, k]
         for s in (1, 0):
-            for c in copies(slot, s):
+            incoming = copies(slot, s)
+            for c in incoming[2:]:
                 c.wait()
-            ax[:, s] = ax[:, s] + rx[slot, :, s]
             ay[:, s] = ay[:, s] + ry[slot, :, s]
             az[s] = az[s] + rz[slot, s]
-            outgoing = copies(nslot, s)
-            for xi in [0, X - 1] + list(range(1, X - 1)):
-                if xi == 1 and not final:
-                    for c in outgoing[:2]:
-                        c.start()
+            for xi in list(range(1, X - 1)) + [0, X - 1]:
+                if xi == 0:
+                    for c in incoming[:2]:
+                        c.wait()
+                    ax[:, s] = ax[:, s] + rx[slot, :, s]
                 c, nb = near(lambda i: dbuf[slot, s, i], rx.at[slot], ry.at[slot], rz.at[slot], s, xi)
                 summed = w_ref[0, xi] * (c - nb[0])
                 for j in range(1, 6):
@@ -147,7 +147,7 @@
                     dbuf[nslot, s, xi] = nd
                     put_faces(s, xi, nd)
             if not final:
-                for c in outgoing[2:]:
+                for c in copies(nslot, s):
                     c.start()
 
     def loop_step(k, carry):

time: 114 us -> 113 us (level)
  no operation moved by 1% of the time
where the time goes in v8:
time: 113 us
  Pallas kernels  105 us (93%)
  local copies, waits for them, and re-layouts  4.79 us (4%)
  between operations  2.72 us (2%)
    pallas_call x1, Pallas kernels, body(): pl.pallas_call(functools.partial(solve_kernel, ngx, ngy), out_shape=(fiel...  105 us
    unnamed x10, local copies, waits for them, and re-layouts  4.53 us

profile of v8, /device:TPU:2, one launch (start us, length us, event | category | flops | bytes accessed | tf_op | source)
XLA Modules:
  0.0 113.2 jit_solution(284189690126662243)
XLA Ops:
  2.7 0.1 stack.127
  2.8 0.1 stack.145
  2.9 0.1 pad.2.clone
  3.0 0.7 maximum_maximum_fusion.ab_ref
  3.6 105.0 %shard_map.84 = (f32[8,128,128]{2,1,0:T(8,128)}, f32[8,128,128]{2,1,0:T(8,128)}, f32[8,128,128]{2,1,0:T(8,128)}, f32[2,8,128,128]{3,2,1,0:T(8,128)}) custom-call(f32[3,16]{1,0:T(4,128)} %maximum_maximum_fusion.ab_ref, f32[8,128,128]{2,1,0:T(8,128)} %kap_ref.1, bf16[8,128,128]{2,1,0:T(8,128)(2,1)} %st_ref.1, f32[8,128]{1,0:T(8,128)} %rs_ref.1, ...), custom_call_target="tpu_custom_call" | custom-call | tf_op jit(solution)/shard_map/pallas_call | solution.py:193
  108.6 0.0 copy-start.2
  108.6 0.0 copy-start.1
  108.6 2.0 %copy.14 = f32[8,128,128]{2,1,0:T(8,128)} copy(f32[8,128,128]{2,1,0:T(8,128)} %get-tuple-element.8) | data formatting | bytes 1048576
  110.6 0.0 copy-done.2
  110.6 0.0 copy-start
  110.6 0.8 copy.15
  111.4 0.0 copy-done.1
  111.4 0.8 copy.16
  112.2 0.0 copy-done
  112.2 1.0 copy.17
Async XLA Ops:
  108.6 2.0 %copy-start.2 = (f32[8,128,128]{2,1,0:T(8,128)S(1)}, f32[8,128,128]{2,1,0:T(8,128)}, u32[]{:S(2)}) copy-start(f32[8,128,128]{2,1,0:T(8,128)} %get-tuple-element.9) | copy-start | bytes 1572868
  108.6 2.8 %copy-start.1 = (f32[8,128,128]{2,1,0:T(8,128)S(1)}, f32[8,128,128]{2,1,0:T(8,128)}, u32[]{:S(2)}) copy-start(f32[8,128,128]{2,1,0:T(8,128)} %get-tuple-element.10) | copy-start | bytes 1572868
  110.6 1.6 %copy-start = (f32[2,8,128,128]{3,2,1,0:T(8,128)S(1)}, f32[2,8,128,128]{3,2,1,0:T(8,128)}, u32[]{:S(2)}) copy-start(f32[2,8,128,128]{3,2,1,0:T(8,128)} %get-tuple-element.11) | copy-start | bytes 3145732

commit v9 on v8

--- a/solution.py
+++ b/solution.py
@@ -63,6 +63,9 @@
 
     row = lax.broadcasted_iota(jnp.int32, (Y, Z), 0)
     lane = lax.broadcasted_iota(jnp.int32, (Y, Z), 1)
+    CH = 32
+    crow = lax.broadcasted_iota(jnp.int32, (CH, Z), 0)
+    clane = lax.broadcasted_iota(jnp.int32, (CH, Z), 1)
 
     def near(plane, hx, hy, hz, s, xi):
         c = plane(xi)
@@ -135,17 +138,35 @@
                     for c in incoming[:2]:
                         c.wait()
                     ax[:, s] = ax[:, s] + rx[slot, :, s]
-                c, nb = near(lambda i: dbuf[slot, s, i], rx.at[slot], ry.at[slot], rz.at[slot], s, xi)
-                summed = w_ref[0, xi] * (c - nb[0])
-                for j in range(1, 6):
-                    summed = summed + w_ref[j, xi] * (c - nb[j])
-                xo[s][xi] = xo[s][xi] + c
-                res = r_ref[s, xi] - (c + summed)
-                r_ref[s, xi] = res
+                zpair = jnp.where(
+                    row < Y // 2,
+                    jnp.broadcast_to(rz[slot, s, 1, pl.ds(xi, 1), :], (Y, Z)),
+                    jnp.broadcast_to(rz[slot, s, 0, pl.ds(xi, 1), :], (Y, Z)),
+                ).T
+                for q in range(Y // CH):
+                    rows = pl.ds(q * CH, CH)
+                    c = dbuf[slot, s, xi, rows, :]
+                    xm = dbuf[slot, s, xi - 1, rows, :] if xi > 0 else rx[slot, 0, s, rows, :]
+                    xp = dbuf[slot, s, xi + 1, rows, :] if xi < X - 1 else rx[slot, 1, s, rows, :]
+                    above = ry[slot, 0, s, pl.ds(xi, 1), :] if q == 0 else dbuf[slot, s, xi, pl.ds(q * CH - 1, 1), :]
+                    below = (ry[slot, 1, s, pl.ds(xi, 1), :] if q == Y // CH - 1
+                             else dbuf[slot, s, xi, pl.ds(q * CH + CH, 1), :])
+                    ym = jnp.where(crow == 0, jnp.broadcast_to(above, (CH, Z)), pltpu.roll(c, 1, 0))
+                    yp = jnp.where(crow == CH - 1, jnp.broadcast_to(below, (CH, Z)), pltpu.roll(c, CH - 1, 0))
+                    zq = zpair[q * CH:(q + 1) * CH]
+                    zm = jnp.where(clane == 0, zq, pltpu.roll(c, 1, 1))
+                    zp = jnp.where(clane == Z - 1, zq, pltpu.roll(c, Z - 1, 1))
+                    nb = (xm, xp, ym, yp, zm, zp)
+                    summed = w_ref[0, xi, rows, :] * (c - nb[0])
+                    for j in range(1, 6):
+                        summed = summed + w_ref[j, xi, rows, :] * (c - nb[j])
+                    xo[s][xi, rows, :] = xo[s][xi, rows, :] + c
+                    res = r_ref[s, xi, rows, :] - (c + summed)
+                    r_ref[s, xi, rows, :] = res
+                    if not final:
+                        dbuf[nslot, s, xi, rows, :] = a * c + b * res
                 if not final:
-                    nd = a * c + b * res
-                    dbuf[nslot, s, xi] = nd
-                    put_faces(s, xi, nd)
+                    put_faces(s, xi, dbuf[nslot, s, xi])
             if not final:
                 for c in copies(nslot, s):
                     c.start()

time: 113 us -> 114 us (level)
  no operation moved by 1% of the time
where the time goes in v9:
time: 114 us; the launch traced here: 113 us
  Pallas kernels  105 us (92%)
  local copies, waits for them, and re-layouts  4.79 us (4%)
  between operations  2.72 us (2%)
    pallas_call x1, Pallas kernels, body(): pl.pallas_call(functools.partial(solve_kernel, ngx, ngy), out_shape=(fiel...  105 us
    unnamed x10, local copies, waits for them, and re-layouts  4.53 us

profile of v9, /device:TPU:2, one launch (start us, length us, event | category | flops | bytes accessed | tf_op | source)
XLA Modules:
  0.0 113.4 jit_solution(761714896887857750)
XLA Ops:
  2.7 0.1 stack.127
  2.8 0.1 stack.145
  2.9 0.1 pad.2.clone
  3.0 0.7 maximum_maximum_fusion.ab_ref
  3.6 105.2 %shard_map.84 = (f32[8,128,128]{2,1,0:T(8,128)}, f32[8,128,128]{2,1,0:T(8,128)}, f32[8,128,128]{2,1,0:T(8,128)}, f32[2,8,128,128]{3,2,1,0:T(8,128)}) custom-call(f32[3,16]{1,0:T(4,128)} %maximum_maximum_fusion.ab_ref, f32[8,128,128]{2,1,0:T(8,128)} %kap_ref.1, bf16[8,128,128]{2,1,0:T(8,128)(2,1)} %st_ref.1, f32[8,128]{1,0:T(8,128)} %rs_ref.1, ...), custom_call_target="tpu_custom_call" | custom-call | tf_op jit(solution)/shard_map/pallas_call | solution.py:214
  108.8 0.0 copy-start.2
  108.8 0.0 copy-start.1
  108.8 2.0 %copy.14 = f32[8,128,128]{2,1,0:T(8,128)} copy(f32[8,128,128]{2,1,0:T(8,128)} %get-tuple-element.8) | data formatting | bytes 1048576
  110.8 0.0 copy-done.2
  110.8 0.0 copy-start
  110.8 0.8 copy.15
  111.6 0.0 copy-done.1
  111.6 0.8 copy.16
  112.4 0.0 copy-done
  112.4 1.0 copy.17
Async XLA Ops:
  108.8 2.0 %copy-start.2 = (f32[8,128,128]{2,1,0:T(8,128)S(1)}, f32[8,128,128]{2,1,0:T(8,128)}, u32[]{:S(2)}) copy-start(f32[8,128,128]{2,1,0:T(8,128)} %get-tuple-element.9) | copy-start | bytes 1572868
  108.8 2.8 %copy-start.1 = (f32[8,128,128]{2,1,0:T(8,128)S(1)}, f32[8,128,128]{2,1,0:T(8,128)}, u32[]{:S(2)}) copy-start(f32[8,128,128]{2,1,0:T(8,128)} %get-tuple-element.10) | copy-start | bytes 1572868
  110.8 1.6 %copy-start = (f32[2,8,128,128]{3,2,1,0:T(8,128)S(1)}, f32[2,8,128,128]{3,2,1,0:T(8,128)}, u32[]{:S(2)}) copy-start(f32[2,8,128,128]{3,2,1,0:T(8,128)} %get-tuple-element.11) | copy-start | bytes 3145732

commit v10 on v9

--- a/solution.py
+++ b/solution.py
@@ -168,8 +168,9 @@
                 if not final:
                     put_faces(s, xi, dbuf[nslot, s, xi])
             if not final:
-                for c in copies(nslot, s):
-                    c.start()
+                outgoing = copies(nslot, s)
+                for i in (4, 2, 3, 0, 1):
+                    outgoing[i].start()
 
     def loop_step(k, carry):
         step(k, lax.rem(k, 2), False)

time: 114 us -> 114 us (level)
  no operation moved by 1% of the time
where the time goes in v10:
time: 114 us
  Pallas kernels  105 us (92%)
  local copies, waits for them, and re-layouts  4.79 us (4%)
  between operations  2.72 us (2%)
    pallas_call x1, Pallas kernels, body(): pl.pallas_call(functools.partial(solve_kernel, ngx, ngy), out_shape=(fiel...  105 us
    unnamed x10, local copies, waits for them, and re-layouts  4.53 us

profile of v10, /device:TPU:2, one launch (start us, length us, event | category | flops | bytes accessed | tf_op | source)
XLA Modules:
  0.0 113.6 jit_solution(13459180551874227433)
XLA Ops:
  2.7 0.1 stack.127
  2.8 0.1 stack.145
  2.9 0.1 pad.2.clone
  3.0 0.7 maximum_maximum_fusion.ab_ref
  3.6 105.5 %shard_map.84 = (f32[8,128,128]{2,1,0:T(8,128)}, f32[8,128,128]{2,1,0:T(8,128)}, f32[8,128,128]{2,1,0:T(8,128)}, f32[2,8,128,128]{3,2,1,0:T(8,128)}) custom-call(f32[3,16]{1,0:T(4,128)} %maximum_maximum_fusion.ab_ref, f32[8,128,128]{2,1,0:T(8,128)} %kap_ref.1, bf16[8,128,128]{2,1,0:T(8,128)(2,1)} %st_ref.1, f32[8,128]{1,0:T(8,128)} %rs_ref.1, ...), custom_call_target="tpu_custom_call" | custom-call | tf_op jit(solution)/shard_map/pallas_call | solution.py:215
  109.1 0.0 copy-start.2
  109.1 0.0 copy-start.1
  109.1 2.0 %copy.14 = f32[8,128,128]{2,1,0:T(8,128)} copy(f32[8,128,128]{2,1,0:T(8,128)} %get-tuple-element.8) | data formatting | bytes 1048576
  111.1 0.0 copy-done.2
  111.1 0.0 copy-start
  111.1 0.8 copy.15
  111.9 0.0 copy-done.1
  111.9 0.8 copy.16
  112.6 0.0 copy-done
  112.6 1.0 copy.17
Async XLA Ops:
  109.1 2.0 %copy-start.2 = (f32[8,128,128]{2,1,0:T(8,128)S(1)}, f32[8,128,128]{2,1,0:T(8,128)}, u32[]{:S(2)}) copy-start(f32[8,128,128]{2,1,0:T(8,128)} %get-tuple-element.9) | copy-start | bytes 1572868
  109.1 2.8 %copy-start.1 = (f32[8,128,128]{2,1,0:T(8,128)S(1)}, f32[8,128,128]{2,1,0:T(8,128)}, u32[]{:S(2)}) copy-start(f32[8,128,128]{2,1,0:T(8,128)} %get-tuple-element.10) | copy-start | bytes 1572868
  111.1 1.6 %copy-start = (f32[2,8,128,128]{3,2,1,0:T(8,128)S(1)}, f32[2,8,128,128]{3,2,1,0:T(8,128)}, u32[]{:S(2)}) copy-start(f32[2,8,128,128]{3,2,1,0:T(8,128)} %get-tuple-element.11) | copy-start | bytes 3145732

commit v11 on v8

--- a/solution.py
+++ b/solution.py
@@ -15,7 +15,8 @@
 
 
 def solve_kernel(ngx, ngy, ab_ref, kap_ref, st_ref, rs_ref, cot_ref, g_ref, adj_ref, state_ref, r_ref,
-                 w_ref, prev, dbuf, sx, sy, sz, rx, ry, rz, ax, ay, az, send_sem, recv_sem, st_sem):
+                 w_ref, prev, dbuf, sx, sy, sz, rx, ry, rz, ax, ay, az, syi, szi, ryi, rzi, ayi, azi,
+                 send_sem, recv_sem, st_sem):
     S = 2
     X, Y, Z = kap_ref.shape
     xo = (state_ref, adj_ref)
@@ -41,6 +42,9 @@
             (sy.at[0, s], ry.at[slot, 1, s], peers[2]),
             (sy.at[1, s], ry.at[slot, 0, s], peers[3]),
             (sz.at[s], rz.at[slot, s], peers[4]),
+            (syi.at[0, s], ryi.at[slot, 1, s], peers[2]),
+            (syi.at[1, s], ryi.at[slot, 0, s], peers[3]),
+            (szi.at[s], rzi.at[slot, s], peers[4]),
         )
         return [
             pltpu.make_async_remote_copy(
@@ -55,11 +59,12 @@
             sx[0, s] = plane
         if xi == X - 1:
             sx[1, s] = plane
-        sy[0, s, pl.ds(xi, 1), :] = plane[0:1, :]
-        sy[1, s, pl.ds(xi, 1), :] = plane[Y - 1:Y, :]
+        fy, fz = (sy, sz) if xi in (0, X - 1) else (syi, szi)
+        fy[0, s, pl.ds(xi, 1), :] = plane[0:1, :]
+        fy[1, s, pl.ds(xi, 1), :] = plane[Y - 1:Y, :]
         t = plane.T
-        sz[s, 0, pl.ds(xi, 1), :] = t[0:1, :]
-        sz[s, 1, pl.ds(xi, 1), :] = t[Z - 1:Z, :]
+        fz[s, 0, pl.ds(xi, 1), :] = t[0:1, :]
+        fz[s, 1, pl.ds(xi, 1), :] = t[Z - 1:Z, :]
 
     row = lax.broadcasted_iota(jnp.int32, (Y, Z), 0)
     lane = lax.broadcasted_iota(jnp.int32, (Y, Z), 1)
@@ -86,6 +91,8 @@
     )
     swap.start()
     theta = ab_ref[2, 0]
+    for q in (sy, sz, syi, szi):
+        q[...] = jnp.zeros(q.shape, jnp.float32)
 
     def start_solve(s):
         for xi in range(X):
@@ -111,13 +118,14 @@
     for c in copies(1, 0):
         c.wait()
     for xi in range(X):
-        kc, nb = near(lambda i: kap_ref[i], rx.at[1], ry.at[1], rz.at[1], 0, xi)
+        hy, hz = (ry, rz) if xi in (0, X - 1) else (ryi, rzi)
+        kc, nb = near(lambda i: kap_ref[i], rx.at[1], hy.at[1], hz.at[1], 0, xi)
         for j in range(6):
             w_ref[j, xi] = (kc + nb[j]) * (0.5 * time_step)
 
     swap.wait()
     start_solve(0)
-    for q in (ax, ay, az):
+    for q in (ax, ay, az, ayi, azi):
         q[...] = jnp.zeros(q.shape, jnp.float32)
 
     def step(k, slot, final):
@@ -126,16 +134,23 @@
         b = ab_ref[1, k]
         for s in (1, 0):
             incoming = copies(slot, s)
-            for c in incoming[2:]:
+            outgoing = copies(nslot, s)
+            for c in incoming[5:]:
                 c.wait()
-            ay[:, s] = ay[:, s] + ry[slot, :, s]
-            az[s] = az[s] + rz[slot, s]
+            ayi[:, s] = ayi[:, s] + ryi[slot, :, s]
+            azi[s] = azi[s] + rzi[slot, s]
             for xi in list(range(1, X - 1)) + [0, X - 1]:
                 if xi == 0:
-                    for c in incoming[:2]:
+                    if not final:
+                        for c in outgoing[5:]:
+                            c.start()
+                    for c in incoming[:5]:
                         c.wait()
                     ax[:, s] = ax[:, s] + rx[slot, :, s]
-                c, nb = near(lambda i: dbuf[slot, s, i], rx.at[slot], ry.at[slot], rz.at[slot], s, xi)
+                    ay[:, s] = ay[:, s] + ry[slot, :, s]
+                    az[s] = az[s] + rz[slot, s]
+                hy, hz = (ry, rz) if xi in (0, X - 1) else (ryi, rzi)
+                c, nb = near(lambda i: dbuf[slot, s, i], rx.at[slot], hy.at[slot], hz.at[slot], s, xi)
                 summed = w_ref[0, xi] * (c - nb[0])
                 for j in range(1, 6):
                     summed = summed + w_ref[j, xi] * (c - nb[j])
@@ -147,7 +162,7 @@
                     dbuf[nslot, s, xi] = nd
                     put_faces(s, xi, nd)
             if not final:
-                for c in copies(nslot, s):
+                for c in outgoing[:5]:
                     c.start()
 
     def loop_step(k, carry):
@@ -158,8 +173,9 @@
     step(CHEB - 1, (CHEB - 1) % 2, True)
 
     for xi in range(X):
-        c0, n0 = near(lambda i: xo[0][i], ax, ay, az, 0, xi)
-        c1, n1 = near(lambda i: xo[1][i], ax, ay, az, 1, xi)
+        hy, hz = (ay, az) if xi in (0, X - 1) else (ayi, azi)
+        c0, n0 = near(lambda i: xo[0][i], ax, hy, hz, 0, xi)
+        c1, n1 = near(lambda i: xo[1][i], ax, hy, hz, 1, xi)
         summed = (c0 - n0[0]) * (c1 - n1[0])
         for j in range(1, 6):
             summed = summed + (c0 - n0[j]) * (c1 - n1[j])
@@ -208,8 +224,14 @@
             pltpu.VMEM((2, S, Y, Z), f32),
             pltpu.VMEM((2, S, X, Z), f32),
             pltpu.VMEM((S, 2, X, Y), f32),
-            pltpu.SemaphoreType.DMA((5, S, 2)),
-            pltpu.SemaphoreType.DMA((5, S, 2)),
+            pltpu.VMEM((2, S, X, Z), f32),
+            pltpu.VMEM((S, 2, X, Y), f32),
+            pltpu.VMEM((2, 2, S, X, Z), f32),
+            pltpu.VMEM((2, S, 2, X, Y), f32),
+            pltpu.VMEM((2, S, X, Z), f32),
+            pltpu.VMEM((S, 2, X, Y), f32),
+            pltpu.SemaphoreType.DMA((8, S, 2)),
+            pltpu.SemaphoreType.DMA((8, S, 2)),
             pltpu.SemaphoreType.DMA((2,)),
         ],
         compiler_params=pltpu.CompilerParams(

time: 113 us -> 117 us (1.035)
  Pallas kernels: 105 us -> 108 us
    pallas_call x1, Pallas kernels: 105 us -> 108 us  [body(): pl.pallas_call(functools.partial(solve_kernel, ngx, ngy), out_shape=(fiel...]
where the time goes in v11:
time: 117 us
  Pallas kernels  108 us (92%)
  local copies, waits for them, and re-layouts  4.79 us (4%)
  between operations  2.72 us (2%)
    pallas_call x1, Pallas kernels, body(): pl.pallas_call(functools.partial(solve_kernel, ngx, ngy), out_shape=(fiel...  108 us
    unnamed x10, local copies, waits for them, and re-layouts  4.53 us

profile of v11, /device:TPU:2, one launch (start us, length us, event | category | flops | bytes accessed | tf_op | source)
XLA Modules:
  0.0 116.5 jit_solution(3396719281847464274)
XLA Ops:
  2.7 0.1 stack.127
  2.8 0.1 stack.145
  2.9 0.1 pad.2.clone
  3.0 0.7 maximum_maximum_fusion.ab_ref
  3.6 108.4 %shard_map.84 = (f32[8,128,128]{2,1,0:T(8,128)}, f32[8,128,128]{2,1,0:T(8,128)}, f32[8,128,128]{2,1,0:T(8,128)}, f32[2,8,128,128]{3,2,1,0:T(8,128)}) custom-call(f32[3,16]{1,0:T(4,128)} %maximum_maximum_fusion.ab_ref, f32[8,128,128]{2,1,0:T(8,128)} %kap_ref.1, bf16[8,128,128]{2,1,0:T(8,128)(2,1)} %st_ref.1, f32[8,128]{1,0:T(8,128)} %rs_ref.1, ...), custom_call_target="tpu_custom_call" | custom-call | tf_op jit(solution)/shard_map/pallas_call | solution.py:209
  112.0 0.0 copy-start.2
  112.0 0.0 copy-start.1
  112.0 2.0 %copy.14 = f32[8,128,128]{2,1,0:T(8,128)} copy(f32[8,128,128]{2,1,0:T(8,128)} %get-tuple-element.8) | data formatting | bytes 1048576
  114.0 0.0 copy-done.2
  114.0 0.0 copy-start
  114.0 0.8 copy.15
  114.8 0.0 copy-done.1
  114.8 0.8 copy.16
  115.6 0.0 copy-done
  115.6 1.0 copy.17
Async XLA Ops:
  112.0 2.0 %copy-start.2 = (f32[8,128,128]{2,1,0:T(8,128)S(1)}, f32[8,128,128]{2,1,0:T(8,128)}, u32[]{:S(2)}) copy-start(f32[8,128,128]{2,1,0:T(8,128)} %get-tuple-element.9) | copy-start | bytes 1572868
  112.0 2.8 %copy-start.1 = (f32[8,128,128]{2,1,0:T(8,128)S(1)}, f32[8,128,128]{2,1,0:T(8,128)}, u32[]{:S(2)}) copy-start(f32[8,128,128]{2,1,0:T(8,128)} %get-tuple-element.10) | copy-start | bytes 1572868
  114.0 1.6 %copy-start = (f32[2,8,128,128]{3,2,1,0:T(8,128)S(1)}, f32[2,8,128,128]{3,2,1,0:T(8,128)}, u32[]{:S(2)}) copy-start(f32[2,8,128,128]{3,2,1,0:T(8,128)} %get-tuple-element.11) | copy-start | bytes 3145732

commit v12 on v8

--- a/solution.py
+++ b/solution.py
@@ -166,6 +166,12 @@
         g_ref[xi] = (-0.5 * time_step) * summed
 
 
+def hand_over(*refs):
+    n = len(refs) // 2
+    for src, dst in zip(refs[:n], refs[n:]):
+        dst[...] = src[...]
+
+
 def body(conductivity, stored_state, row_scales, cotangent, upper_bound):
     X, Y, Z = conductivity.shape
     S = 2
@@ -190,7 +196,7 @@
     f32 = jnp.float32
     vmem = pl.BlockSpec(memory_space=pltpu.VMEM)
     field = jax.ShapeDtypeStruct((X, Y, Z), f32)
-    return pl.pallas_call(
+    results = pl.pallas_call(
         functools.partial(solve_kernel, ngx, ngy),
         out_shape=(field, field, field, jax.ShapeDtypeStruct((S, X, Y, Z), f32)),
         in_specs=[pl.BlockSpec(memory_space=pltpu.SMEM), vmem, vmem, vmem, vmem],
@@ -216,6 +222,12 @@
             collective_id=0, has_side_effects=True, vmem_limit_bytes=60 * 1024 * 1024
         ),
     )(ab, conductivity, stored_state, row_scales, cotangent)
+    return pl.pallas_call(
+        hand_over,
+        out_shape=tuple(jax.ShapeDtypeStruct(o.shape, o.dtype) for o in results),
+        in_specs=[vmem] * len(results),
+        out_specs=tuple([vmem] * len(results)),
+    )(*results)
 
 
 def solution(mesh):

time: 113 us -> 112 us (level)
  local copies, waits for them, and re-layouts: 4.79 us -> 0.27 us
  Pallas kernels: 105 us -> 108 us
    unnamed x10 -> x0, local copies, waits for them, and re-layouts: 4.53 us -> none
    pallas_call x0 -> x1, Pallas kernels: none -> 3.23 us  [body(): pl.pallas_call(hand_over, out_shape=tuple((jax.ShapeDtypeStruct(o.shape,...]
where the time goes in v12:
time: 112 us
  Pallas kernels  108 us (96%)
  between operations  2.7 us (2%)
    pallas_call x1, Pallas kernels, body(): pl.pallas_call(functools.partial(solve_kernel, ngx, ngy), out_shape=(fiel...  105 us
    pallas_call x1, Pallas kernels, body(): pl.pallas_call(hand_over, out_shape=tuple((jax.ShapeDtypeStruct(o.shape,...  3.23 us

profile of v12, /device:TPU:2, one launch (start us, length us, event | category | flops | bytes accessed | tf_op | source)
XLA Modules:
  0.0 111.9 jit_solution(13333203860578260439)
XLA Ops:
  2.7 0.1 stack.127
  2.8 0.1 stack.145
  2.9 0.1 pad.2.clone
  3.0 0.7 maximum_maximum_fusion.ab_ref
  3.6 105.0 %shard_map.84 = (f32[8,128,128]{2,1,0:T(8,128)}, f32[8,128,128]{2,1,0:T(8,128)}, f32[8,128,128]{2,1,0:T(8,128)}, f32[2,8,128,128]{3,2,1,0:T(8,128)}) custom-call(f32[3,16]{1,0:T(4,128)} %maximum_maximum_fusion.ab_ref, f32[8,128,128]{2,1,0:T(8,128)} %kap_ref.1, bf16[8,128,128]{2,1,0:T(8,128)(2,1)} %st_ref.1, f32[8,128]{1,0:T(8,128)} %rs_ref.1, ...), custom_call_target="tpu_custom_call" | custom-call | tf_op jit(solution)/shard_map/pallas_call | solution.py:199
  108.6 3.2 %shard_map.85 = (f32[8,128,128]{2,1,0:T(8,128)}, f32[8,128,128]{2,1,0:T(8,128)}, f32[8,128,128]{2,1,0:T(8,128)}, f32[2,8,128,128]{3,2,1,0:T(8,128)}) custom-call(f32[8,128,128]{2,1,0:T(8,128)} %get-tuple-element.8.refs_0_, f32[8,128,128]{2,1,0:T(8,128)} %get-tuple-element.9.refs_1_, f32[8,128,128]{2,1,0:T(8,128)} %get-tuple-element.10.refs_2_, ...), custom_call_target="tpu_custom_call" | custom-call | tf_op jit(solution)/shard_map/pallas_call | solution.py:225

commit v13 on v12

--- a/solution.py
+++ b/solution.py
@@ -222,11 +222,18 @@
             collective_id=0, has_side_effects=True, vmem_limit_bytes=60 * 1024 * 1024
         ),
     )(ab, conductivity, stored_state, row_scales, cotangent)
+    planes = 2
+    specs = [
+        pl.BlockSpec((planes, Y, Z), lambda i: (i, 0, 0)) if o.ndim == 3
+        else pl.BlockSpec((S, planes, Y, Z), lambda i: (0, i, 0, 0))
+        for o in results
+    ]
     return pl.pallas_call(
         hand_over,
+        grid=(X // planes,),
         out_shape=tuple(jax.ShapeDtypeStruct(o.shape, o.dtype) for o in results),
-        in_specs=[vmem] * len(results),
-        out_specs=tuple([vmem] * len(results)),
+        in_specs=specs,
+        out_specs=tuple(specs),
     )(*results)
 
 

time: 112 us -> 113 us (level)
  no operation moved by 1% of the time
where the time goes in v13:
time: 113 us
  Pallas kernels  109 us (96%)
  between operations  2.7 us (2%)
    pallas_call x1, Pallas kernels, body(): pl.pallas_call(functools.partial(solve_kernel, ngx, ngy), out_shape=(fiel...  105 us
    pallas_call x1, Pallas kernels, body(): pl.pallas_call(hand_over, grid=(X // planes,), out_shape=tuple((jax.Shape...  4 us

profile of v13, /device:TPU:2, one launch (start us, length us, event | category | flops | bytes accessed | tf_op | source)
XLA Modules:
  0.0 112.6 jit_solution(15103860153624200344)
XLA Ops:
  2.7 0.1 stack.127
  2.8 0.1 stack.145
  2.9 0.1 pad.2.clone
  3.0 0.7 maximum_maximum_fusion.ab_ref
  3.6 105.0 %shard_map.84 = (f32[8,128,128]{2,1,0:T(8,128)}, f32[8,128,128]{2,1,0:T(8,128)}, f32[8,128,128]{2,1,0:T(8,128)}, f32[2,8,128,128]{3,2,1,0:T(8,128)}) custom-call(f32[3,16]{1,0:T(4,128)} %maximum_maximum_fusion.ab_ref, f32[8,128,128]{2,1,0:T(8,128)} %kap_ref.1, bf16[8,128,128]{2,1,0:T(8,128)(2,1)} %st_ref.1, f32[8,128]{1,0:T(8,128)} %rs_ref.1, ...), custom_call_target="tpu_custom_call" | custom-call | tf_op jit(solution)/shard_map/pallas_call | solution.py:199
  108.6 4.0 %shard_map.85 = (f32[8,128,128]{2,1,0:T(8,128)}, f32[8,128,128]{2,1,0:T(8,128)}, f32[8,128,128]{2,1,0:T(8,128)}, f32[2,8,128,128]{3,2,1,0:T(8,128)}) custom-call(f32[8,128,128]{2,1,0:T(8,128)} %get-tuple-element.8.refs_0_, f32[8,128,128]{2,1,0:T(8,128)} %get-tuple-element.9.refs_1_, f32[8,128,128]{2,1,0:T(8,128)} %get-tuple-element.10.refs_2_, ...), custom_call_target="tpu_custom_call" | custom-call | tf_op jit(solution)/shard_map/pallas_call | solution.py:231

commit v14 on v12

--- a/solution.py
+++ b/solution.py
@@ -14,8 +14,8 @@
 time_step = 8.0
 
 
-def solve_kernel(ngx, ngy, ab_ref, kap_ref, st_ref, rs_ref, cot_ref, g_ref, adj_ref, state_ref, r_ref,
-                 w_ref, prev, dbuf, sx, sy, sz, rx, ry, rz, ax, ay, az, send_sem, recv_sem, st_sem):
+def solve_kernel(ngx, ngy, ub_ref, kap_ref, st_ref, rs_ref, cot_ref, g_ref, adj_ref, state_ref, r_ref,
+                 w_ref, prev, dbuf, sx, sy, sz, rx, ry, rz, ax, ay, az, coef, send_sem, recv_sem, st_sem):
     S = 2
     X, Y, Z = kap_ref.shape
     xo = (state_ref, adj_ref)
@@ -85,7 +85,17 @@
         device_id=peers[4], device_id_type=MESH,
     )
     swap.start()
-    theta = ab_ref[2, 0]
+    upper = jnp.full((8, Z), ub_ref[0], jnp.float32)
+    theta_v = 0.5 * (upper + 1.0)
+    delta = 0.5 * (upper - 1.0)
+    sigma = theta_v / delta
+    rho = 1.0 / sigma
+    for k in range(CHEB):
+        rho_next = 1.0 / (2.0 * sigma - rho)
+        coef[0, k] = rho_next * rho
+        coef[1, k] = 2.0 * rho_next / delta
+        rho = rho_next
+    theta = jnp.broadcast_to(theta_v[0:1, :], (Y, Z))
 
     def start_solve(s):
         for xi in range(X):
@@ -122,8 +132,8 @@
 
     def step(k, slot, final):
         nslot = 1 - slot
-        a = ab_ref[0, k]
-        b = ab_ref[1, k]
+        a = jnp.broadcast_to(coef[0, k, 0:1, :], (Y, Z))
+        b = jnp.broadcast_to(coef[1, k, 0:1, :], (Y, Z))
         for s in (1, 0):
             incoming = copies(slot, s)
             for c in incoming[2:]:
@@ -175,22 +185,6 @@
 def body(conductivity, stored_state, row_scales, cotangent, upper_bound):
     X, Y, Z = conductivity.shape
     S = 2
-    upper = upper_bound[0]
-    theta = 0.5 * (upper + 1.0)
-    delta = 0.5 * (upper - 1.0)
-    sigma = theta / delta
-    rho = 1.0 / sigma
-    coefs = []
-    for _ in range(CHEB):
-        rho_next = 1.0 / (2.0 * sigma - rho)
-        coefs.append((rho_next * rho, 2.0 * rho_next / delta))
-        rho = rho_next
-    ab = jnp.stack([
-        jnp.stack([c[0] for c in coefs]),
-        jnp.stack([c[1] for c in coefs]),
-        jnp.broadcast_to(theta, (CHEB,)),
-    ])
-
     ngx = lax.axis_size("gx")
     ngy = lax.axis_size("gy")
     f32 = jnp.float32
@@ -214,6 +208,7 @@
             pltpu.VMEM((2, S, Y, Z), f32),
             pltpu.VMEM((2, S, X, Z), f32),
             pltpu.VMEM((S, 2, X, Y), f32),
+            pltpu.VMEM((2, CHEB, 8, Z), f32),
             pltpu.SemaphoreType.DMA((5, S, 2)),
             pltpu.SemaphoreType.DMA((5, S, 2)),
             pltpu.SemaphoreType.DMA((2,)),
@@ -221,7 +216,7 @@
         compiler_params=pltpu.CompilerParams(
             collective_id=0, has_side_effects=True, vmem_limit_bytes=60 * 1024 * 1024
         ),
-    )(ab, conductivity, stored_state, row_scales, cotangent)
+    )(upper_bound, conductivity, stored_state, row_scales, cotangent)
     return pl.pallas_call(
         hand_over,
         out_shape=tuple(jax.ShapeDtypeStruct(o.shape, o.dtype) for o in results),

time: 112 us -> 110 us (0.982)
  between operations: 2.7 us -> 1.29 us
where the time goes in v14:
time: 110 us
  Pallas kernels  108 us (98%)
  between operations  1.29 us (1%)
    pallas_call x1, Pallas kernels, body(): pl.pallas_call(functools.partial(solve_kernel, ngx, ngy), out_shape=(fiel...  105 us
    pallas_call x1, Pallas kernels, body(): pl.pallas_call(hand_over, out_shape=tuple((jax.ShapeDtypeStruct(o.shape,...  3.23 us

profile of v14, /device:TPU:2, one launch (start us, length us, event | category | flops | bytes accessed | tf_op | source)
XLA Modules:
  0.0 109.6 jit_solution(4737990892458751639)
XLA Ops:
  1.3 105.1 %shard_map.84 = (f32[8,128,128]{2,1,0:T(8,128)}, f32[8,128,128]{2,1,0:T(8,128)}, f32[8,128,128]{2,1,0:T(8,128)}, f32[2,8,128,128]{3,2,1,0:T(8,128)}) custom-call(f32[1]{0:T(128)S(6)} %copy.9.ub_ref, f32[8,128,128]{2,1,0:T(8,128)} %kap_ref.1, bf16[8,128,128]{2,1,0:T(8,128)(2,1)} %st_ref.1, f32[8,128]{1,0:T(8,128)} %rs_ref.1, f32[8,128,128]{2,1,0:T(8,128)} %cot_ref.1), custom_call_target="tpu_custom_call" | custom-call | tf_op jit(solution)/shard_map/pallas_call | solution.py:193
  106.4 3.2 %shard_map.85 = (f32[8,128,128]{2,1,0:T(8,128)}, f32[8,128,128]{2,1,0:T(8,128)}, f32[8,128,128]{2,1,0:T(8,128)}, f32[2,8,128,128]{3,2,1,0:T(8,128)}) custom-call(f32[8,128,128]{2,1,0:T(8,128)} %get-tuple-element.8.refs_0_, f32[8,128,128]{2,1,0:T(8,128)} %get-tuple-element.9.refs_1_, f32[8,128,128]{2,1,0:T(8,128)} %get-tuple-element.10.refs_2_, ...), custom_call_target="tpu_custom_call" | custom-call | tf_op jit(solution)/shard_map/pallas_call | solution.py:220

commit v15 on v14

--- a/solution.py
+++ b/solution.py
@@ -177,9 +177,13 @@
 
 
 def hand_over(*refs):
-    n = len(refs) // 2
-    for src, dst in zip(refs[:n], refs[n:]):
-        dst[...] = src[...]
+    n = (len(refs) - 1) // 2
+    srcs, dsts, sem = refs[:n], refs[n:2 * n], refs[2 * n]
+    moves = [pltpu.make_async_copy(src, dst, sem.at[i]) for i, (src, dst) in enumerate(zip(srcs, dsts))]
+    for m in moves:
+        m.start()
+    for m in moves:
+        m.wait()
 
 
 def body(conductivity, stored_state, row_scales, cotangent, upper_bound):
@@ -220,8 +224,9 @@
     return pl.pallas_call(
         hand_over,
         out_shape=tuple(jax.ShapeDtypeStruct(o.shape, o.dtype) for o in results),
-        in_specs=[vmem] * len(results),
+        in_specs=[pl.BlockSpec(memory_space=pl.ANY)] * len(results),
         out_specs=tuple([vmem] * len(results)),
+        scratch_shapes=[pltpu.SemaphoreType.DMA((len(results),))],
     )(*results)
 
 

time: 110 us -> 110 us (level)
  no operation moved by 1% of the time
where the time goes in v15:
time: 110 us
  Pallas kernels  108 us (98%)
  between operations  1.29 us (1%)
    pallas_call x1, Pallas kernels, body(): pl.pallas_call(functools.partial(solve_kernel, ngx, ngy), out_shape=(fiel...  105 us
    pallas_call x1, Pallas kernels, body(): pl.pallas_call(hand_over, out_shape=tuple((jax.ShapeDtypeStruct(o.shape,...  3.23 us

profile of v15, /device:TPU:2, one launch (start us, length us, event | category | flops | bytes accessed | tf_op | source)
XLA Modules:
  0.0 109.6 jit_solution(6874596257995143564)
XLA Ops:
  1.3 105.1 %shard_map.84 = (f32[8,128,128]{2,1,0:T(8,128)}, f32[8,128,128]{2,1,0:T(8,128)}, f32[8,128,128]{2,1,0:T(8,128)}, f32[2,8,128,128]{3,2,1,0:T(8,128)}) custom-call(f32[1]{0:T(128)S(6)} %copy.9.ub_ref, f32[8,128,128]{2,1,0:T(8,128)} %kap_ref.1, bf16[8,128,128]{2,1,0:T(8,128)(2,1)} %st_ref.1, f32[8,128]{1,0:T(8,128)} %rs_ref.1, f32[8,128,128]{2,1,0:T(8,128)} %cot_ref.1), custom_call_target="tpu_custom_call" | custom-call | tf_op jit(solution)/shard_map/pallas_call | solution.py:197
  106.4 3.2 %shard_map.85 = (f32[8,128,128]{2,1,0:T(8,128)}, f32[8,128,128]{2,1,0:T(8,128)}, f32[8,128,128]{2,1,0:T(8,128)}, f32[2,8,128,128]{3,2,1,0:T(8,128)}) custom-call(f32[8,128,128]{2,1,0:T(8,128)} %get-tuple-element.8.refs_0_, f32[8,128,128]{2,1,0:T(8,128)} %get-tuple-element.9.refs_1_, f32[8,128,128]{2,1,0:T(8,128)} %get-tuple-element.10.refs_2_, ...), custom_call_target="tpu_custom_call" | custom-call | tf_op jit(solution)/shard_map/pallas_call | solution.py:224

commit v16 on v14

--- a/solution.py
+++ b/solution.py
@@ -112,12 +112,13 @@
         for c in copies(0, s):
             c.start()
 
-    start_solve(1)
-
     for xi in range(X):
         put_faces(0, xi, kap_ref[xi])
     for c in copies(1, 0):
         c.start()
+
+    start_solve(1)
+
     for c in copies(1, 0):
         c.wait()
     for xi in range(X):

time: 110 us -> 110 us (level)
  no operation moved by 1% of the time
where the time goes in v16:
time: 110 us; the launch traced here: 109 us
  Pallas kernels  108 us (98%)
  between operations  1.29 us (1%)
    pallas_call x1, Pallas kernels, body(): pl.pallas_call(functools.partial(solve_kernel, ngx, ngy), out_shape=(fiel...  105 us
    pallas_call x1, Pallas kernels, body(): pl.pallas_call(hand_over, out_shape=tuple((jax.ShapeDtypeStruct(o.shape,...  3.23 us

profile of v16, /device:TPU:2, one launch (start us, length us, event | category | flops | bytes accessed | tf_op | source)
XLA Modules:
  0.0 109.4 jit_solution(8807905094528397630)
XLA Ops:
  1.3 104.9 %shard_map.84 = (f32[8,128,128]{2,1,0:T(8,128)}, f32[8,128,128]{2,1,0:T(8,128)}, f32[8,128,128]{2,1,0:T(8,128)}, f32[2,8,128,128]{3,2,1,0:T(8,128)}) custom-call(f32[1]{0:T(128)S(6)} %copy.9.ub_ref, f32[8,128,128]{2,1,0:T(8,128)} %kap_ref.1, bf16[8,128,128]{2,1,0:T(8,128)(2,1)} %st_ref.1, f32[8,128]{1,0:T(8,128)} %rs_ref.1, f32[8,128,128]{2,1,0:T(8,128)} %cot_ref.1), custom_call_target="tpu_custom_call" | custom-call | tf_op jit(solution)/shard_map/pallas_call | solution.py:194
  106.2 3.2 %shard_map.85 = (f32[8,128,128]{2,1,0:T(8,128)}, f32[8,128,128]{2,1,0:T(8,128)}, f32[8,128,128]{2,1,0:T(8,128)}, f32[2,8,128,128]{3,2,1,0:T(8,128)}) custom-call(f32[8,128,128]{2,1,0:T(8,128)} %get-tuple-element.8.refs_0_, f32[8,128,128]{2,1,0:T(8,128)} %get-tuple-element.9.refs_1_, f32[8,128,128]{2,1,0:T(8,128)} %get-tuple-element.10.refs_2_, ...), custom_call_target="tpu_custom_call" | custom-call | tf_op jit(solution)/shard_map/pallas_call | solution.py:221
